TPU v7x, 128 devices: a whole 4x4x4 slice. The times are simulated.
128 devices in a mesh: kt: 8 (over x_hi, z), ks: 16 (over y, x_lo, core).
Axes of the slice: x: 4 (x_hi: 2, x_lo: 2; x = x_hi * 2 + x_lo), y: 4, z: 4, core: 2. Of those that a mesh axis runs over, the one named last changes fastest.
Arguments:
- val_target: bfloat16 [16, 32, 512], P('kt', None, 'ks'), may hold values from -6 to 6
- cond_target: bfloat16 [16, 64, 512], P('kt', None, 'ks'), may hold values from -0.03125 to 0.03125
- val_source: bfloat16 [64, 32, 512], P('ks', None, 'kt'), may hold values from -6 to 6
- cond_source: bfloat16 [64, 64, 512], P('ks', None, 'kt'), may hold values from -0.125 to 0.125
- trial_vectors: bfloat16 [64, 16, 2048], P('ks', 'kt'), may hold values from -6 to 6
- screened: bfloat16 [512, 512, 512], P(None, ('kt', 'ks')), may hold values from -0.25 to 0.25
- pair_momentum: int32 [16, 64], replicated, may hold values from 0 to 511
Outputs:
- kernel_out: float32 [16, 16, 2048], P('kt', 'ks')
All inputs are finite; a program needn't handle non-finite values.
Results may differ from a plain program's by a relative error of at most 0.019.
Values may be sent and summed in bfloat16 or wider, within the bound.
No kernel may reach another device: no remote copies, remote signals or barrier semaphores. Data moves between devices by JAX's collectives and lax.ppermute only.
A program may use at most 128 MiB of HBM per device.

v0:
```python
import jax
import jax.numpy as jnp
from jax import lax
from jax.sharding import PartitionSpec as P


def rows_first(arrays, axis, dims):
    turned = [jnp.moveaxis(a, dim, 0) for a, dim in zip(arrays, dims)]
    both = jnp.concatenate([t.reshape(len(t), -1) for t in turned], axis=1)
    whole, at, finished = (lax.all_gather(both, axis, axis=0, tiled=True), 0, [])
    for t, dim in zip(turned, dims):
        slab = whole[:, at : at + t[0].size].reshape(-1, *t.shape[1:])
        finished.append(jnp.moveaxis(slab, 0, dim))
        at += t[0].size
    return tuple(finished)


def sent_together(arrays, axis, dim, along):
    ends, at = ([], 0)
    for a in arrays[:-1]:
        at += a.shape[along]
        ends.append(at)
    both = jnp.concatenate(arrays, axis=along)
    return tuple(jnp.split(lax.all_gather(both, axis, axis=dim, tiled=True), ends, axis=along))


def cut_along(x, dim, peers):
    before, after = (x.shape[:dim], x.shape[dim + 1 :])
    return jnp.moveaxis(x.reshape(*before, peers, -1, *after), dim, 0)


def sum_at_owner(x, axis, dim):
    blocks = cut_along(x, dim, lax.axis_size(axis))
    arrived = lax.all_to_all(blocks, axis, split_axis=0, concat_axis=0, tiled=True)
    return arrived.astype(jnp.float32).sum(axis=0)


def local(val_target, cond_target, val_source, cond_source, trial_vectors, screened, pair_momentum):
    tgt_val, tgt_cond = rows_first((val_target, cond_target), "ks", (2, 2))
    src_val, src_cond, vectors = (
        *sent_together((val_source, cond_source), "kt", 2, 1),
        lax.all_gather(trial_vectors, "kt", axis=1, tiled=True),
    )
    count_kt = lax.axis_size("kt")
    count_ks = lax.axis_size("ks")
    tgt_count = tgt_val.shape[0]
    src_count = src_val.shape[0]
    pair_count = tgt_count * src_count
    width = screened.shape[2]
    val_bands = tgt_val.shape[1]
    cond_bands = tgt_cond.shape[1]
    vec_count = vectors.shape[1]
    table = pair_momentum.reshape(count_kt, tgt_count, count_ks, src_count)
    table = table.transpose(1, 3, 0, 2).reshape(pair_count, count_kt * count_ks)
    outgoing = screened[table]
    arrived = lax.all_to_all(outgoing, ("kt", "ks"), split_axis=1, concat_axis=1, tiled=True)
    pair_mats = arrived.reshape(tgt_count, src_count, width, width)
    trial_four = vectors.reshape(src_count, vec_count, val_bands, cond_bands)
    dressed = jnp.einsum(
        "snwc,scq->snwq", trial_four, src_cond, preferred_element_type=jnp.float32
    ).astype(jnp.bfloat16)
    pair_prod = (
        tgt_val.astype(jnp.float32)[:, None, :, None, :]
        * src_val.astype(jnp.float32)[None, :, None, :, :]
    ).astype(jnp.bfloat16)
    kernels = jnp.einsum(
        "tsvwp,tspq->tsvwq", pair_prod, pair_mats, preferred_element_type=jnp.float32
    ).astype(jnp.bfloat16)
    reduced = jnp.einsum(
        "tsvwq,snwq->tvnq", kernels, dressed, preferred_element_type=jnp.float32
    ).astype(jnp.bfloat16)
    partial_out = jnp.einsum(
        "tvnq,tcq->tnvc", reduced, tgt_cond, preferred_element_type=jnp.float32
    )
    partial_out = partial_out.reshape(tgt_count, vec_count, val_bands * cond_bands)
    return sum_at_owner(partial_out.astype(jnp.bfloat16), "ks", 1)


def solution(mesh):
    in_specs = (
        P("kt", None, "ks"),
        P("kt", None, "ks"),
        P("ks", None, "kt"),
        P("ks", None, "kt"),
        P("ks", "kt", None),
        P(None, ("kt", "ks"), None),
        P(),
    )
    out_specs = P("kt", "ks", None)
    return jax.shard_map(local, mesh=mesh, in_specs=in_specs, out_specs=out_specs, check_vma=False)
```

profile of v0, /device:TPU:1, one launch (start us, length us, event | category | flops | bytes accessed | tf_op | source)
XLA Modules:
  0.0 284.5 jit_solution(2779591411790372973)
XLA Ops:
  0.0 0.9 reshape.72
  1.0 0.2 copy.98
  1.2 0.4 copy-done
  1.6 10.8 %gather_fusion = bf16[1024,4,512]{2,1,0:T(4,128)(2,1)} fusion(bf16[512,4,512]{2,1,0:T(4,128)(2,1)S(1)} %copy-done, s32[1024]{0:T(1024)S(1)} %fusion.16), kind=kCustom, calls=%fused_computation | custom fusion | bytes 8392704 | tf_op jit(solution)/shard_map/gather | solution.py:55
  12.4 6.5 %copy.100 = bf16[8,128,4,512]{3,2,0,1:T(4,128)(2,1)} copy(bf16[8,128,4,512]{3,2,1,0:T(4,128)(2,1)} %bitcast.54) | data formatting | bytes 8388608 | tf_op jit(solution)/shard_map/gather | solution.py:55
  18.9 12.0 %all-to-all-start = ((bf16[8,128,4,512]{3,2,0,1:T(4,128)(2,1)}), bf16[8,128,4,512]{3,2,0,1:T(4,128)(2,1)}, u32[]{:S(2)}, u32[]{:S(2)}) async-start(bf16[8,128,4,512]{3,2,0,1:T(4,128)(2,1)} %copy.100), calls=%async_computation | async-start | bytes 8388608 | tf_op jit(solution)/shard_map/all_to_all | solution.py:56
  31.2 59.9 %all_gather.9 = bf16[512,192]{1,0:T(8,128)(2,1)S(1)} all-gather(bf16[32,192]{1,0:T(8,128)(2,1)S(1)} %pad_maximum_fusion.1), channel_id=1, replica_groups=mesh['kt'=8,'ks'=16] {'ks'}, dimensions={0}, use_global_device_ids=true | all-gather | bytes 208896 | tf_op jit(solution)/shard_map/all_gather | solution.py:10
  91.1 0.1 slice.10
  91.3 0.1 copy.91
  91.4 0.1 copy.92
  91.5 0.1 pad_maximum_fusion
  91.6 30.6 %all_gather.10 = bf16[4,96,512]{1,0,2:T(4,128)(2,1)S(1)} all-gather(bf16[4,96,64]{1,0,2:T(4,128)(2,1)S(1)} %pad_maximum_fusion), channel_id=1, replica_groups=mesh['kt'=8,'ks'=16] {'kt'}, dimensions={2}, use_global_device_ids=true | all-gather | bytes 442368 | tf_op jit(solution)/shard_map/all_gather | solution.py:24
  122.2 0.4 split.8
  122.6 0.3 copy.118
  123.0 0.3 copy.116
  123.3 28.7 %all_gather.11 = bf16[4,16,2048]{2,0,1:T(4,128)(2,1)S(1)} all-gather(bf16[4,2,2048]{2,0,1:T(4,128)(2,1)S(1)} %copy.94), channel_id=1, replica_groups=mesh['kt'=8,'ks'=16] {'kt'}, dimensions={1}, use_global_device_ids=true | all-gather | bytes 294912 | tf_op jit(solution)/shard_map/all_gather | solution.py:42
  152.1 0.1 copy.95
  152.2 0.5 reshape.71
  152.7 0.7 convert_bitcast_fusion
  153.4 12.2 %copy.108 = bf16[4,16,32,512,1]{2,1,0,4,3:T(8,128)(2,1)} copy(bf16[4,16,32,512,1]{3,2,1,0,4:T(8,128)(2,1)S(1)} %convert_bitcast_fusion) | data formatting | bytes 4194304 | tf_op jit(solution)/shard_map/convert_element_type | solution.py:61
  165.6 0.1 copy.90
  165.7 5.6 %copy.101 = bf16[8,128,4,512]{3,2,1,0:T(4,128)(2,1)} copy(bf16[8,128,4,512]{3,2,0,1:T(4,128)(2,1)} %all-to-all-done) | data formatting | bytes 8388608 | tf_op jit(solution)/shard_map/all_to_all | solution.py:56
  171.3 6.9 %reshape.86 = bf16[2,4,512,512,1]{3,2,1,0,4:T(8,128)(2,1)} reshape(bf16[8,128,4,512]{3,2,1,0:T(4,128)(2,1)} %copy.101) | data formatting | bytes 8388608 | tf_op jit(solution)/shard_map/reshape | solution.py:57
  178.2 8.9 %fusion.3 = bf16[2,4,32,32,512]{4,3,2,1,0:T(8,128)(2,1)} fusion(f32[4,32,512]{2,1,0:T(8,128)S(1)} %convert_element_type.54, f32[2,32,512]{2,1,0:T(8,128)S(1)} %convert_bitcast_fusion.1, bf16[2,4,512,512,1]{3,2,1,0,4:T(8,128)(2,1)} %reshape.86), kind=kOutput, calls=%fused_computation.6 | convolution fusion | flops 4307550208 | bytes 12976128 | tf_op jit(solution)/shard_map/tsvwp,tspq->tsvwq/dot_general | solution.py:66
  187.2 44.3 %copy.103 = bf16[2,4,32,32,512]{3,2,1,0,4:T(8,128)(2,1)} copy(bf16[2,4,32,32,512]{4,3,2,1,0:T(8,128)(2,1)} %fusion.3) | data formatting | bytes 16777216 | tf_op jit(solution)/shard_map/convert_element_type | solution.py:68
  231.5 28.3 %fusion.4 = bf16[2,32,16,512]{1,2,0,3:T(8,128)(2,1)} fusion(bf16[4,16,32,512,1]{2,1,0,4,3:T(8,128)(2,1)} %copy.108, bf16[2,4,32,32,512]{3,2,1,0,4:T(8,128)(2,1)} %copy.103), kind=kOutput, calls=%fused_computation.7 | convolution fusion | flops 134742016 | bytes 11534336 | tf_op jit(solution)/shard_map/tsvwq,snwq->tvnq/dot_general | solution.py:69
  259.8 3.7 %fusion.11 = bf16[2,16,32,64]{3,2,1,0:T(8,128)(2,1)S(1)} fusion(bf16[2,64,512,1]{2,1,3,0:T(8,128)(2,1)S(1)} %bitcast.56, bf16[2,32,16,512]{1,2,0,3:T(8,128)(2,1)} %fusion.4), kind=kOutput, calls=%fused_computation.13 | convolution fusion | flops 67174400 | bytes 1310720 | tf_op jit(solution)/shard_map/tvnq,tcq->tnvc/dot_general | solution.py:72
  263.5 0.3 convert_element_type.61
  263.8 0.1 copy.126
  263.9 19.9 %all_to_all.10 = bf16[16,2,1,2048]{3,1,2,0:T(2,128)(2,1)S(1)} all-to-all(bf16[16,2,1,2048]{3,1,2,0:T(2,128)(2,1)S(1)} %bitcast.58), channel_id=1, replica_groups=mesh['kt'=8,'ks'=16] {'ks'}, dimensions={0} | all-to-all | bytes 262144 | tf_op jit(solution)/shard_map/all_to_all | solution.py:34
  283.8 0.1 convert_reduce_fusion
  283.9 0.6 reduce_sum.12
  (25 shorter events, 0.6 us)
Async XLA Ops:
  0.0 1.6 copy-start
  18.9 12.0 %copy-start.6 = (bf16[2,64,32]{1,2,0:T(8,128)(2,1)S(1)}, bf16[2,64,32]{1,2,0:T(8,128)(2,1)}, u32[]{:S(2)}) copy-start(bf16[2,64,32]{1,2,0:T(8,128)(2,1)} %param.8) | copy-start | bytes 24580
  18.9 12.1 %copy-start.5 = (bf16[2,32,32]{2,1,0:T(8,128)(2,1)S(1)}, bf16[2,32,32]{2,1,0:T(8,128)(2,1)}, u32[]{:S(2)}) copy-start(bf16[2,32,32]{2,1,0:T(8,128)(2,1)} %param.7) | copy-start | bytes 12292
  18.9 72.3 %copy-start.3 = (bf16[4,32,64]{2,1,0:T(8,128)(2,1)S(1)}, bf16[4,32,64]{2,1,0:T(8,128)(2,1)}, u32[]{:S(2)}) copy-start(bf16[4,32,64]{2,1,0:T(8,128)(2,1)} %param.9) | copy-start | bytes 49156
  18.9 72.5 %copy-start.2 = (bf16[4,64,64]{2,1,0:T(8,128)(2,1)S(1)}, bf16[4,64,64]{2,1,0:T(8,128)(2,1)}, u32[]{:S(2)}) copy-start(bf16[4,64,64]{2,1,0:T(8,128)(2,1)} %param.10) | copy-start | bytes 98308
  18.9 146.8 %all-to-all-start = ((bf16[8,128,4,512]{3,2,0,1:T(4,128)(2,1)}), bf16[8,128,4,512]{3,2,0,1:T(4,128)(2,1)}, u32[]{:S(2)}, u32[]{:S(2)}) async-start(bf16[8,128,4,512]{3,2,0,1:T(4,128)(2,1)} %copy.100), calls=%async_computation | async-start | bytes 8388608 | tf_op jit(solution)/shard_map/all_to_all | solution.py:56
  30.9 92.4 %copy-start.4 = (bf16[4,2,2048]{2,1,0:T(2,128)(2,1)S(1)}, bf16[4,2,2048]{2,1,0:T(2,128)(2,1)}, u32[]{:S(2)}) copy-start(bf16[4,2,2048]{2,1,0:T(2,128)(2,1)} %param.11) | copy-start | bytes 98308
  231.4 53.1 %copy-start.1 = (bf16[512,4,512]{2,1,0:T(4,128)(2,1)S(1)}, bf16[512,4,512]{2,1,0:T(4,128)(2,1)}, u32[]{:S(2)}) copy-start(bf16[512,4,512]{2,1,0:T(4,128)(2,1)} %param.12) | copy-start | bytes 6291460
where the time goes:
time: 285 us
  blocking collectives  139 us (49%)
  local copies, waits for them, and re-layouts  91.2 us (32%)
  matrix products  41.6 us (15%)
  starting transfers between devices  12 us (4%)
    all_gather x1, blocking collectives, rows_first(): lax.all_gather(both, axis, axis=0, tiled=True)  59.9 us
    convert_element_type x1, local copies, waits for them, and re-layouts, local(): kernels = jnp.einsum('tsvwp,tspq->tsvwq', pair_prod, pair_mats, preferred...  44.3 us
    all_gather x1, blocking collectives, sent_together(): lax.all_gather(both, axis, axis=dim, tiled=True)  30.6 us
    all_gather x1, blocking collectives, local(): lax.all_gather(trial_vectors, 'kt', axis=1, tiled=True)  28.7 us
    dot_general x1, matrix products, local(): jnp.einsum('tsvwq,snwq->tvnq', kernels, dressed, preferred_element_type=j...  28.3 us
    all_to_all x1, blocking collectives, sum_at_owner(): lax.all_to_all(blocks, axis, split_axis=0, concat_axis=0, tiled=True)  19.9 us
    gather x2, local copies, waits for them, and re-layouts, local(): outgoing = screened[table]  17.3 us
    convert_element_type x1, local copies, waits for them, and re-layouts, local(): dressed = jnp.einsum('snwc,scq->snwq', trial_four, src_cond, preferred_el...  12.2 us
  transfers between devices with their start and end apart: 1, of which 0 were waited for; matrix products, arithmetic and copies ran while one was open for 5% of the time, Pallas kernels for 0%

commit v1 on v0

v1 whole, which is shorter than its diff:
```python
import jax
import jax.numpy as jnp
from jax import lax
from jax.experimental import pallas as pl
from jax.experimental.pallas import tpu as pltpu
from jax.sharding import Mesh
from jax.sharding import PartitionSpec as P

ALL = ("xh", "z", "y", "xl", "core")
X = ("xh", "xl")
KT = ("xh", "z")
YX = ("y", "xl")
BF = jnp.bfloat16
F32 = jnp.float32
VMEM_LIMIT = 56 * 1024 * 1024


def swap(x, axes, size, mask):
    return lax.ppermute(x, axes, [(i, i ^ mask) for i in range(size)])


def gathered(x, axes, size):
    return [x] + [swap(x, axes, size, k) for k in range(1, size)]


def flip_if(bit, x, axis):
    return jnp.where(bit == 1, jnp.flip(x, axis), x)


def pair_kernel(svt_ref, *refs):
    trial, outs = refs[:8], refs[8:]
    lane = lax.broadcasted_iota(jnp.int32, (64, 256), 1)
    first = (lane & 64) == 0
    for k in range(8):
        for sp in range(2):
            block = trial[k][sp]
            even = jnp.dot(svt_ref[2 * sp], block, preferred_element_type=F32)
            odd = jnp.dot(svt_ref[2 * sp + 1], block, preferred_element_type=F32)
            both = jnp.where(first, even, odd)
            for peer in range(8):
                rows = both[peer * 8 : peer * 8 + 8]
                piece = jnp.concatenate([rows[:, :128], rows[:, 128:]], axis=0)
                outs[peer][sp, k * 16 : k * 16 + 16, :] = piece.astype(BF)


def main_kernel(me_ref, pm_ref, w_ref, *refs):
    a_refs, pa, pb, pc = refs[:8], refs[8:12], refs[12:16], refs[16:20]
    out_ref, cs, ct, xs, acc = refs[20:]
    xh, z, y, xl, core = (me_ref[i] for i in range(5))
    kt, yx = xh * 4 + z, y * 2 + xl

    def where_from(rx, ry, rz):
        kt_from = kt ^ (((rx >> 1) << 2) | rz)
        yx_rel = (ry << 1) | (rx & 1)
        return kt_from, yx_rel

    def spread(block, rx, ry, rz, q_at, q_rows, ct_at):
        kt_from, yx_rel = where_from(rx, ry, rz)
        for sp in range(2):
            start = pl.multiple_of(kt_from * 64 + q_at, 16)
            cs[yx_rel, sp, pl.ds(start, q_rows), :] = block[sp * q_rows : (sp + 1) * q_rows]
        if ct_at is not None:
            for other in range(2):
                chip = ((yx_rel ^ yx) << 1) | (core ^ other)
                start = pl.multiple_of(chip * 32 + ct_at, 16)
                ct[kt_from, pl.ds(start, 16), :] = block[32 + 16 * other : 48 + 16 * other]

    for last in range(4):

        def one(i, carry, last=last):
            hi, lo = i >> 2, i & 3
            spread(pa[last][hi, lo], lo, hi, last, 0, 32, None)
            spread(pb[last][hi, lo], last, lo, hi, 32, 16, 0)
            spread(pc[last][hi, lo], hi, last, lo, 48, 16, 16)
            return carry

        lax.fori_loop(0, 16, one, 0)

    lane = lax.broadcasted_iota(jnp.int32, (128, 128), 1)
    first = lane < 64
    for chunk in range(4):
        for jj in range(2):
            j = chunk * 2 + jj
            for sp in range(2):
                a = a_refs[j][sp]
                none = jnp.zeros_like(a)
                lhs = jnp.concatenate([jnp.where(first, a, none), jnp.where(first, none, a)], axis=0)
                x = lax.dot_general(
                    lhs, cs[j, sp], (((1,), (1,)), ((), ())), preferred_element_type=F32
                ).astype(BF)
                xs[(jj * 2 + sp) * 2] = x[:128]
                xs[(jj * 2 + sp) * 2 + 1] = x[128:]

        def one_target(t, carry, chunk=chunk):
            mats = []
            for jj in range(2):
                source = (((chunk * 2 + jj) ^ yx) * 2 + core) * 4
                mats += [pm_ref[t, source + i] for i in range(4)]
            for qb in range(4):
                lanes = slice(qb * 128, qb * 128 + 128)
                w = [w_ref[m, :, lanes] for m in mats]
                for nb in range(8):
                    rows = slice(nb * 16, nb * 16 + 16)
                    terms = [w[i] * xs[i, rows, lanes] for i in range(8)]
                    while len(terms) > 1:
                        terms = [terms[i] + terms[i + 1] for i in range(0, len(terms), 2)]
                    total = terms[0].astype(F32)
                    if chunk > 0:
                        total = total + acc[t, rows, lanes]
                    acc[t, rows, lanes] = total
            return carry

        lax.fori_loop(0, 16, one_target, 0)

    def project(pair, carry):
        z0 = jnp.dot(acc[2 * pair].astype(BF), ct[pair], preferred_element_type=F32)
        z1 = jnp.dot(acc[2 * pair + 1].astype(BF), ct[pair], preferred_element_type=F32)
        zz = jnp.where(first, z0, z1).reshape(16, 8, 128).astype(BF)
        for k in range(8):
            n_at = (kt ^ k) * 2
            out_ref[pair, pl.ds(n_at, 2)] = zz[2 * k : 2 * k + 2]
        return carry

    lax.fori_loop(0, 8, project, 0)


def local(val_target, cond_target, val_source, cond_source, trial_vectors, screened, pair_momentum):
    xh, z, y, xl, core = (lax.axis_index(a) for a in ALL)
    me = jnp.stack([xh, z, y, xl, core, xh, xh, xh]).astype(jnp.int32)

    trial = trial_vectors.reshape(2, 2, 2, 32, 64).transpose(0, 3, 2, 1, 4).reshape(2, 32, 256)
    trials = gathered(trial, KT, 8)
    sv = val_source.reshape(4, 32, 2, 2, 2, 2, 4)
    sv = flip_if(y >> 1, sv, 2)
    sv = flip_if(y & 1, sv, 3)
    sv = flip_if(xl, sv, 4)
    sv = flip_if(core, sv, 5)
    svt = sv.reshape(4, 32, 64).transpose(0, 2, 1)

    other = swap(screened, "core", 2, 1)
    w_rep = jnp.concatenate([screened, other, screened, other], axis=1)

    cs = cond_source.reshape(2, 2, 64, 64).transpose(0, 3, 1, 2).reshape(2, 64, 128)
    ct = cond_target.transpose(2, 0, 1).reshape(32, 128)
    part_a = cs[:, :32].reshape(64, 128)
    part_b, ct_b = cs[:, 32:48].reshape(32, 128), ct[:16]
    part_c, ct_c = cs[:, 48:].reshape(32, 128), ct[16:]
    a1 = jnp.stack(gathered(part_a, X, 4))

    def with_other(part, extra, axis):
        own = gathered(jnp.concatenate([part, extra], axis=0), axis, 4)
        cross = [swap(extra, (axis, "core"), 8, 2 * k + 1) for k in range(4)]
        return jnp.stack([jnp.concatenate([o, c], axis=0) for o, c in zip(own, cross)])

    b1 = with_other(part_b, ct_b, "y")
    c1 = with_other(part_c, ct_c, "z")
    a2 = jnp.stack(gathered(a1, "y", 4))
    b2 = jnp.stack(gathered(b1, "z", 4))
    c2 = jnp.stack(gathered(c1, X, 4))
    a3, b3, c3 = gathered(a2, "z", 4), gathered(b2, X, 4), gathered(c2, "y", 4)

    vmem = pl.BlockSpec(memory_space=pltpu.VMEM)
    smem = pl.BlockSpec(memory_space=pltpu.SMEM)
    pieces = pl.pallas_call(
        pair_kernel,
        out_shape=[jax.ShapeDtypeStruct((2, 128, 128), BF)] * 8,
        in_specs=[vmem] * 9,
        out_specs=[vmem] * 8,
        compiler_params=pltpu.CompilerParams(vmem_limit_bytes=VMEM_LIMIT),
        name="pairs",
    )(svt, *trials)
    a = [pieces[0]] + [swap(pieces[k], YX, 8, k) for k in range(1, 8)]

    zs = pl.pallas_call(
        main_kernel,
        out_shape=jax.ShapeDtypeStruct((8, 16, 8, 128), BF),
        in_specs=[smem, smem] + [vmem] * 21,
        out_specs=vmem,
        scratch_shapes=[
            pltpu.VMEM((8, 2, 512, 128), BF),
            pltpu.VMEM((8, 512, 128), BF),
            pltpu.VMEM((8, 128, 512), BF),
            pltpu.VMEM((16, 128, 512), F32),
        ],
        compiler_params=pltpu.CompilerParams(vmem_limit_bytes=VMEM_LIMIT),
        name="screen",
    )(me, pair_momentum, w_rep, *a, *a3, *b3, *c3)

    tv = val_target.reshape(16, 128)
    tv = jnp.stack(gathered(tv, "core", 2))
    tv = jnp.stack(gathered(tv, "xl", 2))
    tv = jnp.stack(gathered(tv, "y", 4)).reshape(2, 2, 2, 2, 2, 32, 32)
    tv = flip_if(y >> 1, tv, 0)
    tv = flip_if(y & 1, tv, 1)
    tv = flip_if(xl, tv, 2)
    tv = flip_if(core, tv, 3)
    tv = tv.reshape(16, 2, 32, 32).transpose(1, 2, 0, 3).reshape(2, 32, 64, 2, 4)
    tv = jnp.stack([tv, jnp.flip(tv, 3)], axis=3).reshape(64, 1024)

    arrived = lax.all_to_all(zs.reshape(128, 8, 128), ALL, split_axis=0, concat_axis=0, tiled=True)
    result = jnp.dot(tv, arrived.reshape(1024, 128), preferred_element_type=F32)
    result = result.reshape(2, 32, 2, 64)
    result = jnp.stack([result[0, :, 0], result[1, :, 1]])
    return result.reshape(2, 1, 2048)


def solution(mesh):
    fine = Mesh(mesh.devices.reshape(2, 4, 4, 2, 2), ALL)
    kt, ks = ("xh", "z"), ("y", "xl", "core")
    in_specs = (
        P(kt, None, ks),
        P(kt, None, ks),
        P(ks, None, kt),
        P(ks, None, kt),
        P(ks, kt, None),
        P(None, kt + ks, None),
        P(),
    )
    return jax.shard_map(local, mesh=fine, in_specs=in_specs, out_specs=P(kt, ks, None), check_vma=False)
```

time: 285 us -> 168 us (0.59)
  blocking collectives: 139 us -> 0 us
  local copies, waits for them, and re-layouts: 91.2 us -> 9.1 us
  starting transfers between devices: 12 us -> 90.1 us
  matrix products: 41.6 us -> 0.28 us
  waiting for transfers between devices: 0.01 us -> 31.1 us
  Pallas kernels: 0 us -> 23.5 us
  other arithmetic: 0.36 us -> 12.1 us
    all_gather x3 -> x0, blocking collectives: 119 us -> none  [the longest x1 59.9 us: rows_first(): lax.all_gather(both, axis, axis=0, tiled=True)]
    ppermute x0 -> x55, starting transfers between devices: none -> 71.2 us  [swap(): return lax.ppermute(x, axes, [(i, i ^ mask) for i in range(size)])]
    convert_element_type x4 -> x0, local copies, waits for them, and re-layouts: 56.9 us -> none  [the longest x1 44.3 us: local(): kernels = jnp.einsum('tsvwp,tspq->tsvwq', pair_prod, pair_mats, preferred...]
    dot_general x4 -> x1, matrix products: 41.6 us -> 0.28 us  [local(): result = jnp.dot(tv, arrived.reshape(1024, 128), preferred_element_type=F32)]
    pallas_call x0 -> x2, Pallas kernels: none -> 23.5 us  [the longest x1 21.3 us: local(): pl.pallas_call(main_kernel, out_shape=jax.ShapeDtypeStruct((8, 16, 8, 128...]
    ppermute x0 -> x55, waiting for transfers between devices: none -> 21.1 us  [swap(): return lax.ppermute(x, axes, [(i, i ^ mask) for i in range(size)])]
    all_to_all x1 -> x0, blocking collectives: 19.9 us -> none  [sum_at_owner(): lax.all_to_all(blocks, axis, split_axis=0, concat_axis=0, tiled=True)]
    gather x2 -> x0, local copies, waits for them, and re-layouts: 17.3 us -> none  [local(): outgoing = screened[table]]
  transfers between devices with their start and end apart: 1 -> 56, of which waited for: 0 -> 16; matrix products, arithmetic and copies ran while one was open for 5% -> 11% of each run, Pallas kernels for 0% -> 1%
where the time goes in v1:
time: 168 us; the launch traced here: 167 us
  starting transfers between devices  90.1 us (54%)
  waiting for transfers between devices  31.1 us (19%)
  Pallas kernels  23.5 us (14%)
  other arithmetic  12.1 us (7%)
  local copies, waits for them, and re-layouts  9.1 us (5%)
    ppermute x55, starting transfers between devices, swap(): return lax.ppermute(x, axes, [(i, i ^ mask) for i in range(size)])  71.2 us
    pallas_call x1, Pallas kernels, local(): pl.pallas_call(main_kernel, out_shape=jax.ShapeDtypeStruct((8, 16, 8, 128...  21.3 us
    ppermute x55, waiting for transfers between devices, swap(): return lax.ppermute(x, axes, [(i, i ^ mask) for i in range(size)])  21.1 us
    all_to_all x1, starting transfers between devices, local(): lax.all_to_all(zs.reshape(128, 8, 128), ALL, split_axis=0, concat_axis=0,...  18.9 us
    all_to_all x1, waiting for transfers between devices, local(): lax.all_to_all(zs.reshape(128, 8, 128), ALL, split_axis=0, concat_axis=0,...  10 us
    concatenate x1, other arithmetic, local(): w_rep = jnp.concatenate([screened, other, screened, other], axis=1)  9.87 us
  transfers between devices with their start and end apart: 56, of which 16 were waited for; matrix products, arithmetic and copies ran while one was open for 11% of the time, Pallas kernels for 1%

profile of v1, /device:TPU:1, one launch (start us, length us, event | category | flops | bytes accessed | tf_op | source)
XLA Modules:
  0.0 166.9 jit_solution(13428013113031662733)
XLA Ops:
  1.1 3.4 %collective-permute-start.22 = (bf16[64,128]{1,0:T(8,128)(2,1)S(1)}, bf16[64,128]{1,0:T(8,128)(2,1)S(1)}, u32[]{:S(2)}, u32[]{:S(2)}) collective-permute-start(bf16[64,128]{1,0:T(8,128)(2,1)S(1)} %bitcast.114), channel_id=1, source_target_pairs={{0,66},{2,64},{64,2},{66,0},{1,67},{3,65},{65,3},{67,1},{4,70},{6,... | collective-permute-start | bytes 49160 | tf_op jit(solution)/shard_map/ppermute | solution.py:19
  5.8 3.9 %collective-permute-start.35 = (bf16[16,128]{1,0:T(8,128)(2,1)S(1)}, bf16[16,128]{1,0:T(8,128)(2,1)S(1)}, u32[]{:S(2)}, u32[]{:S(2)}) collective-permute-start(bf16[16,128]{1,0:T(8,128)(2,1)S(1)} %slice.30), channel_id=1, source_target_pairs={{0,13},{1,12},{4,9},{5,8},{8,5},{9,4},{12,1},{13,0},{2,15},{3,14},... | collective-permute-start | bytes 12296 | tf_op jit(solution)/shard_map/ppermute | solution.py:19
  19.2 2.2 %collective-permute-done.1 = bf16[2,16,128]{2,1,0:T(8,128)(2,1)S(1)} collective-permute-done((bf16[2,16,128]{2,1,0:T(8,128)(2,1)S(1)}, bf16[2,16,128]{2,1,0:T(8,128)(2,1)S(1)}, u32[]{:S(2)}, u32[]{:S(2)}) %collective-permute-start.1) | collective-permute-done | bytes 8224 | tf_op jit(solution)/shard_map/ppermute | solution.py:19
  21.5 1.9 %collective-permute-start.34 = (bf16[48,128]{1,0:T(8,128)(2,1)S(1)}, bf16[48,128]{1,0:T(8,128)(2,1)S(1)}, u32[]{:S(2)}, u32[]{:S(2)}) collective-permute-start(bf16[48,128]{1,0:T(8,128)(2,1)S(1)} %pad_maximum_fusion.11), channel_id=1, source_target_pairs={{0,12},{4,8},{8,4},{12,0},{1,13},{5,9},{9,5},{13,1},{2,14},{6,10},... | collective-permute-start | bytes 36872 | tf_op jit(solution)/shard_map/ppermute | solution.py:19
  25.2 2.5 %collective-permute-start.5 = (bf16[512,4,512]{2,1,0:T(4,128)(2,1)}, bf16[512,4,512]{2,1,0:T(4,128)(2,1)}, u32[]{:S(2)}, u32[]{:S(2)}) collective-permute-start(bf16[512,4,512]{2,1,0:T(4,128)(2,1)} %param.12), channel_id=1, source_target_pairs={{0,1},{1,0},{2,3},{3,2},{4,5},{5,4},{6,7},{7,6},{8,9},{9,8},{10,11... | collective-permute-start | bytes 6291464 | tf_op jit(solution)/shard_map/ppermute | solution.py:19
  27.7 1.4 collective-permute-start.30
  29.1 1.6 collective-permute-done.31
  30.7 3.8 %collective-permute-start.48 = (bf16[16,128]{1,0:T(8,128)(2,1)S(1)}, bf16[16,128]{1,0:T(8,128)(2,1)S(1)}, u32[]{:S(2)}, u32[]{:S(2)}) collective-permute-start(bf16[16,128]{1,0:T(8,128)(2,1)S(1)} %slice.33), channel_id=1, source_target_pairs={{0,49},{1,48},{16,33},{17,32},{32,17},{33,16},{48,1},{49,0},{2,51}... | collective-permute-start | bytes 12296 | tf_op jit(solution)/shard_map/ppermute | solution.py:19
  35.9 1.8 %collective-permute-start.46 = (bf16[16,128]{1,0:T(8,128)(2,1)S(1)}, bf16[16,128]{1,0:T(8,128)(2,1)S(1)}, u32[]{:S(2)}, u32[]{:S(2)}) collective-permute-start(bf16[16,128]{1,0:T(8,128)(2,1)S(1)} %slice.33), channel_id=1, source_target_pairs={{0,33},{1,32},{16,49},{17,48},{32,1},{33,0},{48,17},{49,16},{2,35}... | collective-permute-start | bytes 12296 | tf_op jit(solution)/shard_map/ppermute | solution.py:19
  38.3 2.6 %collective-permute-start.45 = (bf16[48,128]{1,0:T(8,128)(2,1)S(1)}, bf16[48,128]{1,0:T(8,128)(2,1)S(1)}, u32[]{:S(2)}, u32[]{:S(2)}) collective-permute-start(bf16[48,128]{1,0:T(8,128)(2,1)S(1)} %pad_maximum_fusion.12), channel_id=1, source_target_pairs={{0,32},{16,48},{32,0},{48,16},{1,33},{17,49},{33,1},{49,17},{2,34}... | collective-permute-start | bytes 36872 | tf_op jit(solution)/shard_map/ppermute | solution.py:19
  41.0 2.4 %collective-permute-start.44 = (bf16[16,128]{1,0:T(8,128)(2,1)S(1)}, bf16[16,128]{1,0:T(8,128)(2,1)S(1)}, u32[]{:S(2)}, u32[]{:S(2)}) collective-permute-start(bf16[16,128]{1,0:T(8,128)(2,1)S(1)} %slice.33), channel_id=1, source_target_pairs={{0,17},{1,16},{16,1},{17,0},{32,49},{33,48},{48,33},{49,32},{2,19}... | collective-permute-start | bytes 12296 | tf_op jit(solution)/shard_map/ppermute | solution.py:19
  46.7 1.4 collective-permute-start.3
  49.0 1.4 collective-permute-start.7
  50.4 1.7 %collective-permute-start.8 = (bf16[2,32,256]{2,1,0:T(8,128)(2,1)S(1)}, bf16[2,32,256]{2,1,0:T(8,128)(2,1)S(1)}, u32[]{:S(2)}, u32[]{:S(2)}) collective-permute-start(bf16[2,32,256]{2,1,0:T(8,128)(2,1)S(1)} %reshape.65.refs_0_), channel_id=1, source_target_pairs={{0,48},{16,32},{32,16},{48,0},{64,112},{80,96},{96,80},{112,64},{1... | collective-permute-start | bytes 98312 | tf_op jit(solution)/shard_map/ppermute | solution.py:19
  53.2 1.8 %collective-permute-done.2 = bf16[2,2,16,128]{3,2,1,0:T(8,128)(2,1)S(1)} collective-permute-done((bf16[2,2,16,128]{3,2,1,0:T(8,128)(2,1)S(1)}, bf16[2,2,16,128]{3,2,1,0:T(8,128)(2,1)S(1)}, u32[]{:S(2)}, u32[]{:S(2)}) %collective-permute-start.2) | collective-permute-done | bytes 16416 | tf_op jit(solution)/shard_map/ppermute | solution.py:19
  55.0 2.5 %collective-permute-start.9 = (bf16[2,32,256]{2,1,0:T(8,128)(2,1)S(1)}, bf16[2,32,256]{2,1,0:T(8,128)(2,1)S(1)}, u32[]{:S(2)}, u32[]{:S(2)}) collective-permute-start(bf16[2,32,256]{2,1,0:T(8,128)(2,1)S(1)} %reshape.65.refs_0_), channel_id=1, source_target_pairs={{0,64},{16,80},{32,96},{48,112},{64,0},{80,16},{96,32},{112,48},{1... | collective-permute-start | bytes 98312 | tf_op jit(solution)/shard_map/ppermute | solution.py:19
  57.5 4.5 %collective-permute-start.11 = (bf16[2,32,256]{2,1,0:T(8,128)(2,1)S(1)}, bf16[2,32,256]{2,1,0:T(8,128)(2,1)S(1)}, u32[]{:S(2)}, u32[]{:S(2)}) collective-permute-start(bf16[2,32,256]{2,1,0:T(8,128)(2,1)S(1)} %reshape.65.refs_0_), channel_id=1, source_target_pairs={{0,96},{16,112},{32,64},{48,80},{64,32},{80,48},{96,0},{112,16},{1... | collective-permute-start | bytes 98312 | tf_op jit(solution)/shard_map/ppermute | solution.py:19
  62.0 1.9 %collective-permute-start.12 = (bf16[2,32,256]{2,1,0:T(8,128)(2,1)S(1)}, bf16[2,32,256]{2,1,0:T(8,128)(2,1)S(1)}, u32[]{:S(2)}, u32[]{:S(2)}) collective-permute-start(bf16[2,32,256]{2,1,0:T(8,128)(2,1)S(1)} %reshape.65.refs_0_), channel_id=1, source_target_pairs={{0,112},{16,96},{32,80},{48,64},{64,48},{80,32},{96,16},{112,0},{1... | collective-permute-start | bytes 98312 | tf_op jit(solution)/shard_map/ppermute | solution.py:19
  65.4 2.3 %collective-permute-start.36 = (bf16[4,64,128]{2,1,0:T(8,128)(2,1)S(1)}, bf16[4,64,128]{2,1,0:T(8,128)(2,1)S(1)}, u32[]{:S(2)}, u32[]{:S(2)}) collective-permute-start(bf16[4,64,128]{2,1,0:T(8,128)(2,1)S(1)} %get-tuple-element.28), channel_id=1, source_target_pairs={{0,16},{16,0},{32,48},{48,32},{1,17},{17,1},{33,49},{49,33},{2,18}... | collective-permute-start | bytes 196616 | tf_op jit(solution)/shard_map/ppermute | solution.py:19
  69.6 1.6 collective-permute-start.50
  73.2 2.2 %collective-permute-start.24 = (bf16[4,64,128]{2,1,0:T(8,128)(2,1)S(1)}, bf16[4,64,128]{2,1,0:T(8,128)(2,1)S(1)}, u32[]{:S(2)}, u32[]{:S(2)}) collective-permute-start(bf16[4,64,128]{2,1,0:T(8,128)(2,1)S(1)} %get-tuple-element.30), channel_id=1, source_target_pairs={{0,8},{4,12},{8,0},{12,4},{1,9},{5,13},{9,1},{13,5},{2,10},{6,14},... | collective-permute-start | bytes 196616 | tf_op jit(solution)/shard_map/ppermute | solution.py:19
  75.5 2.2 %pairs.1 = (bf16[2,128,128]{2,1,0:T(8,128)(2,1)}, bf16[2,128,128]{2,1,0:T(8,128)(2,1)}, bf16[2,128,128]{2,1,0:T(8,128)(2,1)}, bf16[2,128,128]{2,1,0:T(8,128)(2,1...) custom-call(bf16[4,64,32]{2,1,0:T(8,128)(2,1)} %bitcast.107, ...), custom_call_target="tpu_custom_call" | custom-call | tf_op jit(solution)/shard_map/pairs/pallas_call | solution.py:164
  80.9 2.1 %collective-permute-start.16 = (bf16[2,128,128]{2,1,0:T(8,128)(2,1)}, bf16[2,128,128]{2,1,0:T(8,128)(2,1)S(1)}, u32[]{:S(2)}, u32[]{:S(2)}) collective-permute-start(bf16[2,128,128]{2,1,0:T(8,128)(2,1)} %get-tuple-element.17), channel_id=1, source_target_pairs={{0,8},{2,10},{4,12},{6,14},{8,0},{10,2},{12,4},{14,6},{1,9},{3,11}... | collective-permute-start | bytes 196616 | tf_op jit(solution)/shard_map/ppermute | solution.py:19
  85.1 2.4 %collective-permute-start.19 = (bf16[2,128,128]{2,1,0:T(8,128)(2,1)}, bf16[2,128,128]{2,1,0:T(8,128)(2,1)S(1)}, u32[]{:S(2)}, u32[]{:S(2)}) collective-permute-start(bf16[2,128,128]{2,1,0:T(8,128)(2,1)} %get-tuple-element.20), channel_id=1, source_target_pairs={{0,14},{2,12},{4,10},{6,8},{8,6},{10,4},{12,2},{14,0},{1,15},{3,13... | collective-permute-start | bytes 196616 | tf_op jit(solution)/shard_map/ppermute | solution.py:19
  88.9 1.6 collective-permute-start.40
  91.6 2.2 %collective-permute-done.39.refs_13_ = bf16[4,4,64,128]{3,2,1,0:T(8,128)(2,1)S(1)} collective-permute-done((bf16[4,4,64,128]{3,2,1,0:T(8,128)(2,1)S(1)}, bf16[4,4,64,128]{3,2,1,0:T(8,128)(2,1)S(1)}, u32[]{:S(2)}, u32[]{:S(2)}) %collective-permute-start.39) | collective-permute-done | bytes 262176 | tf_op jit(solution)/shard_map/ppermute | solution.py:19
  94.4 4.1 %collective-permute-done.40.refs_14_ = bf16[4,4,64,128]{3,2,1,0:T(8,128)(2,1)S(1)} collective-permute-done((bf16[4,4,64,128]{3,2,1,0:T(8,128)(2,1)S(1)}, bf16[4,4,64,128]{3,2,1,0:T(8,128)(2,1)S(1)}, u32[]{:S(2)}, u32[]{:S(2)}) %collective-permute-start.40) | collective-permute-done | bytes 262176 | tf_op jit(solution)/shard_map/ppermute | solution.py:19
  100.0 2.3 %collective-permute-start.27 = (bf16[4,4,64,128]{3,2,1,0:T(8,128)(2,1)S(1)}, bf16[4,4,64,128]{3,2,1,0:T(8,128)(2,1)S(1)}, u32[]{:S(2)}, u32[]{:S(2)}) collective-permute-start(bf16[4,4,64,128]{3,2,1,0:T(8,128)(2,1)S(1)} %pad_maximum_fusion.2.refs_8_), channel_id=1, source_target_pairs={{0,32},{16,48},{32,0},{48,16},{1,33},{17,49},{33,1},{49,17},{2,34}... | collective-permute-start | bytes 786440 | tf_op jit(solution)/shard_map/ppermute | solution.py:19
  103.6 9.9 %pad_maximum_fusion.w_ref = bf16[512,16,512]{2,1,0:T(8,128)(2,1)} fusion(bf16[512,4,512]{2,1,0:T(4,128)(2,1)} %collective-permute-done.5, bf16[512,4,512]{2,1,0:T(4,128)(2,1)S(1)} %copy-done), kind=kLoop, calls=%fused_computation | loop fusion | flops 33554432 | bytes 12582912 | tf_op jit(solution)/shard_map/concatenate | solution.py:141
  114.6 21.3 %screen.1 = bf16[8,16,8,128]{3,2,1,0:T(8,128)(2,1)} custom-call(s32[8]{0:T(128)} %stack.168.me_ref, s32[16,64]{1,0:T(8,128)} %pm_ref.1, bf16[512,16,512]{2,1,0:T(8,128)(2,1)} %pad_maximum_fusion.w_ref, bf16[2,128,128]{2,1,0:T(8,128)(2,1)} %get-tuple-element.13.refs_0_, bf16[2,128,128]{2,1,0:T(8,128)(2,1)} %copy-done.14, bf16[2,128,128]{2,1,0:T(8,128)(2,1)} %copy-done.15, ...), custom_call_target="tpu_custom_call" | custom-call | tf_op jit(solution)/shard_map/screen/pallas_call | solution.py:174
  135.9 18.9 %all-to-all-start = ((bf16[128,8,128]{2,1,0:T(8,128)(2,1)}), bf16[128,8,128]{2,1,0:T(8,128)(2,1)S(1)}, u32[]{:S(2)}, u32[]{:S(2)}) async-start(bf16[128,8,128]{2,1,0:T(8,128)(2,1)} %bitcast.102), calls=%async_computation | async-start | bytes 524288 | tf_op jit(solution)/shard_map/all_to_all | solution.py:200
  155.6 10.0 %all-to-all-done = bf16[128,8,128]{2,1,0:T(8,128)(2,1)S(1)} async-done(((bf16[128,8,128]{2,1,0:T(8,128)(2,1)}), bf16[128,8,128]{2,1,0:T(8,128)(2,1)S(1)}, u32[]{:S(2)}, u32[]{:S(2)}) %all-to-all-start) | async-done | bytes 262176 | tf_op jit(solution)/shard_map/all_to_all | solution.py:200
  (193 shorter events, 40.3 us)
Async XLA Ops:
  1.1 45.7 %collective-permute-start.22 = (bf16[64,128]{1,0:T(8,128)(2,1)S(1)}, bf16[64,128]{1,0:T(8,128)(2,1)S(1)}, u32[]{:S(2)}, u32[]{:S(2)}) collective-permute-start(bf16[64,128]{1,0:T(8,128)(2,1)S(1)} %bitcast.114), channel_id=1, source_target_pairs={{0,66},{2,64},{64,2},{66,0},{1,67},{3,65},{65,3},{67,1},{4,70},{6,... | collective-permute-start | bytes 49160 | tf_op jit(solution)/shard_map/ppermute | solution.py:19
  4.4 43.7 %collective-permute-start.21 = (bf16[64,128]{1,0:T(8,128)(2,1)S(1)}, bf16[64,128]{1,0:T(8,128)(2,1)S(1)}, u32[]{:S(2)}, u32[]{:S(2)}) collective-permute-start(bf16[64,128]{1,0:T(8,128)(2,1)S(1)} %bitcast.115), channel_id=1, source_target_pairs={{0,64},{2,66},{64,0},{66,2},{1,65},{3,67},{65,1},{67,3},{4,68},{6,... | collective-permute-start | bytes 49160 | tf_op jit(solution)/shard_map/ppermute | solution.py:19
  5.8 17.6 %collective-permute-start.35 = (bf16[16,128]{1,0:T(8,128)(2,1)S(1)}, bf16[16,128]{1,0:T(8,128)(2,1)S(1)}, u32[]{:S(2)}, u32[]{:S(2)}) collective-permute-start(bf16[16,128]{1,0:T(8,128)(2,1)S(1)} %slice.30), channel_id=1, source_target_pairs={{0,13},{1,12},{4,9},{5,8},{8,5},{9,4},{12,1},{13,0},{2,15},{3,14},... | collective-permute-start | bytes 12296 | tf_op jit(solution)/shard_map/ppermute | solution.py:19
  9.6 18.0 %collective-permute-start.33 = (bf16[16,128]{1,0:T(8,128)(2,1)S(1)}, bf16[16,128]{1,0:T(8,128)(2,1)S(1)}, u32[]{:S(2)}, u32[]{:S(2)}) collective-permute-start(bf16[16,128]{1,0:T(8,128)(2,1)S(1)} %slice.30), channel_id=1, source_target_pairs={{0,9},{1,8},{4,13},{5,12},{8,1},{9,0},{12,5},{13,4},{2,11},{3,10},... | collective-permute-start | bytes 12296 | tf_op jit(solution)/shard_map/ppermute | solution.py:19
  9.9 6.7 %collective-permute-start.29 = (bf16[16,128]{1,0:T(8,128)(2,1)S(1)}, bf16[16,128]{1,0:T(8,128)(2,1)S(1)}, u32[]{:S(2)}, u32[]{:S(2)}) collective-permute-start(bf16[16,128]{1,0:T(8,128)(2,1)S(1)} %slice.30), channel_id=1, source_target_pairs={{0,1},{1,0},{4,5},{5,4},{8,9},{9,8},{12,13},{13,12},{2,3},{3,2},{6... | collective-permute-start | bytes 12296 | tf_op jit(solution)/shard_map/ppermute | solution.py:19
  25.2 77.1 %collective-permute-start.5 = (bf16[512,4,512]{2,1,0:T(4,128)(2,1)}, bf16[512,4,512]{2,1,0:T(4,128)(2,1)}, u32[]{:S(2)}, u32[]{:S(2)}) collective-permute-start(bf16[512,4,512]{2,1,0:T(4,128)(2,1)} %param.12), channel_id=1, source_target_pairs={{0,1},{1,0},{2,3},{3,2},{4,5},{5,4},{6,7},{7,6},{8,9},{9,8},{10,11... | collective-permute-start | bytes 6291464 | tf_op jit(solution)/shard_map/ppermute | solution.py:19
  27.7 6.9 %collective-permute-start.30 = (bf16[48,128]{1,0:T(8,128)(2,1)S(1)}, bf16[48,128]{1,0:T(8,128)(2,1)S(1)}, u32[]{:S(2)}, u32[]{:S(2)}) collective-permute-start(bf16[48,128]{1,0:T(8,128)(2,1)S(1)} %pad_maximum_fusion.11), channel_id=1, source_target_pairs={{0,4},{4,0},{8,12},{12,8},{1,5},{5,1},{9,13},{13,9},{2,6},{6,2},{1... | collective-permute-start | bytes 36872 | tf_op jit(solution)/shard_map/ppermute | solution.py:19
  48.2 9.3 %collective-permute-start.6 = (bf16[2,32,256]{2,1,0:T(8,128)(2,1)S(1)}, bf16[2,32,256]{2,1,0:T(8,128)(2,1)S(1)}, u32[]{:S(2)}, u32[]{:S(2)}) collective-permute-start(bf16[2,32,256]{2,1,0:T(8,128)(2,1)S(1)} %reshape.65.refs_0_), channel_id=1, source_target_pairs={{0,16},{16,0},{32,48},{48,32},{64,80},{80,64},{96,112},{112,96},{1... | collective-permute-start | bytes 98312 | tf_op jit(solution)/shard_map/ppermute | solution.py:19
  49.0 8.5 %collective-permute-start.7 = (bf16[2,32,256]{2,1,0:T(8,128)(2,1)S(1)}, bf16[2,32,256]{2,1,0:T(8,128)(2,1)S(1)}, u32[]{:S(2)}, u32[]{:S(2)}) collective-permute-start(bf16[2,32,256]{2,1,0:T(8,128)(2,1)S(1)} %reshape.65.refs_0_), channel_id=1, source_target_pairs={{0,32},{16,48},{32,0},{48,16},{64,96},{80,112},{96,64},{112,80},{1... | collective-permute-start | bytes 98312 | tf_op jit(solution)/shard_map/ppermute | solution.py:19
  50.4 11.6 %collective-permute-start.8 = (bf16[2,32,256]{2,1,0:T(8,128)(2,1)S(1)}, bf16[2,32,256]{2,1,0:T(8,128)(2,1)S(1)}, u32[]{:S(2)}, u32[]{:S(2)}) collective-permute-start(bf16[2,32,256]{2,1,0:T(8,128)(2,1)S(1)} %reshape.65.refs_0_), channel_id=1, source_target_pairs={{0,48},{16,32},{32,16},{48,0},{64,112},{80,96},{96,80},{112,64},{1... | collective-permute-start | bytes 98312 | tf_op jit(solution)/shard_map/ppermute | solution.py:19
  55.0 9.3 %collective-permute-start.9 = (bf16[2,32,256]{2,1,0:T(8,128)(2,1)S(1)}, bf16[2,32,256]{2,1,0:T(8,128)(2,1)S(1)}, u32[]{:S(2)}, u32[]{:S(2)}) collective-permute-start(bf16[2,32,256]{2,1,0:T(8,128)(2,1)S(1)} %reshape.65.refs_0_), channel_id=1, source_target_pairs={{0,64},{16,80},{32,96},{48,112},{64,0},{80,16},{96,32},{112,48},{1... | collective-permute-start | bytes 98312 | tf_op jit(solution)/shard_map/ppermute | solution.py:19
  57.4 7.9 %collective-permute-start.10 = (bf16[2,32,256]{2,1,0:T(8,128)(2,1)S(1)}, bf16[2,32,256]{2,1,0:T(8,128)(2,1)S(1)}, u32[]{:S(2)}, u32[]{:S(2)}) collective-permute-start(bf16[2,32,256]{2,1,0:T(8,128)(2,1)S(1)} %reshape.65.refs_0_), channel_id=1, source_target_pairs={{0,80},{16,64},{32,112},{48,96},{64,16},{80,0},{96,48},{112,32},{1... | collective-permute-start | bytes 98312 | tf_op jit(solution)/shard_map/ppermute | solution.py:19
  57.5 7.9 %collective-permute-start.11 = (bf16[2,32,256]{2,1,0:T(8,128)(2,1)S(1)}, bf16[2,32,256]{2,1,0:T(8,128)(2,1)S(1)}, u32[]{:S(2)}, u32[]{:S(2)}) collective-permute-start(bf16[2,32,256]{2,1,0:T(8,128)(2,1)S(1)} %reshape.65.refs_0_), channel_id=1, source_target_pairs={{0,96},{16,112},{32,64},{48,80},{64,32},{80,48},{96,0},{112,16},{1... | collective-permute-start | bytes 98312 | tf_op jit(solution)/shard_map/ppermute | solution.py:19
  62.0 6.8 %collective-permute-start.12 = (bf16[2,32,256]{2,1,0:T(8,128)(2,1)S(1)}, bf16[2,32,256]{2,1,0:T(8,128)(2,1)S(1)}, u32[]{:S(2)}, u32[]{:S(2)}) collective-permute-start(bf16[2,32,256]{2,1,0:T(8,128)(2,1)S(1)} %reshape.65.refs_0_), channel_id=1, source_target_pairs={{0,112},{16,96},{32,80},{48,64},{64,48},{80,32},{96,16},{112,0},{1... | collective-permute-start | bytes 98312 | tf_op jit(solution)/shard_map/ppermute | solution.py:19
  65.4 6.8 %collective-permute-start.36 = (bf16[4,64,128]{2,1,0:T(8,128)(2,1)S(1)}, bf16[4,64,128]{2,1,0:T(8,128)(2,1)S(1)}, u32[]{:S(2)}, u32[]{:S(2)}) collective-permute-start(bf16[4,64,128]{2,1,0:T(8,128)(2,1)S(1)} %get-tuple-element.28), channel_id=1, source_target_pairs={{0,16},{16,0},{32,48},{48,32},{1,17},{17,1},{33,49},{49,33},{2,18}... | collective-permute-start | bytes 196616 | tf_op jit(solution)/shard_map/ppermute | solution.py:19
  69.6 8.1 %collective-permute-start.50 = (bf16[4,64,128]{2,1,0:T(8,128)(2,1)S(1)}, bf16[4,64,128]{2,1,0:T(8,128)(2,1)S(1)}, u32[]{:S(2)}, u32[]{:S(2)}) collective-permute-start(bf16[4,64,128]{2,1,0:T(8,128)(2,1)S(1)} %get-tuple-element.24), channel_id=1, source_target_pairs={{0,64},{2,66},{64,0},{66,2},{1,65},{3,67},{65,1},{67,3},{4,68},{6,... | collective-permute-start | bytes 196616 | tf_op jit(solution)/shard_map/ppermute | solution.py:19
  71.2 6.7 %collective-permute-start.49 = (bf16[4,64,128]{2,1,0:T(8,128)(2,1)S(1)}, bf16[4,64,128]{2,1,0:T(8,128)(2,1)S(1)}, u32[]{:S(2)}, u32[]{:S(2)}) collective-permute-start(bf16[4,64,128]{2,1,0:T(8,128)(2,1)S(1)} %get-tuple-element.24), channel_id=1, source_target_pairs={{0,2},{2,0},{64,66},{66,64},{1,3},{3,1},{65,67},{67,65},{4,6},{6,4... | collective-permute-start | bytes 196616 | tf_op jit(solution)/shard_map/ppermute | solution.py:19
  72.2 6.1 %collective-permute-start.25 = (bf16[4,64,128]{2,1,0:T(8,128)(2,1)S(1)}, bf16[4,64,128]{2,1,0:T(8,128)(2,1)S(1)}, u32[]{:S(2)}, u32[]{:S(2)}) collective-permute-start(bf16[4,64,128]{2,1,0:T(8,128)(2,1)S(1)} %get-tuple-element.30), channel_id=1, source_target_pairs={{0,12},{4,8},{8,4},{12,0},{1,13},{5,9},{9,5},{13,1},{2,14},{6,10},... | collective-permute-start | bytes 196616 | tf_op jit(solution)/shard_map/ppermute | solution.py:19
  73.2 6.4 %collective-permute-start.24 = (bf16[4,64,128]{2,1,0:T(8,128)(2,1)S(1)}, bf16[4,64,128]{2,1,0:T(8,128)(2,1)S(1)}, u32[]{:S(2)}, u32[]{:S(2)}) collective-permute-start(bf16[4,64,128]{2,1,0:T(8,128)(2,1)S(1)} %get-tuple-element.30), channel_id=1, source_target_pairs={{0,8},{4,12},{8,0},{12,4},{1,9},{5,13},{9,1},{13,5},{2,10},{6,14},... | collective-permute-start | bytes 196616 | tf_op jit(solution)/shard_map/ppermute | solution.py:19
  80.9 6.6 %collective-permute-start.16 = (bf16[2,128,128]{2,1,0:T(8,128)(2,1)}, bf16[2,128,128]{2,1,0:T(8,128)(2,1)S(1)}, u32[]{:S(2)}, u32[]{:S(2)}) collective-permute-start(bf16[2,128,128]{2,1,0:T(8,128)(2,1)} %get-tuple-element.17), channel_id=1, source_target_pairs={{0,8},{2,10},{4,12},{6,14},{8,0},{10,2},{12,4},{14,6},{1,9},{3,11}... | collective-permute-start | bytes 196616 | tf_op jit(solution)/shard_map/ppermute | solution.py:19
  84.1 6.4 %collective-permute-start.18 = (bf16[2,128,128]{2,1,0:T(8,128)(2,1)}, bf16[2,128,128]{2,1,0:T(8,128)(2,1)S(1)}, u32[]{:S(2)}, u32[]{:S(2)}) collective-permute-start(bf16[2,128,128]{2,1,0:T(8,128)(2,1)} %get-tuple-element.19), channel_id=1, source_target_pairs={{0,12},{2,14},{4,8},{6,10},{8,4},{10,6},{12,0},{14,2},{1,13},{3,15... | collective-permute-start | bytes 196616 | tf_op jit(solution)/shard_map/ppermute | solution.py:19
  85.1 6.4 %collective-permute-start.19 = (bf16[2,128,128]{2,1,0:T(8,128)(2,1)}, bf16[2,128,128]{2,1,0:T(8,128)(2,1)S(1)}, u32[]{:S(2)}, u32[]{:S(2)}) collective-permute-start(bf16[2,128,128]{2,1,0:T(8,128)(2,1)} %get-tuple-element.20), channel_id=1, source_target_pairs={{0,14},{2,12},{4,10},{6,8},{8,6},{10,4},{12,2},{14,0},{1,15},{3,13... | collective-permute-start | bytes 196616 | tf_op jit(solution)/shard_map/ppermute | solution.py:19
  87.5 6.3 %collective-permute-start.39 = (bf16[4,4,64,128]{3,2,1,0:T(8,128)(2,1)S(1)}, bf16[4,4,64,128]{3,2,1,0:T(8,128)(2,1)S(1)}, u32[]{:S(2)}, u32[]{:S(2)}) collective-permute-start(bf16[4,4,64,128]{3,2,1,0:T(8,128)(2,1)S(1)} %pad_maximum_fusion.3.refs_12_), channel_id=1, source_target_pairs={{0,2},{2,0},{64,66},{66,64},{1,3},{3,1},{65,67},{67,65},{4,6},{6,4... | collective-permute-start | bytes 786440 | tf_op jit(solution)/shard_map/ppermute | solution.py:19
  88.9 9.7 %collective-permute-start.40 = (bf16[4,4,64,128]{3,2,1,0:T(8,128)(2,1)S(1)}, bf16[4,4,64,128]{3,2,1,0:T(8,128)(2,1)S(1)}, u32[]{:S(2)}, u32[]{:S(2)}) collective-permute-start(bf16[4,4,64,128]{3,2,1,0:T(8,128)(2,1)S(1)} %pad_maximum_fusion.3.refs_12_), channel_id=1, source_target_pairs={{0,64},{2,66},{64,0},{66,2},{1,65},{3,67},{65,1},{67,3},{4,68},{6,... | collective-permute-start | bytes 786440 | tf_op jit(solution)/shard_map/ppermute | solution.py:19
  90.5 9.2 %collective-permute-start.41 = (bf16[4,4,64,128]{3,2,1,0:T(8,128)(2,1)S(1)}, bf16[4,4,64,128]{3,2,1,0:T(8,128)(2,1)S(1)}, u32[]{:S(2)}, u32[]{:S(2)}) collective-permute-start(bf16[4,4,64,128]{3,2,1,0:T(8,128)(2,1)S(1)} %pad_maximum_fusion.3.refs_12_), channel_id=1, source_target_pairs={{0,66},{2,64},{64,2},{66,0},{1,67},{3,65},{65,3},{67,1},{4,70},{6,... | collective-permute-start | bytes 786440 | tf_op jit(solution)/shard_map/ppermute | solution.py:19
  91.5 8.5 %collective-permute-start.52 = (bf16[4,4,64,128]{3,2,1,0:T(8,128)(2,1)S(1)}, bf16[4,4,64,128]{3,2,1,0:T(8,128)(2,1)S(1)}, u32[]{:S(2)}, u32[]{:S(2)}) collective-permute-start(bf16[4,4,64,128]{3,2,1,0:T(8,128)(2,1)S(1)} %pad_maximum_fusion.4.refs_16_), channel_id=1, source_target_pairs={{0,4},{4,0},{8,12},{12,8},{1,5},{5,1},{9,13},{13,9},{2,6},{6,2},{1... | collective-permute-start | bytes 786440 | tf_op jit(solution)/shard_map/ppermute | solution.py:19
  93.8 19.7 %collective-permute-start.53 = (bf16[4,4,64,128]{3,2,1,0:T(8,128)(2,1)S(1)}, bf16[4,4,64,128]{3,2,1,0:T(8,128)(2,1)S(1)}, u32[]{:S(2)}, u32[]{:S(2)}) collective-permute-start(bf16[4,4,64,128]{3,2,1,0:T(8,128)(2,1)S(1)} %pad_maximum_fusion.4.refs_16_), channel_id=1, source_target_pairs={{0,8},{4,12},{8,0},{12,4},{1,9},{5,13},{9,1},{13,5},{2,10},{6,14},... | collective-permute-start | bytes 786440 | tf_op jit(solution)/shard_map/ppermute | solution.py:19
  98.6 14.9 %collective-permute-start.54 = (bf16[4,4,64,128]{3,2,1,0:T(8,128)(2,1)S(1)}, bf16[4,4,64,128]{3,2,1,0:T(8,128)(2,1)S(1)}, u32[]{:S(2)}, u32[]{:S(2)}) collective-permute-start(bf16[4,4,64,128]{3,2,1,0:T(8,128)(2,1)S(1)} %pad_maximum_fusion.4.refs_16_), channel_id=1, source_target_pairs={{0,12},{4,8},{8,4},{12,0},{1,13},{5,9},{9,5},{13,1},{2,14},{6,10},... | collective-permute-start | bytes 786440 | tf_op jit(solution)/shard_map/ppermute | solution.py:19
  99.7 13.8 %collective-permute-start.26 = (bf16[4,4,64,128]{3,2,1,0:T(8,128)(2,1)S(1)}, bf16[4,4,64,128]{3,2,1,0:T(8,128)(2,1)S(1)}, u32[]{:S(2)}, u32[]{:S(2)}) collective-permute-start(bf16[4,4,64,128]{3,2,1,0:T(8,128)(2,1)S(1)} %pad_maximum_fusion.2.refs_8_), channel_id=1, source_target_pairs={{0,16},{16,0},{32,48},{48,32},{1,17},{17,1},{33,49},{49,33},{2,18}... | collective-permute-start | bytes 786440 | tf_op jit(solution)/shard_map/ppermute | solution.py:19
  100.0 13.5 %collective-permute-start.27 = (bf16[4,4,64,128]{3,2,1,0:T(8,128)(2,1)S(1)}, bf16[4,4,64,128]{3,2,1,0:T(8,128)(2,1)S(1)}, u32[]{:S(2)}, u32[]{:S(2)}) collective-permute-start(bf16[4,4,64,128]{3,2,1,0:T(8,128)(2,1)S(1)} %pad_maximum_fusion.2.refs_8_), channel_id=1, source_target_pairs={{0,32},{16,48},{32,0},{48,16},{1,33},{17,49},{33,1},{49,17},{2,34}... | collective-permute-start | bytes 786440 | tf_op jit(solution)/shard_map/ppermute | solution.py:19
  102.3 11.3 %collective-permute-start.28 = (bf16[4,4,64,128]{3,2,1,0:T(8,128)(2,1)S(1)}, bf16[4,4,64,128]{3,2,1,0:T(8,128)(2,1)S(1)}, u32[]{:S(2)}, u32[]{:S(2)}) collective-permute-start(bf16[4,4,64,128]{3,2,1,0:T(8,128)(2,1)S(1)} %pad_maximum_fusion.2.refs_8_), channel_id=1, source_target_pairs={{0,48},{16,32},{32,16},{48,0},{1,49},{17,33},{33,17},{49,1},{2,50}... | collective-permute-start | bytes 786440 | tf_op jit(solution)/shard_map/ppermute | solution.py:19
  135.9 29.8 %all-to-all-start = ((bf16[128,8,128]{2,1,0:T(8,128)(2,1)}), bf16[128,8,128]{2,1,0:T(8,128)(2,1)S(1)}, u32[]{:S(2)}, u32[]{:S(2)}) async-start(bf16[128,8,128]{2,1,0:T(8,128)(2,1)} %bitcast.102), calls=%async_computation | async-start | bytes 524288 | tf_op jit(solution)/shard_map/all_to_all | solution.py:200
  (52 other events, 683.0 us)

commit v2 on v1

v2 whole, which is shorter than its diff:
```python
import jax
import jax.numpy as jnp
from jax import lax
from jax.experimental import pallas as pl
from jax.experimental.pallas import tpu as pltpu
from jax.sharding import Mesh
from jax.sharding import PartitionSpec as P

ALL = ("xh", "z", "y", "xl", "core")
YX = ("y", "xl")
KT = ("xh", "z")
CHIPS = ("xh", "z", "y", "xl")
CS, CT, TV, ROWS = 256, 1280, 1536, 1552
BF = jnp.bfloat16
F32 = jnp.float32
VMEM_LIMIT = 24 * 1024 * 1024


def swap(x, axes, size, mask):
    return lax.ppermute(x, axes, [(i, i ^ mask) for i in range(size)])


def flip_if(bit, x, axis):
    return jnp.where(bit == 1, jnp.flip(x, axis), x)


def pair_kernel(svt_ref, first_ref, tv_ref, out_ref):
    lane = lax.broadcasted_iota(jnp.int32, (64, 256), 1)
    even_s = (lane & 64) == 0
    for k in range(8):
        for sp in range(2):
            at = sp * 32
            block = jnp.concatenate([first_ref[k, at : at + 32], first_ref[k, 64 + at : 96 + at]], axis=1)
            even = jnp.dot(svt_ref[2 * sp], block, preferred_element_type=F32)
            odd = jnp.dot(svt_ref[2 * sp + 1], block, preferred_element_type=F32)
            both = jnp.where(even_s, even, odd)
            for peer in range(8):
                rows = both[peer * 8 : peer * 8 + 8]
                piece = jnp.concatenate([rows[:, :128], rows[:, 128:]], axis=0)
                at = sp * 128 + k * 16
                out_ref[peer, at : at + 16, :] = piece.astype(BF)
            factors = first_ref[k, 128 + sp * 64 : 192 + sp * 64]
            for peer in range(8):
                at = CS + sp * 512 + k * 64
                out_ref[peer, at : at + 64, :] = factors
        factors = first_ref[k, 256:288]
        for peer in range(8):
            out_ref[peer, CT + k * 32 : CT + k * 32 + 32, :] = factors
    for peer in range(8):
        out_ref[peer, TV:ROWS, :] = tv_ref[...]


def repeat_kernel(own_ref, other_ref, out_ref):
    eight = jnp.concatenate([own_ref[...], other_ref[...]], axis=1)
    out_ref[...] = jnp.concatenate([eight, eight], axis=1)


def screen_kernel(core_ref, pm_ref, w_hbm, all_ref, out_ref, w_ref, xs, acc, sem):
    fetch = pltpu.make_async_copy(w_hbm, w_ref, sem)
    fetch.start()
    core = core_ref[0]
    lane = lax.broadcasted_iota(jnp.int32, (128, 128), 1)
    first = lane < 64

    def one_chip(yx, carry):
        for sp in range(2):
            a = all_ref[yx, sp * 128 : sp * 128 + 128]
            none = jnp.zeros_like(a)
            lhs = jnp.concatenate([jnp.where(first, a, none), jnp.where(first, none, a)], axis=0)
            rhs = all_ref[yx, CS + sp * 512 : CS + sp * 512 + 512]
            x = lax.dot_general(
                lhs, rhs, (((1,), (1,)), ((), ())), preferred_element_type=F32
            ).astype(BF)
            xs[yx * 4 + sp * 2] = x[:128]
            xs[yx * 4 + sp * 2 + 1] = x[128:]
        return carry

    lax.fori_loop(0, 8, one_chip, 0)
    fetch.wait()
    for chunk in range(4):

        def one_target(t, carry, chunk=chunk):
            mats = []
            for jj in range(2):
                source = ((chunk * 2 + jj) * 2 + core) * 4
                mats += [pm_ref[t, source + i] for i in range(4)]
            for qb in range(4):
                lanes = slice(qb * 128, qb * 128 + 128)
                w = [w_ref[m, :, lanes] for m in mats]
                for nb in range(8):
                    rows = slice(nb * 16, nb * 16 + 16)
                    terms = [w[i] * xs[chunk * 8 + i, rows, lanes] for i in range(8)]
                    while len(terms) > 1:
                        terms = [terms[i] + terms[i + 1] for i in range(0, len(terms), 2)]
                    total = terms[0].astype(F32)
                    if chunk > 0:
                        total = total + acc[t, rows, lanes]
                    if chunk < 3:
                        acc[t, rows, lanes] = total
                    else:
                        out_ref[t, rows, lanes] = total.astype(BF)
            return carry

        lax.fori_loop(0, 16, one_target, 0)


def project_kernel(core_ref, y_ref, all_ref, other_ref, keep_ref, give_ref, ct):
    core = core_ref[0]
    lane = lax.broadcasted_iota(jnp.int32, (128, 128), 1)
    first = lane < 64

    def project(kt, carry):
        for yx in range(8):
            ct[pl.ds(pl.multiple_of((yx * 2 + core) * 32, 32), 32), :] = all_ref[
                yx, pl.ds(pl.multiple_of(CT + kt * 32, 32), 32), :
            ]
            ct[pl.ds(pl.multiple_of((yx * 2 + 1 - core) * 32, 32), 32), :] = other_ref[
                yx, pl.ds(pl.multiple_of(kt * 32, 32), 32), :
            ]
        c = ct[...]
        z0 = jnp.dot(y_ref[2 * kt], c, preferred_element_type=F32)
        z1 = jnp.dot(y_ref[2 * kt + 1], c, preferred_element_type=F32)
        zz = jnp.where(first, z0, z1).reshape(8, 2, 8, 128)
        keep_ref[kt] = jnp.where(core == 0, zz[:, 0], zz[:, 1]).astype(BF)
        give = jnp.where(core == 0, zz[:, 1], zz[:, 0])
        give_ref[kt] = jnp.concatenate([give[:, 4:], give[:, :4]], axis=1).astype(BF)
        return carry

    lax.fori_loop(0, 8, project, 0)


def local(val_target, cond_target, val_source, cond_source, trial_vectors, screened, pair_momentum):
    core = lax.axis_index("core")
    me = core.astype(jnp.int32).reshape(1)
    vmem = pl.BlockSpec(memory_space=pltpu.VMEM)
    smem = pl.BlockSpec(memory_space=pltpu.SMEM)
    params = pltpu.CompilerParams(vmem_limit_bytes=VMEM_LIMIT)

    def all_to_all(x, axes):
        return lax.all_to_all(x, axes, split_axis=0, concat_axis=0, tiled=True)

    trial = trial_vectors.reshape(2, 2, 2, 32, 64).transpose(2, 0, 3, 1, 4).reshape(128, 128)
    cs = cond_source.reshape(2, 2, 64, 64).transpose(0, 3, 1, 2).reshape(128, 128)
    ct = cond_target.transpose(2, 0, 1).reshape(32, 128)
    block = jnp.concatenate([trial, cs, ct], axis=0)
    near = all_to_all(jnp.broadcast_to(block[None], (8, 288, 128)), KT)

    other = swap(screened, "core", 2, 1)
    w_rows = pl.pallas_call(
        repeat_kernel,
        out_shape=jax.ShapeDtypeStruct((512, 16, 512), BF),
        grid=(8,),
        in_specs=[pl.BlockSpec((64, 4, 512), lambda i: (i, 0, 0))] * 2,
        out_specs=pl.BlockSpec((64, 16, 512), lambda i: (i, 0, 0)),
        compiler_params=params,
        name="rows",
    )(screened, other)
    near, w_rows = lax.optimization_barrier((near, w_rows))

    sv = flip_if(core, val_source.reshape(4, 32, 8, 2, 4), 3)
    svt = sv.reshape(4, 32, 64).transpose(0, 2, 1)
    pieces = pl.pallas_call(
        pair_kernel,
        out_shape=jax.ShapeDtypeStruct((8, ROWS, 128), BF),
        in_specs=[vmem] * 3,
        out_specs=vmem,
        compiler_params=params,
        name="pairs",
    )(svt, near, val_target.reshape(16, 128))
    every = all_to_all(pieces, YX)

    ys = pl.pallas_call(
        screen_kernel,
        out_shape=jax.ShapeDtypeStruct((16, 128, 512), BF),
        in_specs=[smem, smem, pl.BlockSpec(memory_space=pltpu.HBM), vmem],
        out_specs=vmem,
        scratch_shapes=[
            pltpu.VMEM((512, 16, 512), BF),
            pltpu.VMEM((32, 128, 512), BF),
            pltpu.VMEM((16, 128, 512), F32),
            pltpu.SemaphoreType.DMA,
        ],
        compiler_params=params,
        name="screen",
    )(me, pair_momentum, w_rows, every)
    ct_other = swap(every[:, CT:TV], "core", 2, 1)
    keep, give = pl.pallas_call(
        project_kernel,
        out_shape=[jax.ShapeDtypeStruct((8, 8, 8, 128), BF)] * 2,
        in_specs=[smem, vmem, vmem, vmem],
        out_specs=[vmem, vmem],
        scratch_shapes=[pltpu.VMEM((512, 128), BF)],
        compiler_params=params,
        name="project",
    )(me, ys, every, ct_other)
    taken = swap(give, "core", 2, 1)
    zs = (keep.astype(F32) + taken.astype(F32)).astype(BF)

    tv = every[:, TV:]
    tv_other = swap(tv, "core", 2, 1).reshape(8, 2, 32, 32)
    tv = tv.reshape(8, 2, 32, 32)
    tv = jnp.where(core == 0, jnp.stack([tv, tv_other], axis=1), jnp.stack([tv_other, tv], axis=1))
    tv = tv.transpose(2, 3, 0, 1, 4).reshape(2, 32, 64, 2, 4)
    tv = flip_if(core, tv, 3).reshape(64, 512)

    arrived = all_to_all(zs.reshape(64, 8, 128), CHIPS)
    result = jnp.dot(tv, arrived.reshape(512, 128), preferred_element_type=F32)
    result = result.reshape(2, 32, 2, 64)
    result = jnp.stack([result[0, :, 0], result[1, :, 1]])
    return result.reshape(2, 1, 2048)


def solution(mesh):
    fine = Mesh(mesh.devices.reshape(2, 4, 4, 2, 2), ALL)
    kt, ks = ("xh", "z"), ("y", "xl", "core")
    in_specs = (
        P(kt, None, ks),
        P(kt, None, ks),
        P(ks, None, kt),
        P(ks, None, kt),
        P(ks, kt, None),
        P(None, kt + ks, None),
        P(),
    )
    return jax.shard_map(local, mesh=fine, in_specs=in_specs, out_specs=P(kt, ks, None), check_vma=False)
```

time: 168 us -> 107 us (0.64)
  starting transfers between devices: 90.1 us -> 21.8 us
  blocking collectives: 0 us -> 40.9 us
  waiting for transfers between devices: 31.1 us -> 9.25 us
  other arithmetic: 12.1 us -> 1.59 us
    ppermute x55 -> x4, starting transfers between devices: 71.2 us -> 5.43 us  [swap(): return lax.ppermute(x, axes, [(i, i ^ mask) for i in range(size)])]
    all_to_all x0 -> x1, blocking collectives: none -> 40.9 us  [all_to_all(): return lax.all_to_all(x, axes, split_axis=0, concat_axis=0, tiled=True)]
    ppermute x55 -> x4, waiting for transfers between devices: 21.1 us -> 0.39 us  [swap(): return lax.ppermute(x, axes, [(i, i ^ mask) for i in range(size)])]
    concatenate x3 -> x1, other arithmetic: 9.88 us -> 0.01 us  [local(): block = jnp.concatenate([trial, cs, ct], axis=0)]
    all_to_all x1 -> x2, starting transfers between devices: 18.9 us -> 16.4 us  [all_to_all(): return lax.all_to_all(x, axes, split_axis=0, concat_axis=0, tiled=True)]
    slice x6 -> x2, local copies, waits for them, and re-layouts: 1.94 us -> 0.04 us  [the longest x1 0.03 us: local(): ct_other = swap(every[:, CT:TV], 'core', 2, 1)]
    transpose x0 -> x3, local copies, waits for them, and re-layouts: none -> 1.74 us  [the longest x1 0.94 us: local(): cond_source.reshape(2, 2, 64, 64).transpose(0, 3, 1, 2).reshape(128, 128)]
    all_to_all x1 -> x2, waiting for transfers between devices: 10 us -> 8.86 us  [all_to_all(): return lax.all_to_all(x, axes, split_axis=0, concat_axis=0, tiled=True)]
  transfers between devices with their start and end apart: 56 -> 6, of which waited for: 16 -> 3; matrix products, arithmetic and copies ran while one was open for 11% -> 6% of each run, Pallas kernels for 1% -> 21%
where the time goes in v2:
time: 107 us; the launch traced here: 106 us
  blocking collectives  40.9 us (38%)
  Pallas kernels  22.4 us (21%)
  starting transfers between devices  21.8 us (20%)
  local copies, waits for them, and re-layouts  9.52 us (9%)
  waiting for transfers between devices  9.25 us (9%)
  other arithmetic  1.59 us (1%)
    all_to_all x1, blocking collectives, all_to_all(): return lax.all_to_all(x, axes, split_axis=0, concat_axis=0, tiled=True)  40.9 us
    all_to_all x2, starting transfers between devices, all_to_all(): return lax.all_to_all(x, axes, split_axis=0, concat_axis=0, tiled=True)  16.4 us
    pallas_call x1, Pallas kernels, local(): pl.pallas_call(screen_kernel, out_shape=jax.ShapeDtypeStruct((16, 128, 51...  14.7 us
    all_to_all x2, waiting for transfers between devices, all_to_all(): return lax.all_to_all(x, axes, split_axis=0, concat_axis=0, tiled=True)  8.86 us
    ppermute x4, starting transfers between devices, swap(): return lax.ppermute(x, axes, [(i, i ^ mask) for i in range(size)])  5.43 us
    pallas_call x1, Pallas kernels, local(): pl.pallas_call(repeat_kernel, out_shape=jax.ShapeDtypeStruct((512, 16, 51...  5.08 us
    unnamed x9, local copies, waits for them, and re-layouts  4.09 us
  transfers between devices with their start and end apart: 6, of which 3 were waited for; matrix products, arithmetic and copies ran while one was open for 6% of the time, Pallas kernels for 21%

profile of v2, /device:TPU:1, one launch (start us, length us, event | category | flops | bytes accessed | tf_op | source)
XLA Modules:
  0.0 105.8 jit_solution(9300476430453084605)
XLA Ops:
  0.0 1.4 %collective-permute-start = (bf16[512,4,512]{2,1,0:T(4,128)(2,1)}, bf16[512,4,512]{2,1,0:T(4,128)(2,1)}, u32[]{:S(2)}, u32[]{:S(2)}) collective-permute-start(bf16[512,4,512]{2,1,0:T(4,128)(2,1)} %own_ref.1), channel_id=1, source_target_pairs={{0,1},{1,0},{2,3},{3,2},{4,5},{5,4},{6,7},{7,6},{8,9},{9,8},{10,11... | collective-permute-start | bytes 6291464 | tf_op jit(solution)/shard_map/ppermute | solution.py:20
  1.4 0.9 reshape.49
  2.4 0.1 reshape.50
  2.5 0.9 copy.15
  3.4 0.1 reshape.52
  3.5 0.7 copy.16
  4.3 0.9 broadcast_in_dim.2
  5.3 7.6 %all-to-all-start = ((bf16[8,288,128]{2,1,0:T(8,128)(2,1)}), bf16[8,288,128]{2,1,0:T(8,128)(2,1)S(1)}, u32[]{:S(2)}, u32[]{:S(2)}) async-start(bf16[8,288,128]{2,1,0:T(8,128)(2,1)} %broadcast_in_dim.2), calls=%async_computation | async-start | bytes 1179648 | tf_op jit(solution)/shard_map/all_to_all | solution.py:140
  12.9 0.9 copy.13
  13.7 0.8 reshape.54.tv_ref
  14.6 5.1 %rows.1.w_hbm = bf16[512,16,512]{2,1,0:T(8,128)(2,1)S(1)} custom-call(bf16[512,4,512]{2,1,0:T(4,128)(2,1)S(1)} %copy-done.2, bf16[512,4,512]{2,1,0:T(4,128)(2,1)} %collective-permute-done.other_ref), custom_call_target="tpu_custom_call" | custom-call | tf_op jit(solution)/shard_map/rows/pallas_call | solution.py:149
  19.7 3.2 %copy-done = bf16[512,16,512]{2,1,0:T(8,128)(2,1)} copy-done((bf16[512,16,512]{2,1,0:T(8,128)(2,1)}, bf16[512,16,512]{2,1,0:T(8,128)(2,1)S(1)}, u32[]{:S(2)}) %copy-start) | copy-done | bytes 8388632
  22.9 0.3 all-to-all-done.first_ref
  23.2 0.6 pairs.1
  23.9 40.9 %all_to_all.15.all_ref = bf16[8,1552,128]{2,1,0:T(8,128)(2,1)S(1)} all-to-all(bf16[8,1552,128]{2,1,0:T(8,128)(2,1)S(1)} %pairs.1), channel_id=1, replica_groups=mesh['xh'=2,'z'=4,'y'=4,'xl'=2,'core'=2] {'y','xl'}, dimensions={0} | all-to-all | bytes 6356992 | tf_op jit(solution)/shard_map/all_to_all | solution.py:140
  64.8 3.4 %collective-permute-start.2 = (bf16[8,256,128]{2,1,0:T(8,128)(2,1)S(1)}, bf16[8,256,128]{2,1,0:T(8,128)(2,1)S(1)}, u32[]{:S(2)}, u32[]{:S(2)}) collective-permute-start(bf16[8,256,128]{2,1,0:T(8,128)(2,1)S(1)} %slice.17), channel_id=1, source_target_pairs={{0,1},{1,0},{2,3},{3,2},{4,5},{5,4},{6,7},{7,6},{8,9},{9,8},{10,11... | collective-permute-start | bytes 1572872 | tf_op jit(solution)/shard_map/ppermute | solution.py:20
  68.2 0.1 collective-permute-start.1
  68.3 14.7 %screen.1.y_ref = bf16[16,128,512]{2,1,0:T(8,128)(2,1)S(1)} custom-call(s32[1]{0:T(128)} %bitcast.11.core_ref, s32[16,64]{1,0:T(8,128)S(1)} %copy-done.3, bf16[512,16,512]{2,1,0:T(8,128)(2,1)S(1)} %copy-done.1, bf16[8,1552,128]{2,1,0:T(8,128)(2,1)S(1)} %all_to_all.15.all_ref), custom_call_target="tpu_custom_call" | custom-call | tf_op jit(solution)/shard_map/screen/pallas_call | solution.py:172
  83.1 2.0 %project.1 = (bf16[8,8,8,128]{3,2,1,0:T(8,128)(2,1)S(1)}, bf16[8,8,8,128]{3,2,1,0:T(8,128)(2,1)S(1)}) custom-call(s32[1]{0:T(128)} %bitcast.11.core_ref, bf16[16,128,512]{2,1,0:T(8,128)(2,1)S(1)} %screen.1.y_ref, bf16[8,1552,128]{2,1,0:T(8,128)(2,1)S(1)} %all_to_all.15.all_ref, bf16[8,256,128]{2,1,0:T(8,128)(2,1)S(1)} %collective-permute-done.2.other_ref), custom_call_target="tpu_custom_call" | custom-call | tf_op jit(solution)/shard_map/project/pallas_call | solution.py:187
  85.0 0.5 collective-permute-start.3
  85.5 0.1 stack_reshape.8
  85.6 0.1 copy.17
  85.8 0.1 stack_reshape.9
  85.9 0.1 copy.18
  86.1 0.4 collective-permute-done.3
  86.5 0.7 add_convert_fusion
  87.2 8.8 %all-to-all-start.2 = ((bf16[64,8,128]{2,1,0:T(8,128)(2,1)}), bf16[64,8,128]{2,1,0:T(8,128)(2,1)S(1)}, u32[]{:S(2)}, u32[]{:S(2)}) async-start(bf16[64,8,128]{2,1,0:T(8,128)(2,1)} %bitcast.12), calls=%async_computation.2 | async-start | bytes 262144 | tf_op jit(solution)/shard_map/all_to_all | solution.py:140
  96.0 0.1 reverse_select_fusion
  96.2 8.5 %all-to-all-done.2 = bf16[64,8,128]{2,1,0:T(8,128)(2,1)S(1)} async-done(((bf16[64,8,128]{2,1,0:T(8,128)(2,1)}), bf16[64,8,128]{2,1,0:T(8,128)(2,1)S(1)}, u32[]{:S(2)}, u32[]{:S(2)}) %all-to-all-start.2) | async-done | bytes 131104 | tf_op jit(solution)/shard_map/all_to_all | solution.py:140
  104.7 0.1 copy.21
  104.8 0.2 fusion.1
  105.2 0.6 pad_maximum_fusion.1
  (20 shorter events, 0.5 us)
Async XLA Ops:
  0.0 14.6 %copy-start.2 = (bf16[512,4,512]{2,1,0:T(4,128)(2,1)S(1)}, bf16[512,4,512]{2,1,0:T(4,128)(2,1)}, u32[]{:S(2)}) copy-start(bf16[512,4,512]{2,1,0:T(4,128)(2,1)} %own_ref.1) | copy-start | bytes 6291460
  0.0 14.6 %collective-permute-start = (bf16[512,4,512]{2,1,0:T(4,128)(2,1)}, bf16[512,4,512]{2,1,0:T(4,128)(2,1)}, u32[]{:S(2)}, u32[]{:S(2)}) collective-permute-start(bf16[512,4,512]{2,1,0:T(4,128)(2,1)} %own_ref.1), channel_id=1, source_target_pairs={{0,1},{1,0},{2,3},{3,2},{4,5},{5,4},{6,7},{7,6},{8,9},{9,8},{10,11... | collective-permute-start | bytes 6291464 | tf_op jit(solution)/shard_map/ppermute | solution.py:20
  5.3 18.0 %all-to-all-start = ((bf16[8,288,128]{2,1,0:T(8,128)(2,1)}), bf16[8,288,128]{2,1,0:T(8,128)(2,1)S(1)}, u32[]{:S(2)}, u32[]{:S(2)}) async-start(bf16[8,288,128]{2,1,0:T(8,128)(2,1)} %broadcast_in_dim.2), calls=%async_computation | async-start | bytes 1179648 | tf_op jit(solution)/shard_map/all_to_all | solution.py:140
  19.7 3.2 %copy-start = (bf16[512,16,512]{2,1,0:T(8,128)(2,1)}, bf16[512,16,512]{2,1,0:T(8,128)(2,1)S(1)}, u32[]{:S(2)}) copy-start(bf16[512,16,512]{2,1,0:T(8,128)(2,1)S(1)} %rows.1.w_hbm) | copy-start | bytes 25165828
  23.2 45.1 %copy-start.1 = (bf16[512,16,512]{2,1,0:T(8,128)(2,1)S(1)}, bf16[512,16,512]{2,1,0:T(8,128)(2,1)}, u32[]{:S(2)}) copy-start(bf16[512,16,512]{2,1,0:T(8,128)(2,1)} %copy-done) | copy-start | bytes 25165828
  23.9 44.4 %copy-start.3 = (s32[16,64]{1,0:T(8,128)S(1)}, s32[16,64]{1,0:T(8,128)}, u32[]{:S(2)}) copy-start(s32[16,64]{1,0:T(8,128)} %pm_ref.1) | copy-start | bytes 12292
  64.8 18.3 %collective-permute-start.2 = (bf16[8,256,128]{2,1,0:T(8,128)(2,1)S(1)}, bf16[8,256,128]{2,1,0:T(8,128)(2,1)S(1)}, u32[]{:S(2)}, u32[]{:S(2)}) collective-permute-start(bf16[8,256,128]{2,1,0:T(8,128)(2,1)S(1)} %slice.17), channel_id=1, source_target_pairs={{0,1},{1,0},{2,3},{3,2},{4,5},{5,4},{6,7},{7,6},{8,9},{9,8},{10,11... | collective-permute-start | bytes 1572872 | tf_op jit(solution)/shard_map/ppermute | solution.py:20
  68.2 17.6 %collective-permute-start.1 = (bf16[8,16,128]{2,1,0:T(8,128)(2,1)S(1)}, bf16[8,16,128]{2,1,0:T(8,128)(2,1)S(1)}, u32[]{:S(2)}, u32[]{:S(2)}) collective-permute-start(bf16[8,16,128]{2,1,0:T(8,128)(2,1)S(1)} %slice.16), channel_id=1, source_target_pairs={{0,1},{1,0},{2,3},{3,2},{4,5},{5,4},{6,7},{7,6},{8,9},{9,8},{10,11... | collective-permute-start | bytes 98312 | tf_op jit(solution)/shard_map/ppermute | solution.py:20
  85.0 1.5 %collective-permute-start.3 = (bf16[8,8,8,128]{3,2,1,0:T(8,128)(2,1)S(1)}, bf16[8,8,8,128]{3,2,1,0:T(8,128)(2,1)S(1)}, u32[]{:S(2)}, u32[]{:S(2)}) collective-permute-start(bf16[8,8,8,128]{3,2,1,0:T(8,128)(2,1)S(1)} %get-tuple-element.12), channel_id=1, source_target_pairs={{0,1},{1,0},{2,3},{3,2},{4,5},{5,4},{6,7},{7,6},{8,9},{9,8},{10,11... | collective-permute-start | bytes 393224 | tf_op jit(solution)/shard_map/ppermute | solution.py:20
  87.2 17.5 %all-to-all-start.2 = ((bf16[64,8,128]{2,1,0:T(8,128)(2,1)}), bf16[64,8,128]{2,1,0:T(8,128)(2,1)S(1)}, u32[]{:S(2)}, u32[]{:S(2)}) async-start(bf16[64,8,128]{2,1,0:T(8,128)(2,1)} %bitcast.12), calls=%async_computation.2 | async-start | bytes 262144 | tf_op jit(solution)/shard_map/all_to_all | solution.py:140

commit v3 on v2

v3 whole, which is shorter than its diff:
```python
import functools

import jax
import jax.numpy as jnp
from jax import lax
from jax.experimental import pallas as pl
from jax.experimental.pallas import tpu as pltpu
from jax.sharding import Mesh
from jax.sharding import PartitionSpec as P

ALL = ("xh", "z", "y", "xl", "core")
YX = ("y", "xl")
KT = ("xh", "z")
X = ("xh", "xl")
CHIPS = ("xh", "z", "y", "xl")
BF = jnp.bfloat16
F32 = jnp.float32
VMEM_LIMIT = 8 * 1024 * 1024
NEAR = 48
TV = 256 + 16 * NEAR


def swap(x, axes, size, mask):
    return lax.ppermute(x, axes, [(i, i ^ mask) for i in range(size)])


def flip_if(bit, x, axis):
    return jnp.where(bit == 1, jnp.flip(x, axis), x)


def doubled(x, axes, size, mask):
    return jnp.concatenate([x, swap(x, axes, size, mask)], axis=0)


def cost(flops, bytes_accessed):
    return pl.CostEstimate(flops=flops, bytes_accessed=bytes_accessed, transcendentals=0)


def pair_kernel(svt_ref, near_ref, tv_ref, out_ref):
    lane = lax.broadcasted_iota(jnp.int32, (64, 256), 1)
    even_s = (lane & 64) == 0
    for k in range(8):
        for sp in range(2):
            at = sp * 32
            block = jnp.concatenate([near_ref[k, at : at + 32], near_ref[k, 64 + at : 96 + at]], axis=1)
            even = jnp.dot(svt_ref[2 * sp], block, preferred_element_type=F32)
            odd = jnp.dot(svt_ref[2 * sp + 1], block, preferred_element_type=F32)
            both = jnp.where(even_s, even, odd)
            for peer in range(8):
                rows = both[peer * 8 : peer * 8 + 8]
                piece = jnp.concatenate([rows[:, :128], rows[:, 128:]], axis=0)
                at = sp * 128 + k * 16
                out_ref[peer, at : at + 16, :] = piece.astype(BF)
        for peer in range(8):
            at = 256 + k * 2 * NEAR
            out_ref[peer, at : at + 2 * NEAR, :] = near_ref[k, 128 : 128 + 2 * NEAR]
    for peer in range(8):
        out_ref[peer, TV : TV + 16, :] = tv_ref[...]


def far_index(kt_mask, yx_mask):
    y_mask, xh_mask = yx_mask >> 1, kt_mask >> 2
    place = (((yx_mask & 1) ^ xh_mask) << 2) | (y_mask ^ (y_mask >> 1))
    return kt_mask ^ ((kt_mask >> 1) & 1), place


def screen_kernel(me_ref, pm_ref, own_ref, other_ref, every_ref, far_ref, ct_other_ref, out_ref, w_ref, xs, acc, ct):
    here, yx_here, core = me_ref[0], me_ref[1], me_ref[2]

    def eight_mats(step, carry):
        own, other = own_ref[pl.ds(step * 8, 8)], other_ref[pl.ds(step * 8, 8)]
        for half in range(2):
            parts = []
            for qb in (2 * half, 2 * half + 1):
                lanes = slice(qb * 128, qb * 128 + 128)
                parts += [own[:, :, lanes], other[:, :, lanes]]
            w_ref[pl.ds(step * 8, 8), half] = jnp.concatenate(parts, axis=1)
        return carry

    lax.fori_loop(0, 64, eight_mats, 0)
    lane = lax.broadcasted_iota(jnp.int32, (128, 128), 1)
    first = lane < 64

    def one_chip(yx, carry):
        for sp in range(2):
            a = every_ref[yx, sp * 128 : sp * 128 + 128]
            none = jnp.zeros_like(a)
            lhs = jnp.concatenate([jnp.where(first, a, none), jnp.where(first, none, a)], axis=0)
            factors = []
            for kt in range(8):
                at = 256 + (kt * 2 + sp) * NEAR
                j, i = far_index(kt ^ here, yx ^ yx_here)
                rest = far_ref[j, i, sp * (64 - NEAR) : (sp + 1) * (64 - NEAR)]
                factors += [every_ref[yx, at : at + NEAR], rest]
            rhs = jnp.concatenate(factors, axis=0)
            x = lax.dot_general(lhs, rhs, (((1,), (1,)), ((), ())), preferred_element_type=F32)
            x = x.reshape(2, 16, 8, 512)
            for half in range(2):
                at = half * 256
                tile = jnp.concatenate([x[..., at : at + 128], x[..., at + 128 : at + 256]], axis=2)
                xs[pl.ds(yx * 4 + sp * 2, 2), half] = tile.astype(BF)
        return carry

    lax.fori_loop(0, 8, one_chip, 0)
    for chunk in range(4):

        def one_target(t, carry, chunk=chunk):
            mats = []
            for yx in (2 * chunk, 2 * chunk + 1):
                source = (yx * 2 + core) * 4
                mats += [pm_ref[t, source + j] for j in range(4)]
            for half in range(2):
                w = [w_ref[m, half] for m in mats]
                for n in range(16):
                    terms = [w[j] * xs[chunk * 8 + j, half, n] for j in range(8)]
                    while len(terms) > 1:
                        terms = [terms[j] + terms[j + 1] for j in range(0, len(terms), 2)]
                    total = terms[0].astype(F32)
                    rows = slice(n * 8, n * 8 + 8)
                    for qb in range(2):
                        lanes = slice(half * 256 + qb * 128, half * 256 + qb * 128 + 128)
                        part = total[qb * 8 : qb * 8 + 8]
                        if chunk > 0:
                            part = part + acc[t, rows, lanes]
                        acc[t, rows, lanes] = part
            return carry

        lax.fori_loop(0, 16, one_target, 0)

    def project(kt, carry):
        for yx in range(8):
            j, i = far_index(kt ^ here, yx ^ yx_here)
            ct[pl.ds(pl.multiple_of((yx * 2 + core) * 32, 32), 32), :] = far_ref[j, i, 128 - 2 * NEAR :]
            ct[pl.ds(pl.multiple_of((yx * 2 + 1 - core) * 32, 32), 32), :] = ct_other_ref[j, i]
        c = ct[...]
        z0 = jnp.dot(acc[2 * kt].astype(BF), c, preferred_element_type=F32)
        z1 = jnp.dot(acc[2 * kt + 1].astype(BF), c, preferred_element_type=F32)
        out_ref[kt] = jnp.where(first, z0, z1).reshape(16, 8, 128).astype(BF)
        return carry

    lax.fori_loop(0, 8, project, 0)


def local(val_target, cond_target, val_source, cond_source, trial_vectors, screened, pair_momentum):
    xh, z, y, xl, core = (lax.axis_index(a) for a in ALL)
    me = jnp.stack([xh * 4 + z, y * 2 + xl, core]).astype(jnp.int32)
    vmem = pl.BlockSpec(memory_space=pltpu.VMEM)
    smem = pl.BlockSpec(memory_space=pltpu.SMEM)
    params = pltpu.CompilerParams(vmem_limit_bytes=VMEM_LIMIT)

    def all_to_all(x, axes):
        return lax.all_to_all(x, axes, split_axis=0, concat_axis=0, tiled=True)

    other = swap(screened, "core", 2, 1)

    trial = trial_vectors.reshape(2, 2, 2, 32, 64).transpose(2, 0, 3, 1, 4).reshape(128, 128)
    cs = cond_source.reshape(2, 2, 64, 64).transpose(0, 3, 1, 2).reshape(2, 64, 128)
    sent = jnp.concatenate([trial, cs[:, :NEAR].reshape(2 * NEAR, 128)], axis=0)
    sent = jnp.broadcast_to(sent[None], (8, 128 + 2 * NEAR, 128))
    near = all_to_all(sent, KT)

    sv = flip_if(core, val_source.reshape(4, 32, 8, 2, 4), 3)
    svt = sv.reshape(4, 32, 64).transpose(0, 2, 1)
    ct = cond_target.transpose(2, 0, 1).reshape(32, 128)
    block = jnp.concatenate([cs[:, NEAR:].reshape(128 - 2 * NEAR, 128), ct], axis=0)[None]
    block = doubled(block, "y", 4, 1)
    block, svt = lax.optimization_barrier((block, svt))
    block = doubled(block, "y", 4, 3)
    block = doubled(block, X, 4, 1)[None]
    near, block = lax.optimization_barrier((near, block))

    pieces = pl.pallas_call(
        pair_kernel,
        out_shape=jax.ShapeDtypeStruct((8, TV + 16, 128), BF),
        in_specs=[vmem] * 3,
        out_specs=vmem,
        compiler_params=params,
        name="pairs",
    )(svt, near, val_target.reshape(16, 128))
    every = all_to_all(pieces, YX)

    block = doubled(block, "z", 4, 1)
    block = doubled(block, "z", 4, 3)
    far = doubled(block, X, 4, 3)
    ct_other = swap(far[:, :, 128 - 2 * NEAR :], "core", 2, 1)

    zs = pl.pallas_call(
        screen_kernel,
        out_shape=jax.ShapeDtypeStruct((8, 16, 8, 128), BF),
        in_specs=[smem, smem] + [vmem] * 5,
        out_specs=vmem,
        scratch_shapes=[
            pltpu.VMEM((512, 2, 16, 128), BF),
            pltpu.VMEM((32, 2, 16, 16, 128), BF),
            pltpu.VMEM((16, 128, 512), F32),
            pltpu.VMEM((512, 128), BF),
        ],
        compiler_params=pltpu.CompilerParams(vmem_limit_bytes=24 * 1024 * 1024),
        cost_estimate=cost(8_000_000_000, 16_000_000),
        name="screen",
    )(me, pair_momentum, screened, other, every, far, ct_other)

    tv = every[:, TV:]
    tv_other = swap(tv, "core", 2, 1).reshape(8, 2, 32, 32)
    tv = tv.reshape(8, 2, 32, 32)
    tv = jnp.where(core == 0, jnp.stack([tv, tv_other], axis=1), jnp.stack([tv_other, tv], axis=1))
    tv = tv.transpose(2, 3, 0, 1, 4).reshape(2, 32, 64, 2, 4)
    tv = jnp.stack([tv, jnp.flip(tv, 3)], axis=3).reshape(64, 1024)

    arrived = all_to_all(zs.reshape(128, 8, 128), ALL)
    result = jnp.dot(tv, arrived.reshape(1024, 128), preferred_element_type=F32)
    result = result.reshape(2, 32, 2, 64)
    result = jnp.stack([result[0, :, 0], result[1, :, 1]])
    return result.reshape(2, 1, 2048)


def solution(mesh):
    fine = Mesh(mesh.devices.reshape(2, 4, 4, 2, 2), ALL)
    kt, ks = ("xh", "z"), ("y", "xl", "core")
    in_specs = (
        P(kt, None, ks),
        P(kt, None, ks),
        P(ks, None, kt),
        P(ks, None, kt),
        P(ks, kt, None),
        P(None, kt + ks, None),
        P(),
    )
    return jax.shard_map(local, mesh=fine, in_specs=in_specs, out_specs=P(kt, ks, None), check_vma=False)
```

time: 107 us -> 99.6 us (0.931)
  blocking collectives: 40.9 us -> 0 us
  waiting for transfers between devices: 9.25 us -> 30.1 us
  starting transfers between devices: 21.8 us -> 38.8 us
  local copies, waits for them, and re-layouts: 9.52 us -> 6.87 us
    all_to_all x1 -> x0, blocking collectives: 40.9 us -> none  [all_to_all(): return lax.all_to_all(x, axes, split_axis=0, concat_axis=0, tiled=True)]
    ppermute x4 -> x9, waiting for transfers between devices: 0.39 us -> 19.7 us  [swap(): return lax.ppermute(x, axes, [(i, i ^ mask) for i in range(size)])]
    ppermute x4 -> x9, starting transfers between devices: 5.43 us -> 18.4 us  [swap(): return lax.ppermute(x, axes, [(i, i ^ mask) for i in range(size)])]
    all_to_all x2 -> x3, starting transfers between devices: 16.4 us -> 20.4 us  [all_to_all(): return lax.all_to_all(x, axes, split_axis=0, concat_axis=0, tiled=True)]
    unnamed x9 -> x12, local copies, waits for them, and re-layouts: 4.09 us -> 1.17 us
    slice x1 -> x2, local copies, waits for them, and re-layouts: 0.03 us -> 1.77 us  [the longest x1 0.93 us: local(): cs[:, NEAR:].reshape(128 - 2 * NEAR, 128)]
    all_to_all x2 -> x3, waiting for transfers between devices: 8.86 us -> 10.4 us  [all_to_all(): return lax.all_to_all(x, axes, split_axis=0, concat_axis=0, tiled=True)]
    pallas_call x4 -> x2, Pallas kernels: 22.4 us -> 21.4 us  [the longest x1 19.5 us: local(): pl.pallas_call(screen_kernel, out_shape=jax.ShapeDtypeStruct((8, 16, 8, 1...]
  transfers between devices with their start and end apart: 6 -> 12, of which waited for: 3 -> 8; matrix products, arithmetic and copies ran while one was open for 6% -> 6% of each run, Pallas kernels for 21% -> 22%
where the time goes in v3:
time: 99.6 us; the launch traced here: 99 us
  starting transfers between devices  38.8 us (39%)
  waiting for transfers between devices  30.1 us (30%)
  Pallas kernels  21.4 us (21%)
  local copies, waits for them, and re-layouts  6.87 us (7%)
  other arithmetic  1.39 us (1%)
    all_to_all x3, starting transfers between devices, all_to_all(): return lax.all_to_all(x, axes, split_axis=0, concat_axis=0, tiled=True)  20.4 us
    ppermute x9, waiting for transfers between devices, swap(): return lax.ppermute(x, axes, [(i, i ^ mask) for i in range(size)])  19.7 us
    pallas_call x1, Pallas kernels, local(): pl.pallas_call(screen_kernel, out_shape=jax.ShapeDtypeStruct((8, 16, 8, 1...  19.5 us
    ppermute x9, starting transfers between devices, swap(): return lax.ppermute(x, axes, [(i, i ^ mask) for i in range(size)])  18.4 us
    all_to_all x3, waiting for transfers between devices, all_to_all(): return lax.all_to_all(x, axes, split_axis=0, concat_axis=0, tiled=True)  10.4 us
  transfers between devices with their start and end apart: 12, of which 8 were waited for; matrix products, arithmetic and copies ran while one was open for 6% of the time, Pallas kernels for 22%

profile of v3, /device:TPU:1, one launch (start us, length us, event | category | flops | bytes accessed | tf_op | source)
XLA Modules:
  0.0 99.0 jit_solution(7124838529456645652)
XLA Ops:
  0.0 0.9 slice.24
  1.0 0.8 copy.15
  1.9 2.2 %collective-permute-start = (bf16[1,64,128]{2,1,0:T(8,128)(2,1)S(1)}, bf16[1,64,128]{2,1,0:T(8,128)(2,1)S(1)}, u32[]{:S(2)}, u32[]{:S(2)}) collective-permute-start(bf16[1,64,128]{2,1,0:T(8,128)(2,1)S(1)} %maximum_bitcast_fusion.1), channel_id=1, source_target_pairs={{0,4},{4,0},{8,12},{12,8},{1,5},{5,1},{9,13},{13,9},{2,6},{6,2},{1... | collective-permute-start | bytes 49160 | tf_op jit(solution)/shard_map/ppermute | solution.py:24
  4.0 0.9 copy.30
  5.0 0.9 reshape.56
  6.0 0.8 broadcast_in_dim.13
  6.9 7.5 %all-to-all-start = ((bf16[8,224,128]{2,1,0:T(8,128)(2,1)}), bf16[8,224,128]{2,1,0:T(8,128)(2,1)S(1)}, u32[]{:S(2)}, u32[]{:S(2)}) async-start(bf16[8,224,128]{2,1,0:T(8,128)(2,1)} %broadcast_in_dim.13), calls=%async_computation | async-start | bytes 917504 | tf_op jit(solution)/shard_map/all_to_all | solution.py:152
  14.5 2.0 %collective-permute-start.1 = (bf16[2,64,128]{2,1,0:T(8,128)(2,1)S(1)}, bf16[2,64,128]{2,1,0:T(8,128)(2,1)S(1)}, u32[]{:S(2)}, u32[]{:S(2)}) collective-permute-start(bf16[2,64,128]{2,1,0:T(8,128)(2,1)S(1)} %pad_maximum_fusion.5), channel_id=1, source_target_pairs={{0,12},{4,8},{8,4},{12,0},{1,13},{5,9},{9,5},{13,1},{2,14},{6,10},... | collective-permute-start | bytes 98312 | tf_op jit(solution)/shard_map/ppermute | solution.py:24
  16.5 1.5 %collective-permute-start.4 = (bf16[512,4,512]{2,1,0:T(4,128)(2,1)}, bf16[512,4,512]{2,1,0:T(4,128)(2,1)}, u32[]{:S(2)}, u32[]{:S(2)}) collective-permute-start(bf16[512,4,512]{2,1,0:T(4,128)(2,1)} %own_ref.1), channel_id=1, source_target_pairs={{0,1},{1,0},{2,3},{3,2},{4,5},{5,4},{6,7},{7,6},{8,9},{9,8},{10,11... | collective-permute-start | bytes 6291464 | tf_op jit(solution)/shard_map/ppermute | solution.py:24
  18.0 0.6 collective-permute-done.1
  18.6 0.4 collective-permute-start.2
  19.1 3.0 %collective-permute-done.2 = bf16[4,64,128]{2,1,0:T(8,128)(2,1)S(1)} collective-permute-done((bf16[4,64,128]{2,1,0:T(8,128)(2,1)S(1)}, bf16[4,64,128]{2,1,0:T(8,128)(2,1)S(1)}, u32[]{:S(2)}, u32[]{:S(2)}) %collective-permute-start.2) | collective-permute-done | bytes 65568 | tf_op jit(solution)/shard_map/ppermute | solution.py:24
  22.1 0.6 all-to-all-done.near_ref
  22.7 1.9 %pairs.1 = bf16[8,1040,128]{2,1,0:T(8,128)(2,1)} custom-call(bf16[4,64,32]{2,1,0:T(8,128)(2,1)S(1)} %bitcast.50, bf16[8,224,128]{2,1,0:T(8,128)(2,1)S(1)} %all-to-all-done.near_ref, bf16[16,128]{1,0:T(8,128)(2,1)S(1)} %reshape.59.tv_ref), custom_call_target="tpu_custom_call" | custom-call | tf_op jit(solution)/shard_map/pairs/pallas_call | solution.py:172
  24.6 3.9 %all-to-all-start.1 = ((bf16[8,1040,128]{2,1,0:T(8,128)(2,1)}), bf16[8,1040,128]{2,1,0:T(8,128)(2,1)S(1)}, u32[]{:S(2)}, u32[]{:S(2)}) async-start(bf16[8,1040,128]{2,1,0:T(8,128)(2,1)} %pairs.1), calls=%async_computation.1 | async-start | bytes 4259840 | tf_op jit(solution)/shard_map/all_to_all | solution.py:152
  28.6 0.7 collective-permute-start.5
  29.2 3.2 %collective-permute-done.5 = bf16[1,8,64,128]{3,2,1,0:T(8,128)(2,1)S(1)} collective-permute-done((bf16[1,8,64,128]{3,2,1,0:T(8,128)(2,1)S(1)}, bf16[1,8,64,128]{3,2,1,0:T(8,128)(2,1)S(1)}, u32[]{:S(2)}, u32[]{:S(2)}) %collective-permute-start.5) | collective-permute-done | bytes 131104 | tf_op jit(solution)/shard_map/ppermute | solution.py:24
  32.4 2.0 %collective-permute-start.6 = (bf16[2,8,64,128]{3,2,1,0:T(8,128)(2,1)S(1)}, bf16[2,8,64,128]{3,2,1,0:T(8,128)(2,1)S(1)}, u32[]{:S(2)}, u32[]{:S(2)}) collective-permute-start(bf16[2,8,64,128]{3,2,1,0:T(8,128)(2,1)S(1)} %pad_maximum_fusion.2), channel_id=1, source_target_pairs={{0,48},{16,32},{32,16},{48,0},{1,49},{17,33},{33,17},{49,1},{2,50}... | collective-permute-start | bytes 786440 | tf_op jit(solution)/shard_map/ppermute | solution.py:24
  34.4 4.8 %collective-permute-done.6 = bf16[2,8,64,128]{3,2,1,0:T(8,128)(2,1)S(1)} collective-permute-done((bf16[2,8,64,128]{3,2,1,0:T(8,128)(2,1)S(1)}, bf16[2,8,64,128]{3,2,1,0:T(8,128)(2,1)S(1)}, u32[]{:S(2)}, u32[]{:S(2)}) %collective-permute-start.6) | collective-permute-done | bytes 262176 | tf_op jit(solution)/shard_map/ppermute | solution.py:24
  39.3 2.9 %collective-permute-start.7 = (bf16[4,8,64,128]{3,2,1,0:T(8,128)(2,1)S(1)}, bf16[4,8,64,128]{3,2,1,0:T(8,128)(2,1)S(1)}, u32[]{:S(2)}, u32[]{:S(2)}) collective-permute-start(bf16[4,8,64,128]{3,2,1,0:T(8,128)(2,1)S(1)} %pad_maximum_fusion.1), channel_id=1, source_target_pairs={{0,66},{2,64},{64,2},{66,0},{1,67},{3,65},{65,3},{67,1},{4,70},{6,... | collective-permute-start | bytes 1572872 | tf_op jit(solution)/shard_map/ppermute | solution.py:24
  42.3 6.8 %collective-permute-done.7 = bf16[4,8,64,128]{3,2,1,0:T(8,128)(2,1)S(1)} collective-permute-done((bf16[4,8,64,128]{3,2,1,0:T(8,128)(2,1)S(1)}, bf16[4,8,64,128]{3,2,1,0:T(8,128)(2,1)S(1)}, u32[]{:S(2)}, u32[]{:S(2)}) %collective-permute-start.7) | collective-permute-done | bytes 524320 | tf_op jit(solution)/shard_map/ppermute | solution.py:24
  49.1 0.8 slice.27
  50.0 6.4 %collective-permute-start.8 = (bf16[8,8,32,128]{3,2,1,0:T(8,128)(2,1)}, bf16[8,8,32,128]{3,2,1,0:T(8,128)(2,1)}, u32[]{:S(2)}, u32[]{:S(2)}) collective-permute-start(bf16[8,8,32,128]{3,2,1,0:T(8,128)(2,1)} %slice.27), channel_id=1, source_target_pairs={{0,1},{1,0},{2,3},{3,2},{4,5},{5,4},{6,7},{7,6},{8,9},{9,8},{10,11... | collective-permute-start | bytes 1572872 | tf_op jit(solution)/shard_map/ppermute | solution.py:24
  56.4 0.4 collective-permute-start.3
  56.8 1.4 %collective-permute-done.8.ct_other_ref = bf16[8,8,32,128]{3,2,1,0:T(8,128)(2,1)} collective-permute-done((bf16[8,8,32,128]{3,2,1,0:T(8,128)(2,1)}, bf16[8,8,32,128]{3,2,1,0:T(8,128)(2,1)}, u32[]{:S(2)}, u32[]{:S(2)}) %collective-permute-start.8) | collective-permute-done | bytes 524320 | tf_op jit(solution)/shard_map/ppermute | solution.py:24
  58.2 19.5 %screen.1 = bf16[8,16,8,128]{3,2,1,0:T(8,128)(2,1)} custom-call(s32[3]{0:T(128)S(1)} %pad_add_fusion.me_ref, s32[16,64]{1,0:T(8,128)S(1)} %copy-done, bf16[512,4,512]{2,1,0:T(4,128)(2,1)} %own_ref.1, bf16[512,4,512]{2,1,0:T(4,128)(2,1)} %collective-permute-done.4.other_ref, bf16[8,1040,128]{2,1,0:T(8,128)(2,1)S(1)} %all-to-all-done.1.every_ref, ...), custom_call_target="tpu_custom_call" | custom-call | flops 8000000000 | bytes 16000000 | tf_op jit(solution)/shard_map/screen/pallas_call | solution.py:187
  77.8 9.0 %all-to-all-start.2 = ((bf16[128,8,128]{2,1,0:T(8,128)(2,1)}), bf16[128,8,128]{2,1,0:T(8,128)(2,1)S(1)}, u32[]{:S(2)}, u32[]{:S(2)}) async-start(bf16[128,8,128]{2,1,0:T(8,128)(2,1)} %bitcast.23), calls=%async_computation.2 | async-start | bytes 524288 | tf_op jit(solution)/shard_map/all_to_all | solution.py:152
  87.4 0.4 pad_maximum_fusion
  87.9 0.2 copy.22
  88.1 9.8 %all-to-all-done.2 = bf16[128,8,128]{2,1,0:T(8,128)(2,1)S(1)} async-done(((bf16[128,8,128]{2,1,0:T(8,128)(2,1)}), bf16[128,8,128]{2,1,0:T(8,128)(2,1)S(1)}, u32[]{:S(2)}, u32[]{:S(2)}) %all-to-all-start.2) | async-done | bytes 262176 | tf_op jit(solution)/shard_map/all_to_all | solution.py:152
  98.0 0.3 fusion.1
  98.4 0.6 pad_maximum_fusion.6
  (40 shorter events, 1.9 us)
Async XLA Ops:
  0.0 14.4 %copy-start.1 = (bf16[4,32,64]{2,1,0:T(8,128)(2,1)S(1)}, bf16[4,32,64]{2,1,0:T(8,128)(2,1)}, u32[]{:S(2)}) copy-start(bf16[4,32,64]{2,1,0:T(8,128)(2,1)} %param.9) | copy-start | bytes 49156
  0.0 19.0 %copy-start.2 = (bf16[2,32,32]{2,1,0:T(8,128)(2,1)S(1)}, bf16[2,32,32]{2,1,0:T(8,128)(2,1)}, u32[]{:S(2)}) copy-start(bf16[2,32,32]{2,1,0:T(8,128)(2,1)} %param.7) | copy-start | bytes 12292
  1.9 12.7 %collective-permute-start = (bf16[1,64,128]{2,1,0:T(8,128)(2,1)S(1)}, bf16[1,64,128]{2,1,0:T(8,128)(2,1)S(1)}, u32[]{:S(2)}, u32[]{:S(2)}) collective-permute-start(bf16[1,64,128]{2,1,0:T(8,128)(2,1)S(1)} %maximum_bitcast_fusion.1), channel_id=1, source_target_pairs={{0,4},{4,0},{8,12},{12,8},{1,5},{5,1},{9,13},{13,9},{2,6},{6,2},{1... | collective-permute-start | bytes 49160 | tf_op jit(solution)/shard_map/ppermute | solution.py:24
  6.9 15.9 %all-to-all-start = ((bf16[8,224,128]{2,1,0:T(8,128)(2,1)}), bf16[8,224,128]{2,1,0:T(8,128)(2,1)S(1)}, u32[]{:S(2)}, u32[]{:S(2)}) async-start(bf16[8,224,128]{2,1,0:T(8,128)(2,1)} %broadcast_in_dim.13), calls=%async_computation | async-start | bytes 917504 | tf_op jit(solution)/shard_map/all_to_all | solution.py:152
  14.5 4.1 %collective-permute-start.1 = (bf16[2,64,128]{2,1,0:T(8,128)(2,1)S(1)}, bf16[2,64,128]{2,1,0:T(8,128)(2,1)S(1)}, u32[]{:S(2)}, u32[]{:S(2)}) collective-permute-start(bf16[2,64,128]{2,1,0:T(8,128)(2,1)S(1)} %pad_maximum_fusion.5), channel_id=1, source_target_pairs={{0,12},{4,8},{8,4},{12,0},{1,13},{5,9},{9,5},{13,1},{2,14},{6,10},... | collective-permute-start | bytes 98312 | tf_op jit(solution)/shard_map/ppermute | solution.py:24
  16.5 41.7 %collective-permute-start.4 = (bf16[512,4,512]{2,1,0:T(4,128)(2,1)}, bf16[512,4,512]{2,1,0:T(4,128)(2,1)}, u32[]{:S(2)}, u32[]{:S(2)}) collective-permute-start(bf16[512,4,512]{2,1,0:T(4,128)(2,1)} %own_ref.1), channel_id=1, source_target_pairs={{0,1},{1,0},{2,3},{3,2},{4,5},{5,4},{6,7},{7,6},{8,9},{9,8},{10,11... | collective-permute-start | bytes 6291464 | tf_op jit(solution)/shard_map/ppermute | solution.py:24
  18.6 3.5 %collective-permute-start.2 = (bf16[4,64,128]{2,1,0:T(8,128)(2,1)S(1)}, bf16[4,64,128]{2,1,0:T(8,128)(2,1)S(1)}, u32[]{:S(2)}, u32[]{:S(2)}) collective-permute-start(bf16[4,64,128]{2,1,0:T(8,128)(2,1)S(1)} %pad_maximum_fusion.3), channel_id=1, source_target_pairs={{0,2},{2,0},{64,66},{66,64},{1,3},{3,1},{65,67},{67,65},{4,6},{6,4... | collective-permute-start | bytes 196616 | tf_op jit(solution)/shard_map/ppermute | solution.py:24
  24.6 31.8 %all-to-all-start.1 = ((bf16[8,1040,128]{2,1,0:T(8,128)(2,1)}), bf16[8,1040,128]{2,1,0:T(8,128)(2,1)S(1)}, u32[]{:S(2)}, u32[]{:S(2)}) async-start(bf16[8,1040,128]{2,1,0:T(8,128)(2,1)} %pairs.1), calls=%async_computation.1 | async-start | bytes 4259840 | tf_op jit(solution)/shard_map/all_to_all | solution.py:152
  28.6 3.8 %collective-permute-start.5 = (bf16[1,8,64,128]{3,2,1,0:T(8,128)(2,1)S(1)}, bf16[1,8,64,128]{3,2,1,0:T(8,128)(2,1)S(1)}, u32[]{:S(2)}, u32[]{:S(2)}) collective-permute-start(bf16[1,8,64,128]{3,2,1,0:T(8,128)(2,1)S(1)} %maximum_bitcast_fusion), channel_id=1, source_target_pairs={{0,16},{16,0},{32,48},{48,32},{1,17},{17,1},{33,49},{49,33},{2,18}... | collective-permute-start | bytes 393224 | tf_op jit(solution)/shard_map/ppermute | solution.py:24
  32.4 25.8 %copy-start = (s32[16,64]{1,0:T(8,128)S(1)}, s32[16,64]{1,0:T(8,128)}, u32[]{:S(2)}) copy-start(s32[16,64]{1,0:T(8,128)} %pm_ref.1) | copy-start | bytes 12292
  32.4 6.8 %collective-permute-start.6 = (bf16[2,8,64,128]{3,2,1,0:T(8,128)(2,1)S(1)}, bf16[2,8,64,128]{3,2,1,0:T(8,128)(2,1)S(1)}, u32[]{:S(2)}, u32[]{:S(2)}) collective-permute-start(bf16[2,8,64,128]{3,2,1,0:T(8,128)(2,1)S(1)} %pad_maximum_fusion.2), channel_id=1, source_target_pairs={{0,48},{16,32},{32,16},{48,0},{1,49},{17,33},{33,17},{49,1},{2,50}... | collective-permute-start | bytes 786440 | tf_op jit(solution)/shard_map/ppermute | solution.py:24
  39.3 9.8 %collective-permute-start.7 = (bf16[4,8,64,128]{3,2,1,0:T(8,128)(2,1)S(1)}, bf16[4,8,64,128]{3,2,1,0:T(8,128)(2,1)S(1)}, u32[]{:S(2)}, u32[]{:S(2)}) collective-permute-start(bf16[4,8,64,128]{3,2,1,0:T(8,128)(2,1)S(1)} %pad_maximum_fusion.1), channel_id=1, source_target_pairs={{0,66},{2,64},{64,2},{66,0},{1,67},{3,65},{65,3},{67,1},{4,70},{6,... | collective-permute-start | bytes 1572872 | tf_op jit(solution)/shard_map/ppermute | solution.py:24
  50.0 8.2 %collective-permute-start.8 = (bf16[8,8,32,128]{3,2,1,0:T(8,128)(2,1)}, bf16[8,8,32,128]{3,2,1,0:T(8,128)(2,1)}, u32[]{:S(2)}, u32[]{:S(2)}) collective-permute-start(bf16[8,8,32,128]{3,2,1,0:T(8,128)(2,1)} %slice.27), channel_id=1, source_target_pairs={{0,1},{1,0},{2,3},{3,2},{4,5},{5,4},{6,7},{7,6},{8,9},{9,8},{10,11... | collective-permute-start | bytes 1572872 | tf_op jit(solution)/shard_map/ppermute | solution.py:24
  56.4 30.6 %collective-permute-start.3 = (bf16[8,16,128]{2,1,0:T(8,128)(2,1)S(1)}, bf16[8,16,128]{2,1,0:T(8,128)(2,1)S(1)}, u32[]{:S(2)}, u32[]{:S(2)}) collective-permute-start(bf16[8,16,128]{2,1,0:T(8,128)(2,1)S(1)} %slice.26), channel_id=1, source_target_pairs={{0,1},{1,0},{2,3},{3,2},{4,5},{5,4},{6,7},{7,6},{8,9},{9,8},{10,11... | collective-permute-start | bytes 98312 | tf_op jit(solution)/shard_map/ppermute | solution.py:24
  77.8 20.0 %all-to-all-start.2 = ((bf16[128,8,128]{2,1,0:T(8,128)(2,1)}), bf16[128,8,128]{2,1,0:T(8,128)(2,1)S(1)}, u32[]{:S(2)}, u32[]{:S(2)}) async-start(bf16[128,8,128]{2,1,0:T(8,128)(2,1)} %bitcast.23), calls=%async_computation.2 | async-start | bytes 524288 | tf_op jit(solution)/shard_map/all_to_all | solution.py:152

commit v4 on v3

--- a/solution.py
+++ b/solution.py
@@ -36,19 +36,43 @@
     return pl.CostEstimate(flops=flops, bytes_accessed=bytes_accessed, transcendentals=0)
 
 
-def pair_kernel(svt_ref, near_ref, tv_ref, out_ref):
-    lane = lax.broadcasted_iota(jnp.int32, (64, 256), 1)
-    even_s = (lane & 64) == 0
+def prepare_kernel(trial_ref, cs_ref, ct_ref, sent_ref, block_ref):
+    trial = trial_ref[...]
+    for k in range(8):
+        sent_ref[k, :128, :] = trial
+    for sp in range(2):
+        pair = jnp.concatenate([cs_ref[2 * sp], cs_ref[2 * sp + 1]], axis=0)
+        turned = jnp.transpose(pair.astype(F32)).astype(BF)
+        for k in range(8):
+            sent_ref[k, 128 + sp * NEAR : 128 + (sp + 1) * NEAR, :] = turned[:NEAR]
+        block_ref[sp * (64 - NEAR) : (sp + 1) * (64 - NEAR), :] = turned[NEAR:]
+    block_ref[128 - 2 * NEAR :, :] = jnp.concatenate([ct_ref[0], ct_ref[1]], axis=1)
+
+
+def pair_kernel(sv_ref, near_ref, tv_ref, out_ref):
+    row = lax.broadcasted_iota(jnp.int32, (32, 32), 0)
+    column = lax.broadcasted_iota(jnp.int32, (32, 32), 1)
+    lane = lax.broadcasted_iota(jnp.int32, (32, 128), 1)
+    parity = lax.broadcasted_iota(jnp.int32, (32, 128), 0) & 1
+    mine = (lane >> 6) == parity
+    factors = []
+    for s in range(4):
+        for odd in range(2):
+            chosen = ((row >> 1) * 2 + odd == column).astype(F32).astype(BF)
+            values = jnp.dot(chosen, sv_ref[s], preferred_element_type=F32)
+            values = jnp.where(mine, jnp.concatenate([values, values], axis=1), 0.0)
+            factors.append(jnp.transpose(values).astype(BF))
+    low = lax.broadcasted_iota(jnp.int32, (128, 128), 1) < 64
     for k in range(8):
         for sp in range(2):
-            at = sp * 32
-            block = jnp.concatenate([near_ref[k, at : at + 32], near_ref[k, 64 + at : 96 + at]], axis=1)
-            even = jnp.dot(svt_ref[2 * sp], block, preferred_element_type=F32)
-            odd = jnp.dot(svt_ref[2 * sp + 1], block, preferred_element_type=F32)
-            both = jnp.where(even_s, even, odd)
+            parts = []
+            for s in (2 * sp, 2 * sp + 1):
+                block = near_ref[k, s * 32 : s * 32 + 32]
+                parts += [jnp.dot(factors[2 * s + odd], block, preferred_element_type=F32) for odd in range(2)]
+            crossed = pltpu.roll(jnp.where(low, parts[2], parts[1]), 64, 1)
+            both = (jnp.where(low, parts[0], parts[3]) + crossed).reshape(2, 8, 8, 128)
             for peer in range(8):
-                rows = both[peer * 8 : peer * 8 + 8]
-                piece = jnp.concatenate([rows[:, :128], rows[:, 128:]], axis=0)
+                piece = jnp.concatenate([both[0, peer], both[1, peer]], axis=0)
                 at = sp * 128 + k * 16
                 out_ref[peer, at : at + 16, :] = piece.astype(BF)
         for peer in range(8):
@@ -64,8 +88,19 @@
     return kt_mask ^ ((kt_mask >> 1) & 1), place
 
 
-def screen_kernel(me_ref, pm_ref, own_ref, other_ref, every_ref, far_ref, ct_other_ref, out_ref, w_ref, xs, acc, ct):
+def chosen(near_ref, far_ref, j, i):
+    return jnp.where(j < 4, near_ref[j & 3, i], far_ref[j & 3, i])
+
+
+def screen_kernel(
+    me_ref, pm_ref, own_hbm, other_hbm, every_ref, near_ref, far_ref, ct_near_ref, ct_far_ref, out_ref,
+    own_ref, other_ref, w_ref, xs, acc, ys, ct, sems,
+):
     here, yx_here, core = me_ref[0], me_ref[1], me_ref[2]
+    pairs = ((own_hbm, own_ref), (other_hbm, other_ref))
+    fetches = [pltpu.make_async_copy(a, b, sems.at[i]) for i, (a, b) in enumerate(pairs)]
+    for fetch in fetches:
+        fetch.start()
 
     def eight_mats(step, carry):
         own, other = own_ref[pl.ds(step * 8, 8)], other_ref[pl.ds(step * 8, 8)]
@@ -77,7 +112,6 @@
             w_ref[pl.ds(step * 8, 8), half] = jnp.concatenate(parts, axis=1)
         return carry
 
-    lax.fori_loop(0, 64, eight_mats, 0)
     lane = lax.broadcasted_iota(jnp.int32, (128, 128), 1)
     first = lane < 64
 
@@ -90,7 +124,7 @@
             for kt in range(8):
                 at = 256 + (kt * 2 + sp) * NEAR
                 j, i = far_index(kt ^ here, yx ^ yx_here)
-                rest = far_ref[j, i, sp * (64 - NEAR) : (sp + 1) * (64 - NEAR)]
+                rest = chosen(near_ref, far_ref, j, i)[sp * (64 - NEAR) : (sp + 1) * (64 - NEAR)]
                 factors += [every_ref[yx, at : at + NEAR], rest]
             rhs = jnp.concatenate(factors, axis=0)
             x = lax.dot_general(lhs, rhs, (((1,), (1,)), ((), ())), preferred_element_type=F32)
@@ -102,6 +136,9 @@
         return carry
 
     lax.fori_loop(0, 8, one_chip, 0)
+    for fetch in fetches:
+        fetch.wait()
+    lax.fori_loop(0, 64, eight_mats, 0)
     for chunk in range(4):
 
         def one_target(t, carry, chunk=chunk):
@@ -111,30 +148,36 @@
                 mats += [pm_ref[t, source + j] for j in range(4)]
             for half in range(2):
                 w = [w_ref[m, half] for m in mats]
-                for n in range(16):
-                    terms = [w[j] * xs[chunk * 8 + j, half, n] for j in range(8)]
-                    while len(terms) > 1:
-                        terms = [terms[j] + terms[j + 1] for j in range(0, len(terms), 2)]
-                    total = terms[0].astype(F32)
-                    rows = slice(n * 8, n * 8 + 8)
+                for two in range(8):
+                    sums = []
+                    for n in (2 * two, 2 * two + 1):
+                        terms = [w[j] * xs[chunk * 8 + j, half, n] for j in range(8)]
+                        while len(terms) > 1:
+                            terms = [terms[j] + terms[j + 1] for j in range(0, len(terms), 2)]
+                        sums.append(terms[0].astype(F32))
+                    rows = slice(two * 16, two * 16 + 16)
                     for qb in range(2):
                         lanes = slice(half * 256 + qb * 128, half * 256 + qb * 128 + 128)
-                        part = total[qb * 8 : qb * 8 + 8]
+                        part = jnp.concatenate([x[qb * 8 : qb * 8 + 8] for x in sums], axis=0)
                         if chunk > 0:
                             part = part + acc[t, rows, lanes]
-                        acc[t, rows, lanes] = part
+                        if chunk < 3:
+                            acc[t, rows, lanes] = part
+                        else:
+                            ys[t, rows, lanes] = part.astype(BF)
             return carry
 
-        lax.fori_loop(0, 16, one_target, 0)
+        lax.fori_loop(0, 16, one_target, 0, unroll=4)
 
     def project(kt, carry):
         for yx in range(8):
             j, i = far_index(kt ^ here, yx ^ yx_here)
-            ct[pl.ds(pl.multiple_of((yx * 2 + core) * 32, 32), 32), :] = far_ref[j, i, 128 - 2 * NEAR :]
-            ct[pl.ds(pl.multiple_of((yx * 2 + 1 - core) * 32, 32), 32), :] = ct_other_ref[j, i]
+            ct[pl.ds(pl.multiple_of((yx * 2 + core) * 32, 32), 32), :] = chosen(near_ref, far_ref, j, i)[128 - 2 * NEAR :]
+            sibling = chosen(ct_near_ref, ct_far_ref, j, i)
+            ct[pl.ds(pl.multiple_of((yx * 2 + 1 - core) * 32, 32), 32), :] = sibling
         c = ct[...]
-        z0 = jnp.dot(acc[2 * kt].astype(BF), c, preferred_element_type=F32)
-        z1 = jnp.dot(acc[2 * kt + 1].astype(BF), c, preferred_element_type=F32)
+        z0 = jnp.dot(ys[2 * kt], c, preferred_element_type=F32)
+        z1 = jnp.dot(ys[2 * kt + 1], c, preferred_element_type=F32)
         out_ref[kt] = jnp.where(first, z0, z1).reshape(16, 8, 128).astype(BF)
         return carry
 
@@ -146,6 +189,7 @@
     me = jnp.stack([xh * 4 + z, y * 2 + xl, core]).astype(jnp.int32)
     vmem = pl.BlockSpec(memory_space=pltpu.VMEM)
     smem = pl.BlockSpec(memory_space=pltpu.SMEM)
+    hbm = pl.BlockSpec(memory_space=pl.ANY)
     params = pltpu.CompilerParams(vmem_limit_bytes=VMEM_LIMIT)
 
     def all_to_all(x, axes):
@@ -153,18 +197,25 @@
 
     other = swap(screened, "core", 2, 1)
 
-    trial = trial_vectors.reshape(2, 2, 2, 32, 64).transpose(2, 0, 3, 1, 4).reshape(128, 128)
-    cs = cond_source.reshape(2, 2, 64, 64).transpose(0, 3, 1, 2).reshape(2, 64, 128)
-    sent = jnp.concatenate([trial, cs[:, :NEAR].reshape(2 * NEAR, 128)], axis=0)
-    sent = jnp.broadcast_to(sent[None], (8, 128 + 2 * NEAR, 128))
+    trial = trial_vectors.reshape(4, 2, 16, 128).transpose(0, 2, 1, 3).reshape(128, 128)
+    sent, block = pl.pallas_call(
+        prepare_kernel,
+        out_shape=[
+            jax.ShapeDtypeStruct((8, 128 + 2 * NEAR, 128), BF),
+            jax.ShapeDtypeStruct((160 - 2 * NEAR, 128), BF),
+        ],
+        in_specs=[vmem] * 3,
+        out_specs=[vmem] * 2,
+        compiler_params=pltpu.CompilerParams(vmem_limit_bytes=62 * 1024 * 1024),
+        name="prepare",
+    )(trial, cond_source, cond_target.transpose(0, 2, 1))
     near = all_to_all(sent, KT)
 
-    sv = flip_if(core, val_source.reshape(4, 32, 8, 2, 4), 3)
-    svt = sv.reshape(4, 32, 64).transpose(0, 2, 1)
-    ct = cond_target.transpose(2, 0, 1).reshape(32, 128)
-    block = jnp.concatenate([cs[:, NEAR:].reshape(128 - 2 * NEAR, 128), ct], axis=0)[None]
+    sv = flip_if(core, val_source.reshape(4, 32, 8, 2, 4), 3).reshape(4, 32, 64)
+
+    block = block[None]
     block = doubled(block, "y", 4, 1)
-    block, svt = lax.optimization_barrier((block, svt))
+    block, sv = lax.optimization_barrier((block, sv))
     block = doubled(block, "y", 4, 3)
     block = doubled(block, X, 4, 1)[None]
     near, block = lax.optimization_barrier((near, block))
@@ -176,29 +227,33 @@
         out_specs=vmem,
         compiler_params=params,
         name="pairs",
-    )(svt, near, val_target.reshape(16, 128))
+    )(sv, near, val_target.reshape(16, 128))
     every = all_to_all(pieces, YX)
 
     block = doubled(block, "z", 4, 1)
     block = doubled(block, "z", 4, 3)
-    far = doubled(block, X, 4, 3)
-    ct_other = swap(far[:, :, 128 - 2 * NEAR :], "core", 2, 1)
+    far = swap(block, X, 4, 3)
+    ct_near, ct_far = (swap(x[:, :, 128 - 2 * NEAR :], "core", 2, 1) for x in (block, far))
 
     zs = pl.pallas_call(
         screen_kernel,
         out_shape=jax.ShapeDtypeStruct((8, 16, 8, 128), BF),
-        in_specs=[smem, smem] + [vmem] * 5,
+        in_specs=[smem, smem, hbm, hbm] + [vmem] * 5,
         out_specs=vmem,
         scratch_shapes=[
+            pltpu.VMEM((512, 4, 512), BF),
+            pltpu.VMEM((512, 4, 512), BF),
             pltpu.VMEM((512, 2, 16, 128), BF),
             pltpu.VMEM((32, 2, 16, 16, 128), BF),
             pltpu.VMEM((16, 128, 512), F32),
+            pltpu.VMEM((16, 128, 512), BF),
             pltpu.VMEM((512, 128), BF),
+            pltpu.SemaphoreType.DMA((2,)),
         ],
         compiler_params=pltpu.CompilerParams(vmem_limit_bytes=24 * 1024 * 1024),
         cost_estimate=cost(8_000_000_000, 16_000_000),
         name="screen",
-    )(me, pair_momentum, screened, other, every, far, ct_other)
+    )(me, pair_momentum, screened, other, every, block, far, ct_near, ct_far)
 
     tv = every[:, TV:]
     tv_other = swap(tv, "core", 2, 1).reshape(8, 2, 32, 32)

time: 99.6 us -> 98.2 us (0.986)
  waiting for transfers between devices: 30.1 us -> 21 us
  starting transfers between devices: 38.8 us -> 45.9 us
    ppermute x9 -> x10, waiting for transfers between devices: 19.7 us -> 11.2 us  [swap(): return lax.ppermute(x, axes, [(i, i ^ mask) for i in range(size)])]
    ppermute x9 -> x10, starting transfers between devices: 18.4 us -> 25.8 us  [swap(): return lax.ppermute(x, axes, [(i, i ^ mask) for i in range(size)])]
    pallas_call x0 -> x1, Pallas kernels: none -> 1.7 us  [local(): pl.pallas_call(prepare_kernel, out_shape=[jax.ShapeDtypeStruct((8, 128 +...]
    pallas_call x1, Pallas kernels: 19.5 us -> 18.1 us  [local(): pl.pallas_call(screen_kernel, out_shape=jax.ShapeDtypeStruct((8, 16, 8, 1...]
    unnamed x12 -> x7, local copies, waits for them, and re-layouts: 1.17 us -> 2.48 us
    reshape x3 -> x0, local copies, waits for them, and re-layouts: 1.06 us -> none  [the longest x2 0.97 us: local(): trial_vectors.reshape(2, 2, 2, 32, 64).transpose(2, 0, 3, 1, 4)]
  transfers between devices with their start and end apart: 12 -> 13, of which waited for: 8 -> 6; matrix products, arithmetic and copies ran while one was open for 6% -> 6% of each run, Pallas kernels for 22% -> 21%
where the time goes in v4:
time: 98.2 us; the launch traced here: 97.7 us
  starting transfers between devices  45.9 us (47%)
  Pallas kernels  22.3 us (23%)
  waiting for transfers between devices  21 us (21%)
  local copies, waits for them, and re-layouts  5.94 us (6%)
  other arithmetic  2.04 us (2%)
    ppermute x10, starting transfers between devices, swap(): return lax.ppermute(x, axes, [(i, i ^ mask) for i in range(size)])  25.8 us
    all_to_all x3, starting transfers between devices, all_to_all(): return lax.all_to_all(x, axes, split_axis=0, concat_axis=0, tiled=True)  20.1 us
    pallas_call x1, Pallas kernels, local(): pl.pallas_call(screen_kernel, out_shape=jax.ShapeDtypeStruct((8, 16, 8, 1...  18.1 us
    ppermute x10, waiting for transfers between devices, swap(): return lax.ppermute(x, axes, [(i, i ^ mask) for i in range(size)])  11.2 us
    all_to_all x3, waiting for transfers between devices, all_to_all(): return lax.all_to_all(x, axes, split_axis=0, concat_axis=0, tiled=True)  9.76 us
    pallas_call x1, Pallas kernels, local(): pl.pallas_call(pair_kernel, out_shape=jax.ShapeDtypeStruct((8, TV + 16, 1...  2.58 us
    unnamed x7, local copies, waits for them, and re-layouts  2.48 us
  transfers between devices with their start and end apart: 13, of which 6 were waited for; matrix products, arithmetic and copies ran while one was open for 6% of the time, Pallas kernels for 21%

profile of v4, /device:TPU:1, one launch (start us, length us, event | category | flops | bytes accessed | tf_op | source)
XLA Modules:
  0.0 97.7 jit_solution(13086986515570053945)
XLA Ops:
  0.0 1.7 %prepare.1 = (bf16[8,224,128]{2,1,0:T(8,128)(2,1)}, bf16[64,128]{1,0:T(8,128)(2,1)}) custom-call(bf16[128,128]{1,0:T(8,128)(2,1)} %bitcast.50, bf16[4,64,64]{2,1,0:T(8,128)(2,1)} %cs_ref.1, bf16[2,32,64]{2,1,0:T(8,128)(2,1)} %bitcast.51), custom_call_target="tpu_custom_call" | custom-call | tf_op jit(solution)/shard_map/prepare/pallas_call | solution.py:201
  1.7 2.1 %collective-permute-start = (bf16[1,64,128]{2,1,0:T(8,128)(2,1)}, bf16[1,64,128]{2,1,0:T(8,128)(2,1)S(1)}, u32[]{:S(2)}, u32[]{:S(2)}) collective-permute-start(bf16[1,64,128]{2,1,0:T(8,128)(2,1)} %bitcast.52), channel_id=1, source_target_pairs={{0,4},{4,0},{8,12},{12,8},{1,5},{5,1},{9,13},{13,9},{2,6},{6,2},{1... | collective-permute-start | bytes 49160 | tf_op jit(solution)/shard_map/ppermute | solution.py:24
  3.8 7.5 %all-to-all-start = ((bf16[8,224,128]{2,1,0:T(8,128)(2,1)}), bf16[8,224,128]{2,1,0:T(8,128)(2,1)S(1)}, u32[]{:S(2)}, u32[]{:S(2)}) async-start(bf16[8,224,128]{2,1,0:T(8,128)(2,1)} %get-tuple-element.13), calls=%async_computation | async-start | bytes 917504 | tf_op jit(solution)/shard_map/all_to_all | solution.py:196
  11.3 0.9 copy.11
  12.2 0.7 pad_maximum_fusion.3
  13.0 1.9 %collective-permute-start.1 = (bf16[2,64,128]{2,1,0:T(8,128)(2,1)S(1)}, bf16[2,64,128]{2,1,0:T(8,128)(2,1)S(1)}, u32[]{:S(2)}, u32[]{:S(2)}) collective-permute-start(bf16[2,64,128]{2,1,0:T(8,128)(2,1)S(1)} %pad_maximum_fusion.3), channel_id=1, source_target_pairs={{0,12},{4,8},{8,4},{12,0},{1,13},{5,9},{9,5},{13,1},{2,14},{6,10},... | collective-permute-start | bytes 98312 | tf_op jit(solution)/shard_map/ppermute | solution.py:24
  14.9 1.5 %collective-permute-start.4 = (bf16[512,4,512]{2,1,0:T(4,128)(2,1)}, bf16[512,4,512]{2,1,0:T(4,128)(2,1)}, u32[]{:S(2)}, u32[]{:S(2)}) collective-permute-start(bf16[512,4,512]{2,1,0:T(4,128)(2,1)} %own_hbm.1), channel_id=1, source_target_pairs={{0,1},{1,0},{2,3},{3,2},{4,5},{5,4},{6,7},{7,6},{8,9},{9,8},{10,11... | collective-permute-start | bytes 6291464 | tf_op jit(solution)/shard_map/ppermute | solution.py:24
  16.4 0.9 collective-permute-done.1
  17.2 0.4 collective-permute-start.2
  17.6 0.8 reshape.38.tv_ref
  18.5 2.2 %collective-permute-done.2 = bf16[4,64,128]{2,1,0:T(8,128)(2,1)S(1)} collective-permute-done((bf16[4,64,128]{2,1,0:T(8,128)(2,1)S(1)}, bf16[4,64,128]{2,1,0:T(8,128)(2,1)S(1)}, u32[]{:S(2)}, u32[]{:S(2)}) %collective-permute-start.2) | collective-permute-done | bytes 65568 | tf_op jit(solution)/shard_map/ppermute | solution.py:24
  20.8 2.6 %pairs.1 = bf16[8,1040,128]{2,1,0:T(8,128)(2,1)} custom-call(bf16[4,32,64]{2,1,0:T(8,128)(2,1)S(1)} %copy.12.sv_ref, bf16[8,224,128]{2,1,0:T(8,128)(2,1)S(1)} %all-to-all-done.near_ref, bf16[16,128]{1,0:T(8,128)(2,1)S(1)} %reshape.38.tv_ref), custom_call_target="tpu_custom_call" | custom-call | tf_op jit(solution)/shard_map/pairs/pallas_call | solution.py:223
  23.3 3.6 %all-to-all-start.1 = ((bf16[8,1040,128]{2,1,0:T(8,128)(2,1)}), bf16[8,1040,128]{2,1,0:T(8,128)(2,1)S(1)}, u32[]{:S(2)}, u32[]{:S(2)}) async-start(bf16[8,1040,128]{2,1,0:T(8,128)(2,1)} %pairs.1), calls=%async_computation.1 | async-start | bytes 4259840 | tf_op jit(solution)/shard_map/all_to_all | solution.py:196
  27.0 1.4 %collective-permute-start.5 = (bf16[1,8,64,128]{3,2,1,0:T(8,128)(2,1)S(1)}, bf16[1,8,64,128]{3,2,1,0:T(8,128)(2,1)S(1)}, u32[]{:S(2)}, u32[]{:S(2)}) collective-permute-start(bf16[1,8,64,128]{3,2,1,0:T(8,128)(2,1)S(1)} %maximum_bitcast_fusion), channel_id=1, source_target_pairs={{0,16},{16,0},{32,48},{48,32},{1,17},{17,1},{33,49},{49,33},{2,18}... | collective-permute-start | bytes 393224 | tf_op jit(solution)/shard_map/ppermute | solution.py:24
  28.3 2.5 %collective-permute-done.5 = bf16[1,8,64,128]{3,2,1,0:T(8,128)(2,1)S(1)} collective-permute-done((bf16[1,8,64,128]{3,2,1,0:T(8,128)(2,1)S(1)}, bf16[1,8,64,128]{3,2,1,0:T(8,128)(2,1)S(1)}, u32[]{:S(2)}, u32[]{:S(2)}) %collective-permute-start.5) | collective-permute-done | bytes 131104 | tf_op jit(solution)/shard_map/ppermute | solution.py:24
  30.9 2.5 %collective-permute-start.6 = (bf16[2,8,64,128]{3,2,1,0:T(8,128)(2,1)S(1)}, bf16[2,8,64,128]{3,2,1,0:T(8,128)(2,1)S(1)}, u32[]{:S(2)}, u32[]{:S(2)}) collective-permute-start(bf16[2,8,64,128]{3,2,1,0:T(8,128)(2,1)S(1)} %pad_maximum_fusion.1), channel_id=1, source_target_pairs={{0,48},{16,32},{32,16},{48,0},{1,49},{17,33},{33,17},{49,1},{2,50}... | collective-permute-start | bytes 786440 | tf_op jit(solution)/shard_map/ppermute | solution.py:24
  33.4 4.3 %collective-permute-done.6 = bf16[2,8,64,128]{3,2,1,0:T(8,128)(2,1)S(1)} collective-permute-done((bf16[2,8,64,128]{3,2,1,0:T(8,128)(2,1)S(1)}, bf16[2,8,64,128]{3,2,1,0:T(8,128)(2,1)S(1)}, u32[]{:S(2)}, u32[]{:S(2)}) %collective-permute-start.6) | collective-permute-done | bytes 262176 | tf_op jit(solution)/shard_map/ppermute | solution.py:24
  37.7 3.1 %collective-permute-start.7 = (bf16[4,8,64,128]{3,2,1,0:T(8,128)(2,1)S(1)}, bf16[4,8,64,128]{3,2,1,0:T(8,128)(2,1)S(1)}, u32[]{:S(2)}, u32[]{:S(2)}) collective-permute-start(bf16[4,8,64,128]{3,2,1,0:T(8,128)(2,1)S(1)} %constant_dynamic-update-slice_fusion.near_ref), channel_id=1, source_target_pairs={{0,66},{2,64},{64,2},{66,0},{1,67},{3,65},{65,3},{67,1},{4,70},{6,... | collective-permute-start | bytes 1572872 | tf_op jit(solution)/shard_map/ppermute | solution.py:24
  40.9 0.7 slice.21
  41.6 6.4 %collective-permute-start.8 = (bf16[4,8,32,128]{3,2,1,0:T(8,128)(2,1)}, bf16[4,8,32,128]{3,2,1,0:T(8,128)(2,1)S(1)}, u32[]{:S(2)}, u32[]{:S(2)}) collective-permute-start(bf16[4,8,32,128]{3,2,1,0:T(8,128)(2,1)} %slice.21), channel_id=1, source_target_pairs={{0,1},{1,0},{2,3},{3,2},{4,5},{5,4},{6,7},{7,6},{8,9},{9,8},{10,11... | collective-permute-start | bytes 786440 | tf_op jit(solution)/shard_map/ppermute | solution.py:24
  48.0 0.7 slice.22
  48.7 6.4 %collective-permute-start.9 = (bf16[4,8,32,128]{3,2,1,0:T(8,128)(2,1)}, bf16[4,8,32,128]{3,2,1,0:T(8,128)(2,1)}, u32[]{:S(2)}, u32[]{:S(2)}) collective-permute-start(bf16[4,8,32,128]{3,2,1,0:T(8,128)(2,1)} %slice.22), channel_id=1, source_target_pairs={{0,1},{1,0},{2,3},{3,2},{4,5},{5,4},{6,7},{7,6},{8,9},{9,8},{10,11... | collective-permute-start | bytes 786440 | tf_op jit(solution)/shard_map/ppermute | solution.py:24
  55.3 1.3 %collective-permute-done.9.ct_far_ref = bf16[4,8,32,128]{3,2,1,0:T(8,128)(2,1)} collective-permute-done((bf16[4,8,32,128]{3,2,1,0:T(8,128)(2,1)}, bf16[4,8,32,128]{3,2,1,0:T(8,128)(2,1)}, u32[]{:S(2)}, u32[]{:S(2)}) %collective-permute-start.9) | collective-permute-done | bytes 262176 | tf_op jit(solution)/shard_map/ppermute | solution.py:24
  56.6 1.6 %copy-done = bf16[512,4,512]{2,1,0:T(4,128)(2,1)S(1)} copy-done((bf16[512,4,512]{2,1,0:T(4,128)(2,1)S(1)}, bf16[512,4,512]{2,1,0:T(4,128)(2,1)}, u32[]{:S(2)}) %copy-start) | copy-done | bytes 2097176
  58.2 18.1 %screen.1 = bf16[8,16,8,128]{3,2,1,0:T(8,128)(2,1)} custom-call(s32[3]{0:T(128)S(1)} %pad_add_fusion.me_ref, s32[16,64]{1,0:T(8,128)S(1)} %copy-done.1, bf16[512,4,512]{2,1,0:T(4,128)(2,1)S(1)} %copy-done, bf16[512,4,512]{2,1,0:T(4,128)(2,1)} %collective-permute-done.4.other_hbm, bf16[8,1040,128]{2,1,0:T(8,128)(2,1)S(1)} %all-to-all-done.1.every_ref, ...), custom_call_target="tpu_custom_call" | custom-call | flops 8000000000 | bytes 16000000 | tf_op jit(solution)/shard_map/screen/pallas_call | solution.py:238
  76.4 9.0 %all-to-all-start.2 = ((bf16[128,8,128]{2,1,0:T(8,128)(2,1)}), bf16[128,8,128]{2,1,0:T(8,128)(2,1)S(1)}, u32[]{:S(2)}, u32[]{:S(2)}) async-start(bf16[128,8,128]{2,1,0:T(8,128)(2,1)} %bitcast.17), calls=%async_computation.2 | async-start | bytes 524288 | tf_op jit(solution)/shard_map/all_to_all | solution.py:196
  86.0 0.4 pad_maximum_fusion
  86.5 0.2 copy.17
  86.7 9.8 %all-to-all-done.2 = bf16[128,8,128]{2,1,0:T(8,128)(2,1)S(1)} async-done(((bf16[128,8,128]{2,1,0:T(8,128)(2,1)}), bf16[128,8,128]{2,1,0:T(8,128)(2,1)S(1)}, u32[]{:S(2)}, u32[]{:S(2)}) %all-to-all-start.2) | async-done | bytes 262176 | tf_op jit(solution)/shard_map/all_to_all | solution.py:196
  96.4 0.1 copy.18
  96.6 0.3 fusion.1
  97.0 0.6 pad_maximum_fusion.4
  (30 shorter events, 1.3 us)
Async XLA Ops:
  1.7 10.5 %collective-permute-start = (bf16[1,64,128]{2,1,0:T(8,128)(2,1)}, bf16[1,64,128]{2,1,0:T(8,128)(2,1)S(1)}, u32[]{:S(2)}, u32[]{:S(2)}) collective-permute-start(bf16[1,64,128]{2,1,0:T(8,128)(2,1)} %bitcast.52), channel_id=1, source_target_pairs={{0,4},{4,0},{8,12},{12,8},{1,5},{5,1},{9,13},{13,9},{2,6},{6,2},{1... | collective-permute-start | bytes 49160 | tf_op jit(solution)/shard_map/ppermute | solution.py:24
  3.8 16.9 %all-to-all-start = ((bf16[8,224,128]{2,1,0:T(8,128)(2,1)}), bf16[8,224,128]{2,1,0:T(8,128)(2,1)S(1)}, u32[]{:S(2)}, u32[]{:S(2)}) async-start(bf16[8,224,128]{2,1,0:T(8,128)(2,1)} %get-tuple-element.13), calls=%async_computation | async-start | bytes 917504 | tf_op jit(solution)/shard_map/all_to_all | solution.py:196
  13.0 4.3 %collective-permute-start.1 = (bf16[2,64,128]{2,1,0:T(8,128)(2,1)S(1)}, bf16[2,64,128]{2,1,0:T(8,128)(2,1)S(1)}, u32[]{:S(2)}, u32[]{:S(2)}) collective-permute-start(bf16[2,64,128]{2,1,0:T(8,128)(2,1)S(1)} %pad_maximum_fusion.3), channel_id=1, source_target_pairs={{0,12},{4,8},{8,4},{12,0},{1,13},{5,9},{9,5},{13,1},{2,14},{6,10},... | collective-permute-start | bytes 98312 | tf_op jit(solution)/shard_map/ppermute | solution.py:24
  14.9 41.8 %collective-permute-start.4 = (bf16[512,4,512]{2,1,0:T(4,128)(2,1)}, bf16[512,4,512]{2,1,0:T(4,128)(2,1)}, u32[]{:S(2)}, u32[]{:S(2)}) collective-permute-start(bf16[512,4,512]{2,1,0:T(4,128)(2,1)} %own_hbm.1), channel_id=1, source_target_pairs={{0,1},{1,0},{2,3},{3,2},{4,5},{5,4},{6,7},{7,6},{8,9},{9,8},{10,11... | collective-permute-start | bytes 6291464 | tf_op jit(solution)/shard_map/ppermute | solution.py:24
  17.2 3.5 %collective-permute-start.2 = (bf16[4,64,128]{2,1,0:T(8,128)(2,1)S(1)}, bf16[4,64,128]{2,1,0:T(8,128)(2,1)S(1)}, u32[]{:S(2)}, u32[]{:S(2)}) collective-permute-start(bf16[4,64,128]{2,1,0:T(8,128)(2,1)S(1)} %pad_maximum_fusion.2), channel_id=1, source_target_pairs={{0,2},{2,0},{64,66},{66,64},{1,3},{3,1},{65,67},{67,65},{4,6},{6,4... | collective-permute-start | bytes 196616 | tf_op jit(solution)/shard_map/ppermute | solution.py:24
  23.3 31.9 %all-to-all-start.1 = ((bf16[8,1040,128]{2,1,0:T(8,128)(2,1)}), bf16[8,1040,128]{2,1,0:T(8,128)(2,1)S(1)}, u32[]{:S(2)}, u32[]{:S(2)}) async-start(bf16[8,1040,128]{2,1,0:T(8,128)(2,1)} %pairs.1), calls=%async_computation.1 | async-start | bytes 4259840 | tf_op jit(solution)/shard_map/all_to_all | solution.py:196
  27.0 29.7 %copy-start.1 = (s32[16,64]{1,0:T(8,128)S(1)}, s32[16,64]{1,0:T(8,128)}, u32[]{:S(2)}) copy-start(s32[16,64]{1,0:T(8,128)} %pm_ref.1) | copy-start | bytes 12292
  27.0 3.9 %collective-permute-start.5 = (bf16[1,8,64,128]{3,2,1,0:T(8,128)(2,1)S(1)}, bf16[1,8,64,128]{3,2,1,0:T(8,128)(2,1)S(1)}, u32[]{:S(2)}, u32[]{:S(2)}) collective-permute-start(bf16[1,8,64,128]{3,2,1,0:T(8,128)(2,1)S(1)} %maximum_bitcast_fusion), channel_id=1, source_target_pairs={{0,16},{16,0},{32,48},{48,32},{1,17},{17,1},{33,49},{49,33},{2,18}... | collective-permute-start | bytes 393224 | tf_op jit(solution)/shard_map/ppermute | solution.py:24
  30.9 6.8 %collective-permute-start.6 = (bf16[2,8,64,128]{3,2,1,0:T(8,128)(2,1)S(1)}, bf16[2,8,64,128]{3,2,1,0:T(8,128)(2,1)S(1)}, u32[]{:S(2)}, u32[]{:S(2)}) collective-permute-start(bf16[2,8,64,128]{3,2,1,0:T(8,128)(2,1)S(1)} %pad_maximum_fusion.1), channel_id=1, source_target_pairs={{0,48},{16,32},{32,16},{48,0},{1,49},{17,33},{33,17},{49,1},{2,50}... | collective-permute-start | bytes 786440 | tf_op jit(solution)/shard_map/ppermute | solution.py:24
  37.7 10.2 %collective-permute-start.7 = (bf16[4,8,64,128]{3,2,1,0:T(8,128)(2,1)S(1)}, bf16[4,8,64,128]{3,2,1,0:T(8,128)(2,1)S(1)}, u32[]{:S(2)}, u32[]{:S(2)}) collective-permute-start(bf16[4,8,64,128]{3,2,1,0:T(8,128)(2,1)S(1)} %constant_dynamic-update-slice_fusion.near_ref), channel_id=1, source_target_pairs={{0,66},{2,64},{64,2},{66,0},{1,67},{3,65},{65,3},{67,1},{4,70},{6,... | collective-permute-start | bytes 1572872 | tf_op jit(solution)/shard_map/ppermute | solution.py:24
  41.6 13.7 %collective-permute-start.8 = (bf16[4,8,32,128]{3,2,1,0:T(8,128)(2,1)}, bf16[4,8,32,128]{3,2,1,0:T(8,128)(2,1)S(1)}, u32[]{:S(2)}, u32[]{:S(2)}) collective-permute-start(bf16[4,8,32,128]{3,2,1,0:T(8,128)(2,1)} %slice.21), channel_id=1, source_target_pairs={{0,1},{1,0},{2,3},{3,2},{4,5},{5,4},{6,7},{7,6},{8,9},{9,8},{10,11... | collective-permute-start | bytes 786440 | tf_op jit(solution)/shard_map/ppermute | solution.py:24
  48.7 7.9 %collective-permute-start.9 = (bf16[4,8,32,128]{3,2,1,0:T(8,128)(2,1)}, bf16[4,8,32,128]{3,2,1,0:T(8,128)(2,1)}, u32[]{:S(2)}, u32[]{:S(2)}) collective-permute-start(bf16[4,8,32,128]{3,2,1,0:T(8,128)(2,1)} %slice.22), channel_id=1, source_target_pairs={{0,1},{1,0},{2,3},{3,2},{4,5},{5,4},{6,7},{7,6},{8,9},{9,8},{10,11... | collective-permute-start | bytes 786440 | tf_op jit(solution)/shard_map/ppermute | solution.py:24
  55.2 30.4 %collective-permute-start.3 = (bf16[8,16,128]{2,1,0:T(8,128)(2,1)S(1)}, bf16[8,16,128]{2,1,0:T(8,128)(2,1)S(1)}, u32[]{:S(2)}, u32[]{:S(2)}) collective-permute-start(bf16[8,16,128]{2,1,0:T(8,128)(2,1)S(1)} %slice.20), channel_id=1, source_target_pairs={{0,1},{1,0},{2,3},{3,2},{4,5},{5,4},{6,7},{7,6},{8,9},{9,8},{10,11... | collective-permute-start | bytes 98312 | tf_op jit(solution)/shard_map/ppermute | solution.py:24
  56.6 1.6 %copy-start = (bf16[512,4,512]{2,1,0:T(4,128)(2,1)S(1)}, bf16[512,4,512]{2,1,0:T(4,128)(2,1)}, u32[]{:S(2)}) copy-start(bf16[512,4,512]{2,1,0:T(4,128)(2,1)} %own_hbm.1) | copy-start | bytes 6291460
  76.4 20.0 %all-to-all-start.2 = ((bf16[128,8,128]{2,1,0:T(8,128)(2,1)}), bf16[128,8,128]{2,1,0:T(8,128)(2,1)S(1)}, u32[]{:S(2)}, u32[]{:S(2)}) async-start(bf16[128,8,128]{2,1,0:T(8,128)(2,1)} %bitcast.17), calls=%async_computation.2 | async-start | bytes 524288 | tf_op jit(solution)/shard_map/all_to_all | solution.py:196

commit v5 on v4

--- a/solution.py
+++ b/solution.py
@@ -49,7 +49,14 @@
     block_ref[128 - 2 * NEAR :, :] = jnp.concatenate([ct_ref[0], ct_ref[1]], axis=1)
 
 
-def pair_kernel(sv_ref, near_ref, tv_ref, out_ref):
+def pair_kernel(sv_ref, near_ref, tv_ref, out_hbm, out_ref, sems):
+    for peer in range(8):
+        for k in range(8):
+            at = 256 + k * 2 * NEAR
+            out_ref[peer, at : at + 2 * NEAR, :] = near_ref[k, 128 : 128 + 2 * NEAR]
+        out_ref[peer, TV : TV + 16, :] = tv_ref[...]
+    early = pltpu.make_async_copy(out_ref.at[:, 256:], out_hbm.at[:, 256:], sems.at[0])
+    early.start()
     row = lax.broadcasted_iota(jnp.int32, (32, 32), 0)
     column = lax.broadcasted_iota(jnp.int32, (32, 32), 1)
     lane = lax.broadcasted_iota(jnp.int32, (32, 128), 1)
@@ -75,11 +82,10 @@
                 piece = jnp.concatenate([both[0, peer], both[1, peer]], axis=0)
                 at = sp * 128 + k * 16
                 out_ref[peer, at : at + 16, :] = piece.astype(BF)
-        for peer in range(8):
-            at = 256 + k * 2 * NEAR
-            out_ref[peer, at : at + 2 * NEAR, :] = near_ref[k, 128 : 128 + 2 * NEAR]
-    for peer in range(8):
-        out_ref[peer, TV : TV + 16, :] = tv_ref[...]
+    last = pltpu.make_async_copy(out_ref.at[:, :256], out_hbm.at[:, :256], sems.at[1])
+    last.start()
+    early.wait()
+    last.wait()
 
 
 def far_index(kt_mask, yx_mask):
@@ -93,11 +99,11 @@
 
 
 def screen_kernel(
-    me_ref, pm_ref, own_hbm, other_hbm, every_ref, near_ref, far_ref, ct_near_ref, ct_far_ref, out_ref,
-    own_ref, other_ref, w_ref, xs, acc, ys, ct, sems,
+    me_ref, pm_ref, own_ref, other_hbm, every_ref, near_ref, far_ref, ct_near_ref, ct_far_ref, out_ref,
+    other_ref, w_ref, xs, acc, ys, ct, sems,
 ):
     here, yx_here, core = me_ref[0], me_ref[1], me_ref[2]
-    pairs = ((own_hbm, own_ref), (other_hbm, other_ref))
+    pairs = ((other_hbm, other_ref),)
     fetches = [pltpu.make_async_copy(a, b, sems.at[i]) for i, (a, b) in enumerate(pairs)]
     for fetch in fetches:
         fetch.start()
@@ -224,7 +230,8 @@
         pair_kernel,
         out_shape=jax.ShapeDtypeStruct((8, TV + 16, 128), BF),
         in_specs=[vmem] * 3,
-        out_specs=vmem,
+        out_specs=hbm,
+        scratch_shapes=[pltpu.VMEM((8, TV + 16, 128), BF), pltpu.SemaphoreType.DMA((2,))],
         compiler_params=params,
         name="pairs",
     )(sv, near, val_target.reshape(16, 128))
@@ -238,17 +245,16 @@
     zs = pl.pallas_call(
         screen_kernel,
         out_shape=jax.ShapeDtypeStruct((8, 16, 8, 128), BF),
-        in_specs=[smem, smem, hbm, hbm] + [vmem] * 5,
+        in_specs=[smem, smem, vmem, hbm] + [vmem] * 5,
         out_specs=vmem,
         scratch_shapes=[
-            pltpu.VMEM((512, 4, 512), BF),
             pltpu.VMEM((512, 4, 512), BF),
             pltpu.VMEM((512, 2, 16, 128), BF),
             pltpu.VMEM((32, 2, 16, 16, 128), BF),
             pltpu.VMEM((16, 128, 512), F32),
             pltpu.VMEM((16, 128, 512), BF),
             pltpu.VMEM((512, 128), BF),
-            pltpu.SemaphoreType.DMA((2,)),
+            pltpu.SemaphoreType.DMA((1,)),
         ],
         compiler_params=pltpu.CompilerParams(vmem_limit_bytes=24 * 1024 * 1024),
         cost_estimate=cost(8_000_000_000, 16_000_000),

time: 98.2 us -> 97.6 us (level)
  no operation moved by 1% of the time
where the time goes in v5:
time: 97.6 us; the launch traced here: 97 us
  starting transfers between devices  45.9 us (47%)
  Pallas kernels  21.7 us (22%)
  waiting for transfers between devices  21 us (22%)
  local copies, waits for them, and re-layouts  5.94 us (6%)
  other arithmetic  2.04 us (2%)
    ppermute x10, starting transfers between devices, swap(): return lax.ppermute(x, axes, [(i, i ^ mask) for i in range(size)])  25.8 us
    all_to_all x3, starting transfers between devices, all_to_all(): return lax.all_to_all(x, axes, split_axis=0, concat_axis=0, tiled=True)  20.1 us
    pallas_call x1, Pallas kernels, local(): pl.pallas_call(screen_kernel, out_shape=jax.ShapeDtypeStruct((8, 16, 8, 1...  17.9 us
    ppermute x10, waiting for transfers between devices, swap(): return lax.ppermute(x, axes, [(i, i ^ mask) for i in range(size)])  11.2 us
    all_to_all x3, waiting for transfers between devices, all_to_all(): return lax.all_to_all(x, axes, split_axis=0, concat_axis=0, tiled=True)  9.76 us
    unnamed x7, local copies, waits for them, and re-layouts  2.48 us
    pallas_call x1, Pallas kernels, local(): pl.pallas_call(pair_kernel, out_shape=jax.ShapeDtypeStruct((8, TV + 16, 1...  2.07 us
  transfers between devices with their start and end apart: 13, of which 6 were waited for; matrix products, arithmetic and copies ran while one was open for 6% of the time, Pallas kernels for 21%

profile of v5, /device:TPU:1, one launch (start us, length us, event | category | flops | bytes accessed | tf_op | source)
XLA Modules:
  0.0 97.0 jit_solution(12206326565268758835)
XLA Ops:
  0.0 1.7 %prepare.1 = (bf16[8,224,128]{2,1,0:T(8,128)(2,1)}, bf16[64,128]{1,0:T(8,128)(2,1)}) custom-call(bf16[128,128]{1,0:T(8,128)(2,1)} %bitcast.50, bf16[4,64,64]{2,1,0:T(8,128)(2,1)} %cs_ref.1, bf16[2,32,64]{2,1,0:T(8,128)(2,1)} %bitcast.51), custom_call_target="tpu_custom_call" | custom-call | tf_op jit(solution)/shard_map/prepare/pallas_call | solution.py:207
  1.7 2.1 %collective-permute-start = (bf16[1,64,128]{2,1,0:T(8,128)(2,1)}, bf16[1,64,128]{2,1,0:T(8,128)(2,1)S(1)}, u32[]{:S(2)}, u32[]{:S(2)}) collective-permute-start(bf16[1,64,128]{2,1,0:T(8,128)(2,1)} %bitcast.52), channel_id=1, source_target_pairs={{0,4},{4,0},{8,12},{12,8},{1,5},{5,1},{9,13},{13,9},{2,6},{6,2},{1... | collective-permute-start | bytes 49160 | tf_op jit(solution)/shard_map/ppermute | solution.py:24
  3.8 7.5 %all-to-all-start = ((bf16[8,224,128]{2,1,0:T(8,128)(2,1)}), bf16[8,224,128]{2,1,0:T(8,128)(2,1)S(1)}, u32[]{:S(2)}, u32[]{:S(2)}) async-start(bf16[8,224,128]{2,1,0:T(8,128)(2,1)} %get-tuple-element.13), calls=%async_computation | async-start | bytes 917504 | tf_op jit(solution)/shard_map/all_to_all | solution.py:202
  11.3 0.9 copy.11
  12.2 0.7 pad_maximum_fusion.3
  13.0 1.9 %collective-permute-start.1 = (bf16[2,64,128]{2,1,0:T(8,128)(2,1)S(1)}, bf16[2,64,128]{2,1,0:T(8,128)(2,1)S(1)}, u32[]{:S(2)}, u32[]{:S(2)}) collective-permute-start(bf16[2,64,128]{2,1,0:T(8,128)(2,1)S(1)} %pad_maximum_fusion.3), channel_id=1, source_target_pairs={{0,12},{4,8},{8,4},{12,0},{1,13},{5,9},{9,5},{13,1},{2,14},{6,10},... | collective-permute-start | bytes 98312 | tf_op jit(solution)/shard_map/ppermute | solution.py:24
  14.9 1.5 %collective-permute-start.4 = (bf16[512,4,512]{2,1,0:T(4,128)(2,1)}, bf16[512,4,512]{2,1,0:T(4,128)(2,1)}, u32[]{:S(2)}, u32[]{:S(2)}) collective-permute-start(bf16[512,4,512]{2,1,0:T(4,128)(2,1)} %own_ref.1), channel_id=1, source_target_pairs={{0,1},{1,0},{2,3},{3,2},{4,5},{5,4},{6,7},{7,6},{8,9},{9,8},{10,11... | collective-permute-start | bytes 6291464 | tf_op jit(solution)/shard_map/ppermute | solution.py:24
  16.4 0.9 collective-permute-done.1
  17.2 0.4 collective-permute-start.2
  17.6 0.8 reshape.38.tv_ref
  18.5 2.2 %collective-permute-done.2 = bf16[4,64,128]{2,1,0:T(8,128)(2,1)S(1)} collective-permute-done((bf16[4,64,128]{2,1,0:T(8,128)(2,1)S(1)}, bf16[4,64,128]{2,1,0:T(8,128)(2,1)S(1)}, u32[]{:S(2)}, u32[]{:S(2)}) %collective-permute-start.2) | collective-permute-done | bytes 65568 | tf_op jit(solution)/shard_map/ppermute | solution.py:24
  20.8 2.1 %pairs.1 = bf16[8,1040,128]{2,1,0:T(8,128)(2,1)} custom-call(bf16[4,32,64]{2,1,0:T(8,128)(2,1)S(1)} %copy.12.sv_ref, bf16[8,224,128]{2,1,0:T(8,128)(2,1)S(1)} %all-to-all-done.near_ref, bf16[16,128]{1,0:T(8,128)(2,1)S(1)} %reshape.38.tv_ref), custom_call_target="tpu_custom_call" | custom-call | tf_op jit(solution)/shard_map/pairs/pallas_call | solution.py:229
  22.8 3.6 %all-to-all-start.1 = ((bf16[8,1040,128]{2,1,0:T(8,128)(2,1)}), bf16[8,1040,128]{2,1,0:T(8,128)(2,1)S(1)}, u32[]{:S(2)}, u32[]{:S(2)}) async-start(bf16[8,1040,128]{2,1,0:T(8,128)(2,1)} %pairs.1), calls=%async_computation.1 | async-start | bytes 4259840 | tf_op jit(solution)/shard_map/all_to_all | solution.py:202
  26.5 1.4 %collective-permute-start.5 = (bf16[1,8,64,128]{3,2,1,0:T(8,128)(2,1)S(1)}, bf16[1,8,64,128]{3,2,1,0:T(8,128)(2,1)S(1)}, u32[]{:S(2)}, u32[]{:S(2)}) collective-permute-start(bf16[1,8,64,128]{3,2,1,0:T(8,128)(2,1)S(1)} %maximum_bitcast_fusion), channel_id=1, source_target_pairs={{0,16},{16,0},{32,48},{48,32},{1,17},{17,1},{33,49},{49,33},{2,18}... | collective-permute-start | bytes 393224 | tf_op jit(solution)/shard_map/ppermute | solution.py:24
  27.9 2.5 %collective-permute-done.5 = bf16[1,8,64,128]{3,2,1,0:T(8,128)(2,1)S(1)} collective-permute-done((bf16[1,8,64,128]{3,2,1,0:T(8,128)(2,1)S(1)}, bf16[1,8,64,128]{3,2,1,0:T(8,128)(2,1)S(1)}, u32[]{:S(2)}, u32[]{:S(2)}) %collective-permute-start.5) | collective-permute-done | bytes 131104 | tf_op jit(solution)/shard_map/ppermute | solution.py:24
  30.4 2.5 %collective-permute-start.6 = (bf16[2,8,64,128]{3,2,1,0:T(8,128)(2,1)S(1)}, bf16[2,8,64,128]{3,2,1,0:T(8,128)(2,1)S(1)}, u32[]{:S(2)}, u32[]{:S(2)}) collective-permute-start(bf16[2,8,64,128]{3,2,1,0:T(8,128)(2,1)S(1)} %pad_maximum_fusion.1), channel_id=1, source_target_pairs={{0,48},{16,32},{32,16},{48,0},{1,49},{17,33},{33,17},{49,1},{2,50}... | collective-permute-start | bytes 786440 | tf_op jit(solution)/shard_map/ppermute | solution.py:24
  32.9 4.3 %collective-permute-done.6 = bf16[2,8,64,128]{3,2,1,0:T(8,128)(2,1)S(1)} collective-permute-done((bf16[2,8,64,128]{3,2,1,0:T(8,128)(2,1)S(1)}, bf16[2,8,64,128]{3,2,1,0:T(8,128)(2,1)S(1)}, u32[]{:S(2)}, u32[]{:S(2)}) %collective-permute-start.6) | collective-permute-done | bytes 262176 | tf_op jit(solution)/shard_map/ppermute | solution.py:24
  37.3 3.1 %collective-permute-start.7 = (bf16[4,8,64,128]{3,2,1,0:T(8,128)(2,1)S(1)}, bf16[4,8,64,128]{3,2,1,0:T(8,128)(2,1)S(1)}, u32[]{:S(2)}, u32[]{:S(2)}) collective-permute-start(bf16[4,8,64,128]{3,2,1,0:T(8,128)(2,1)S(1)} %constant_dynamic-update-slice_fusion.near_ref), channel_id=1, source_target_pairs={{0,66},{2,64},{64,2},{66,0},{1,67},{3,65},{65,3},{67,1},{4,70},{6,... | collective-permute-start | bytes 1572872 | tf_op jit(solution)/shard_map/ppermute | solution.py:24
  40.4 0.7 slice.21
  41.1 6.4 %collective-permute-start.8 = (bf16[4,8,32,128]{3,2,1,0:T(8,128)(2,1)}, bf16[4,8,32,128]{3,2,1,0:T(8,128)(2,1)S(1)}, u32[]{:S(2)}, u32[]{:S(2)}) collective-permute-start(bf16[4,8,32,128]{3,2,1,0:T(8,128)(2,1)} %slice.21), channel_id=1, source_target_pairs={{0,1},{1,0},{2,3},{3,2},{4,5},{5,4},{6,7},{7,6},{8,9},{9,8},{10,11... | collective-permute-start | bytes 786440 | tf_op jit(solution)/shard_map/ppermute | solution.py:24
  47.5 0.7 slice.22
  48.2 6.4 %collective-permute-start.9 = (bf16[4,8,32,128]{3,2,1,0:T(8,128)(2,1)}, bf16[4,8,32,128]{3,2,1,0:T(8,128)(2,1)}, u32[]{:S(2)}, u32[]{:S(2)}) collective-permute-start(bf16[4,8,32,128]{3,2,1,0:T(8,128)(2,1)} %slice.22), channel_id=1, source_target_pairs={{0,1},{1,0},{2,3},{3,2},{4,5},{5,4},{6,7},{7,6},{8,9},{9,8},{10,11... | collective-permute-start | bytes 786440 | tf_op jit(solution)/shard_map/ppermute | solution.py:24
  54.8 1.3 %collective-permute-done.9.ct_far_ref = bf16[4,8,32,128]{3,2,1,0:T(8,128)(2,1)} collective-permute-done((bf16[4,8,32,128]{3,2,1,0:T(8,128)(2,1)}, bf16[4,8,32,128]{3,2,1,0:T(8,128)(2,1)}, u32[]{:S(2)}, u32[]{:S(2)}) %collective-permute-start.9) | collective-permute-done | bytes 262176 | tf_op jit(solution)/shard_map/ppermute | solution.py:24
  56.2 1.6 %copy-done = bf16[512,4,512]{2,1,0:T(4,128)(2,1)S(1)} copy-done((bf16[512,4,512]{2,1,0:T(4,128)(2,1)S(1)}, bf16[512,4,512]{2,1,0:T(4,128)(2,1)}, u32[]{:S(2)}) %copy-start) | copy-done | bytes 2097176
  57.8 17.9 %screen.1 = bf16[8,16,8,128]{3,2,1,0:T(8,128)(2,1)} custom-call(s32[3]{0:T(128)S(1)} %pad_add_fusion.me_ref, s32[16,64]{1,0:T(8,128)S(1)} %copy-done.1, bf16[512,4,512]{2,1,0:T(4,128)(2,1)S(1)} %copy-done, bf16[512,4,512]{2,1,0:T(4,128)(2,1)} %collective-permute-done.4.other_hbm, bf16[8,1040,128]{2,1,0:T(8,128)(2,1)S(1)} %all-to-all-done.1.every_ref, ...), custom_call_target="tpu_custom_call" | custom-call | flops 8000000000 | bytes 16000000 | tf_op jit(solution)/shard_map/screen/pallas_call | solution.py:245
  75.8 9.0 %all-to-all-start.2 = ((bf16[128,8,128]{2,1,0:T(8,128)(2,1)}), bf16[128,8,128]{2,1,0:T(8,128)(2,1)S(1)}, u32[]{:S(2)}, u32[]{:S(2)}) async-start(bf16[128,8,128]{2,1,0:T(8,128)(2,1)} %bitcast.17), calls=%async_computation.2 | async-start | bytes 524288 | tf_op jit(solution)/shard_map/all_to_all | solution.py:202
  85.4 0.4 pad_maximum_fusion
  85.8 0.2 copy.17
  86.0 9.8 %all-to-all-done.2 = bf16[128,8,128]{2,1,0:T(8,128)(2,1)S(1)} async-done(((bf16[128,8,128]{2,1,0:T(8,128)(2,1)}), bf16[128,8,128]{2,1,0:T(8,128)(2,1)S(1)}, u32[]{:S(2)}, u32[]{:S(2)}) %all-to-all-start.2) | async-done | bytes 262176 | tf_op jit(solution)/shard_map/all_to_all | solution.py:202
  95.8 0.1 copy.18
  95.9 0.3 fusion.1
  96.4 0.6 pad_maximum_fusion.4
  (30 shorter events, 1.3 us)
Async XLA Ops:
  1.7 10.5 %collective-permute-start = (bf16[1,64,128]{2,1,0:T(8,128)(2,1)}, bf16[1,64,128]{2,1,0:T(8,128)(2,1)S(1)}, u32[]{:S(2)}, u32[]{:S(2)}) collective-permute-start(bf16[1,64,128]{2,1,0:T(8,128)(2,1)} %bitcast.52), channel_id=1, source_target_pairs={{0,4},{4,0},{8,12},{12,8},{1,5},{5,1},{9,13},{13,9},{2,6},{6,2},{1... | collective-permute-start | bytes 49160 | tf_op jit(solution)/shard_map/ppermute | solution.py:24
  3.8 16.9 %all-to-all-start = ((bf16[8,224,128]{2,1,0:T(8,128)(2,1)}), bf16[8,224,128]{2,1,0:T(8,128)(2,1)S(1)}, u32[]{:S(2)}, u32[]{:S(2)}) async-start(bf16[8,224,128]{2,1,0:T(8,128)(2,1)} %get-tuple-element.13), calls=%async_computation | async-start | bytes 917504 | tf_op jit(solution)/shard_map/all_to_all | solution.py:202
  13.0 4.3 %collective-permute-start.1 = (bf16[2,64,128]{2,1,0:T(8,128)(2,1)S(1)}, bf16[2,64,128]{2,1,0:T(8,128)(2,1)S(1)}, u32[]{:S(2)}, u32[]{:S(2)}) collective-permute-start(bf16[2,64,128]{2,1,0:T(8,128)(2,1)S(1)} %pad_maximum_fusion.3), channel_id=1, source_target_pairs={{0,12},{4,8},{8,4},{12,0},{1,13},{5,9},{9,5},{13,1},{2,14},{6,10},... | collective-permute-start | bytes 98312 | tf_op jit(solution)/shard_map/ppermute | solution.py:24
  14.9 41.3 %collective-permute-start.4 = (bf16[512,4,512]{2,1,0:T(4,128)(2,1)}, bf16[512,4,512]{2,1,0:T(4,128)(2,1)}, u32[]{:S(2)}, u32[]{:S(2)}) collective-permute-start(bf16[512,4,512]{2,1,0:T(4,128)(2,1)} %own_ref.1), channel_id=1, source_target_pairs={{0,1},{1,0},{2,3},{3,2},{4,5},{5,4},{6,7},{7,6},{8,9},{9,8},{10,11... | collective-permute-start | bytes 6291464 | tf_op jit(solution)/shard_map/ppermute | solution.py:24
  17.2 3.5 %collective-permute-start.2 = (bf16[4,64,128]{2,1,0:T(8,128)(2,1)S(1)}, bf16[4,64,128]{2,1,0:T(8,128)(2,1)S(1)}, u32[]{:S(2)}, u32[]{:S(2)}) collective-permute-start(bf16[4,64,128]{2,1,0:T(8,128)(2,1)S(1)} %pad_maximum_fusion.2), channel_id=1, source_target_pairs={{0,2},{2,0},{64,66},{66,64},{1,3},{3,1},{65,67},{67,65},{4,6},{6,4... | collective-permute-start | bytes 196616 | tf_op jit(solution)/shard_map/ppermute | solution.py:24
  22.8 31.9 %all-to-all-start.1 = ((bf16[8,1040,128]{2,1,0:T(8,128)(2,1)}), bf16[8,1040,128]{2,1,0:T(8,128)(2,1)S(1)}, u32[]{:S(2)}, u32[]{:S(2)}) async-start(bf16[8,1040,128]{2,1,0:T(8,128)(2,1)} %pairs.1), calls=%async_computation.1 | async-start | bytes 4259840 | tf_op jit(solution)/shard_map/all_to_all | solution.py:202
  26.5 29.7 %copy-start.1 = (s32[16,64]{1,0:T(8,128)S(1)}, s32[16,64]{1,0:T(8,128)}, u32[]{:S(2)}) copy-start(s32[16,64]{1,0:T(8,128)} %pm_ref.1) | copy-start | bytes 12292
  26.5 3.9 %collective-permute-start.5 = (bf16[1,8,64,128]{3,2,1,0:T(8,128)(2,1)S(1)}, bf16[1,8,64,128]{3,2,1,0:T(8,128)(2,1)S(1)}, u32[]{:S(2)}, u32[]{:S(2)}) collective-permute-start(bf16[1,8,64,128]{3,2,1,0:T(8,128)(2,1)S(1)} %maximum_bitcast_fusion), channel_id=1, source_target_pairs={{0,16},{16,0},{32,48},{48,32},{1,17},{17,1},{33,49},{49,33},{2,18}... | collective-permute-start | bytes 393224 | tf_op jit(solution)/shard_map/ppermute | solution.py:24
  30.4 6.8 %collective-permute-start.6 = (bf16[2,8,64,128]{3,2,1,0:T(8,128)(2,1)S(1)}, bf16[2,8,64,128]{3,2,1,0:T(8,128)(2,1)S(1)}, u32[]{:S(2)}, u32[]{:S(2)}) collective-permute-start(bf16[2,8,64,128]{3,2,1,0:T(8,128)(2,1)S(1)} %pad_maximum_fusion.1), channel_id=1, source_target_pairs={{0,48},{16,32},{32,16},{48,0},{1,49},{17,33},{33,17},{49,1},{2,50}... | collective-permute-start | bytes 786440 | tf_op jit(solution)/shard_map/ppermute | solution.py:24
  37.3 10.2 %collective-permute-start.7 = (bf16[4,8,64,128]{3,2,1,0:T(8,128)(2,1)S(1)}, bf16[4,8,64,128]{3,2,1,0:T(8,128)(2,1)S(1)}, u32[]{:S(2)}, u32[]{:S(2)}) collective-permute-start(bf16[4,8,64,128]{3,2,1,0:T(8,128)(2,1)S(1)} %constant_dynamic-update-slice_fusion.near_ref), channel_id=1, source_target_pairs={{0,66},{2,64},{64,2},{66,0},{1,67},{3,65},{65,3},{67,1},{4,70},{6,... | collective-permute-start | bytes 1572872 | tf_op jit(solution)/shard_map/ppermute | solution.py:24
  41.1 13.7 %collective-permute-start.8 = (bf16[4,8,32,128]{3,2,1,0:T(8,128)(2,1)}, bf16[4,8,32,128]{3,2,1,0:T(8,128)(2,1)S(1)}, u32[]{:S(2)}, u32[]{:S(2)}) collective-permute-start(bf16[4,8,32,128]{3,2,1,0:T(8,128)(2,1)} %slice.21), channel_id=1, source_target_pairs={{0,1},{1,0},{2,3},{3,2},{4,5},{5,4},{6,7},{7,6},{8,9},{9,8},{10,11... | collective-permute-start | bytes 786440 | tf_op jit(solution)/shard_map/ppermute | solution.py:24
  48.2 7.9 %collective-permute-start.9 = (bf16[4,8,32,128]{3,2,1,0:T(8,128)(2,1)}, bf16[4,8,32,128]{3,2,1,0:T(8,128)(2,1)}, u32[]{:S(2)}, u32[]{:S(2)}) collective-permute-start(bf16[4,8,32,128]{3,2,1,0:T(8,128)(2,1)} %slice.22), channel_id=1, source_target_pairs={{0,1},{1,0},{2,3},{3,2},{4,5},{5,4},{6,7},{7,6},{8,9},{9,8},{10,11... | collective-permute-start | bytes 786440 | tf_op jit(solution)/shard_map/ppermute | solution.py:24
  54.7 30.2 %collective-permute-start.3 = (bf16[8,16,128]{2,1,0:T(8,128)(2,1)S(1)}, bf16[8,16,128]{2,1,0:T(8,128)(2,1)S(1)}, u32[]{:S(2)}, u32[]{:S(2)}) collective-permute-start(bf16[8,16,128]{2,1,0:T(8,128)(2,1)S(1)} %slice.20), channel_id=1, source_target_pairs={{0,1},{1,0},{2,3},{3,2},{4,5},{5,4},{6,7},{7,6},{8,9},{9,8},{10,11... | collective-permute-start | bytes 98312 | tf_op jit(solution)/shard_map/ppermute | solution.py:24
  56.2 1.6 %copy-start = (bf16[512,4,512]{2,1,0:T(4,128)(2,1)S(1)}, bf16[512,4,512]{2,1,0:T(4,128)(2,1)}, u32[]{:S(2)}) copy-start(bf16[512,4,512]{2,1,0:T(4,128)(2,1)} %own_ref.1) | copy-start | bytes 6291460
  75.8 20.0 %all-to-all-start.2 = ((bf16[128,8,128]{2,1,0:T(8,128)(2,1)}), bf16[128,8,128]{2,1,0:T(8,128)(2,1)S(1)}, u32[]{:S(2)}, u32[]{:S(2)}) async-start(bf16[128,8,128]{2,1,0:T(8,128)(2,1)} %bitcast.17), calls=%async_computation.2 | async-start | bytes 524288 | tf_op jit(solution)/shard_map/all_to_all | solution.py:202

commit v6 on v5

--- a/solution.py
+++ b/solution.py
@@ -100,7 +100,7 @@
 
 def screen_kernel(
     me_ref, pm_ref, own_ref, other_hbm, every_ref, near_ref, far_ref, ct_near_ref, ct_far_ref, out_ref,
-    other_ref, w_ref, xs, acc, ys, ct, sems,
+    other_ref, w_ref, xs, acc, ys, sems,
 ):
     here, yx_here, core = me_ref[0], me_ref[1], me_ref[2]
     pairs = ((other_hbm, other_ref),)
@@ -141,7 +141,7 @@
                 xs[pl.ds(yx * 4 + sp * 2, 2), half] = tile.astype(BF)
         return carry
 
-    lax.fori_loop(0, 8, one_chip, 0)
+    lax.fori_loop(0, 8, one_chip, 0, unroll=4)
     for fetch in fetches:
         fetch.wait()
     lax.fori_loop(0, 64, eight_mats, 0)
@@ -176,18 +176,19 @@
         lax.fori_loop(0, 16, one_target, 0, unroll=4)
 
     def project(kt, carry):
+        parts = []
         for yx in range(8):
             j, i = far_index(kt ^ here, yx ^ yx_here)
-            ct[pl.ds(pl.multiple_of((yx * 2 + core) * 32, 32), 32), :] = chosen(near_ref, far_ref, j, i)[128 - 2 * NEAR :]
+            mine = chosen(near_ref, far_ref, j, i)[128 - 2 * NEAR :]
             sibling = chosen(ct_near_ref, ct_far_ref, j, i)
-            ct[pl.ds(pl.multiple_of((yx * 2 + 1 - core) * 32, 32), 32), :] = sibling
-        c = ct[...]
+            parts += [jnp.where(core == 0, mine, sibling), jnp.where(core == 0, sibling, mine)]
+        c = jnp.concatenate(parts, axis=0)
         z0 = jnp.dot(ys[2 * kt], c, preferred_element_type=F32)
         z1 = jnp.dot(ys[2 * kt + 1], c, preferred_element_type=F32)
         out_ref[kt] = jnp.where(first, z0, z1).reshape(16, 8, 128).astype(BF)
         return carry
 
-    lax.fori_loop(0, 8, project, 0)
+    lax.fori_loop(0, 8, project, 0, unroll=4)
 
 
 def local(val_target, cond_target, val_source, cond_source, trial_vectors, screened, pair_momentum):
@@ -253,7 +254,6 @@
             pltpu.VMEM((32, 2, 16, 16, 128), BF),
             pltpu.VMEM((16, 128, 512), F32),
             pltpu.VMEM((16, 128, 512), BF),
-            pltpu.VMEM((512, 128), BF),
             pltpu.SemaphoreType.DMA((1,)),
         ],
         compiler_params=pltpu.CompilerParams(vmem_limit_bytes=24 * 1024 * 1024),

time: 97.6 us -> 95.3 us (0.976)
  Pallas kernels: 21.7 us -> 19.3 us
    pallas_call x1, Pallas kernels: 17.9 us -> 15.6 us  [local(): pl.pallas_call(screen_kernel, out_shape=jax.ShapeDtypeStruct((8, 16, 8, 1...]
  transfers between devices with their start and end apart: 13 -> 13, of which waited for: 6 -> 6; matrix products, arithmetic and copies ran while one was open for 6% -> 6% of each run, Pallas kernels for 21% -> 19%
where the time goes in v6:
time: 95.3 us; the launch traced here: 94.6 us
  starting transfers between devices  45.9 us (48%)
  waiting for transfers between devices  21 us (22%)
  Pallas kernels  19.3 us (20%)
  local copies, waits for them, and re-layouts  5.94 us (6%)
  other arithmetic  2.04 us (2%)
    ppermute x10, starting transfers between devices, swap(): return lax.ppermute(x, axes, [(i, i ^ mask) for i in range(size)])  25.8 us
    all_to_all x3, starting transfers between devices, all_to_all(): return lax.all_to_all(x, axes, split_axis=0, concat_axis=0, tiled=True)  20.1 us
    pallas_call x1, Pallas kernels, local(): pl.pallas_call(screen_kernel, out_shape=jax.ShapeDtypeStruct((8, 16, 8, 1...  15.6 us
    ppermute x10, waiting for transfers between devices, swap(): return lax.ppermute(x, axes, [(i, i ^ mask) for i in range(size)])  11.2 us
    all_to_all x3, waiting for transfers between devices, all_to_all(): return lax.all_to_all(x, axes, split_axis=0, concat_axis=0, tiled=True)  9.76 us
    unnamed x7, local copies, waits for them, and re-layouts  2.48 us
    pallas_call x1, Pallas kernels, local(): pl.pallas_call(pair_kernel, out_shape=jax.ShapeDtypeStruct((8, TV + 16, 1...  2.07 us
  transfers between devices with their start and end apart: 13, of which 6 were waited for; matrix products, arithmetic and copies ran while one was open for 6% of the time, Pallas kernels for 19%

profile of v6, /device:TPU:1, one launch (start us, length us, event | category | flops | bytes accessed | tf_op | source)
XLA Modules:
  0.0 94.6 jit_solution(17439481107941519978)
XLA Ops:
  0.0 1.7 %prepare.1 = (bf16[8,224,128]{2,1,0:T(8,128)(2,1)}, bf16[64,128]{1,0:T(8,128)(2,1)}) custom-call(bf16[128,128]{1,0:T(8,128)(2,1)} %bitcast.50, bf16[4,64,64]{2,1,0:T(8,128)(2,1)} %cs_ref.1, bf16[2,32,64]{2,1,0:T(8,128)(2,1)} %bitcast.51), custom_call_target="tpu_custom_call" | custom-call | tf_op jit(solution)/shard_map/prepare/pallas_call | solution.py:208
  1.7 2.1 %collective-permute-start = (bf16[1,64,128]{2,1,0:T(8,128)(2,1)}, bf16[1,64,128]{2,1,0:T(8,128)(2,1)S(1)}, u32[]{:S(2)}, u32[]{:S(2)}) collective-permute-start(bf16[1,64,128]{2,1,0:T(8,128)(2,1)} %bitcast.52), channel_id=1, source_target_pairs={{0,4},{4,0},{8,12},{12,8},{1,5},{5,1},{9,13},{13,9},{2,6},{6,2},{1... | collective-permute-start | bytes 49160 | tf_op jit(solution)/shard_map/ppermute | solution.py:24
  3.8 7.5 %all-to-all-start = ((bf16[8,224,128]{2,1,0:T(8,128)(2,1)}), bf16[8,224,128]{2,1,0:T(8,128)(2,1)S(1)}, u32[]{:S(2)}, u32[]{:S(2)}) async-start(bf16[8,224,128]{2,1,0:T(8,128)(2,1)} %get-tuple-element.13), calls=%async_computation | async-start | bytes 917504 | tf_op jit(solution)/shard_map/all_to_all | solution.py:203
  11.3 0.9 copy.11
  12.2 0.7 pad_maximum_fusion.3
  13.0 1.9 %collective-permute-start.1 = (bf16[2,64,128]{2,1,0:T(8,128)(2,1)S(1)}, bf16[2,64,128]{2,1,0:T(8,128)(2,1)S(1)}, u32[]{:S(2)}, u32[]{:S(2)}) collective-permute-start(bf16[2,64,128]{2,1,0:T(8,128)(2,1)S(1)} %pad_maximum_fusion.3), channel_id=1, source_target_pairs={{0,12},{4,8},{8,4},{12,0},{1,13},{5,9},{9,5},{13,1},{2,14},{6,10},... | collective-permute-start | bytes 98312 | tf_op jit(solution)/shard_map/ppermute | solution.py:24
  14.9 1.5 %collective-permute-start.4 = (bf16[512,4,512]{2,1,0:T(4,128)(2,1)}, bf16[512,4,512]{2,1,0:T(4,128)(2,1)}, u32[]{:S(2)}, u32[]{:S(2)}) collective-permute-start(bf16[512,4,512]{2,1,0:T(4,128)(2,1)} %own_ref.1), channel_id=1, source_target_pairs={{0,1},{1,0},{2,3},{3,2},{4,5},{5,4},{6,7},{7,6},{8,9},{9,8},{10,11... | collective-permute-start | bytes 6291464 | tf_op jit(solution)/shard_map/ppermute | solution.py:24
  16.4 0.9 collective-permute-done.1
  17.2 0.4 collective-permute-start.2
  17.6 0.8 reshape.38.tv_ref
  18.5 2.2 %collective-permute-done.2 = bf16[4,64,128]{2,1,0:T(8,128)(2,1)S(1)} collective-permute-done((bf16[4,64,128]{2,1,0:T(8,128)(2,1)S(1)}, bf16[4,64,128]{2,1,0:T(8,128)(2,1)S(1)}, u32[]{:S(2)}, u32[]{:S(2)}) %collective-permute-start.2) | collective-permute-done | bytes 65568 | tf_op jit(solution)/shard_map/ppermute | solution.py:24
  20.8 2.1 %pairs.1 = bf16[8,1040,128]{2,1,0:T(8,128)(2,1)} custom-call(bf16[4,32,64]{2,1,0:T(8,128)(2,1)S(1)} %copy.12.sv_ref, bf16[8,224,128]{2,1,0:T(8,128)(2,1)S(1)} %all-to-all-done.near_ref, bf16[16,128]{1,0:T(8,128)(2,1)S(1)} %reshape.38.tv_ref), custom_call_target="tpu_custom_call" | custom-call | tf_op jit(solution)/shard_map/pairs/pallas_call | solution.py:230
  22.8 3.6 %all-to-all-start.1 = ((bf16[8,1040,128]{2,1,0:T(8,128)(2,1)}), bf16[8,1040,128]{2,1,0:T(8,128)(2,1)S(1)}, u32[]{:S(2)}, u32[]{:S(2)}) async-start(bf16[8,1040,128]{2,1,0:T(8,128)(2,1)} %pairs.1), calls=%async_computation.1 | async-start | bytes 4259840 | tf_op jit(solution)/shard_map/all_to_all | solution.py:203
  26.5 1.4 %collective-permute-start.5 = (bf16[1,8,64,128]{3,2,1,0:T(8,128)(2,1)S(1)}, bf16[1,8,64,128]{3,2,1,0:T(8,128)(2,1)S(1)}, u32[]{:S(2)}, u32[]{:S(2)}) collective-permute-start(bf16[1,8,64,128]{3,2,1,0:T(8,128)(2,1)S(1)} %maximum_bitcast_fusion), channel_id=1, source_target_pairs={{0,16},{16,0},{32,48},{48,32},{1,17},{17,1},{33,49},{49,33},{2,18}... | collective-permute-start | bytes 393224 | tf_op jit(solution)/shard_map/ppermute | solution.py:24
  27.9 2.5 %collective-permute-done.5 = bf16[1,8,64,128]{3,2,1,0:T(8,128)(2,1)S(1)} collective-permute-done((bf16[1,8,64,128]{3,2,1,0:T(8,128)(2,1)S(1)}, bf16[1,8,64,128]{3,2,1,0:T(8,128)(2,1)S(1)}, u32[]{:S(2)}, u32[]{:S(2)}) %collective-permute-start.5) | collective-permute-done | bytes 131104 | tf_op jit(solution)/shard_map/ppermute | solution.py:24
  30.4 2.5 %collective-permute-start.6 = (bf16[2,8,64,128]{3,2,1,0:T(8,128)(2,1)S(1)}, bf16[2,8,64,128]{3,2,1,0:T(8,128)(2,1)S(1)}, u32[]{:S(2)}, u32[]{:S(2)}) collective-permute-start(bf16[2,8,64,128]{3,2,1,0:T(8,128)(2,1)S(1)} %pad_maximum_fusion.1), channel_id=1, source_target_pairs={{0,48},{16,32},{32,16},{48,0},{1,49},{17,33},{33,17},{49,1},{2,50}... | collective-permute-start | bytes 786440 | tf_op jit(solution)/shard_map/ppermute | solution.py:24
  32.9 4.3 %collective-permute-done.6 = bf16[2,8,64,128]{3,2,1,0:T(8,128)(2,1)S(1)} collective-permute-done((bf16[2,8,64,128]{3,2,1,0:T(8,128)(2,1)S(1)}, bf16[2,8,64,128]{3,2,1,0:T(8,128)(2,1)S(1)}, u32[]{:S(2)}, u32[]{:S(2)}) %collective-permute-start.6) | collective-permute-done | bytes 262176 | tf_op jit(solution)/shard_map/ppermute | solution.py:24
  37.3 3.1 %collective-permute-start.7 = (bf16[4,8,64,128]{3,2,1,0:T(8,128)(2,1)S(1)}, bf16[4,8,64,128]{3,2,1,0:T(8,128)(2,1)S(1)}, u32[]{:S(2)}, u32[]{:S(2)}) collective-permute-start(bf16[4,8,64,128]{3,2,1,0:T(8,128)(2,1)S(1)} %constant_dynamic-update-slice_fusion.near_ref), channel_id=1, source_target_pairs={{0,66},{2,64},{64,2},{66,0},{1,67},{3,65},{65,3},{67,1},{4,70},{6,... | collective-permute-start | bytes 1572872 | tf_op jit(solution)/shard_map/ppermute | solution.py:24
  40.4 0.7 slice.21
  41.1 6.4 %collective-permute-start.8 = (bf16[4,8,32,128]{3,2,1,0:T(8,128)(2,1)}, bf16[4,8,32,128]{3,2,1,0:T(8,128)(2,1)S(1)}, u32[]{:S(2)}, u32[]{:S(2)}) collective-permute-start(bf16[4,8,32,128]{3,2,1,0:T(8,128)(2,1)} %slice.21), channel_id=1, source_target_pairs={{0,1},{1,0},{2,3},{3,2},{4,5},{5,4},{6,7},{7,6},{8,9},{9,8},{10,11... | collective-permute-start | bytes 786440 | tf_op jit(solution)/shard_map/ppermute | solution.py:24
  47.5 0.7 slice.22
  48.2 6.4 %collective-permute-start.9 = (bf16[4,8,32,128]{3,2,1,0:T(8,128)(2,1)}, bf16[4,8,32,128]{3,2,1,0:T(8,128)(2,1)}, u32[]{:S(2)}, u32[]{:S(2)}) collective-permute-start(bf16[4,8,32,128]{3,2,1,0:T(8,128)(2,1)} %slice.22), channel_id=1, source_target_pairs={{0,1},{1,0},{2,3},{3,2},{4,5},{5,4},{6,7},{7,6},{8,9},{9,8},{10,11... | collective-permute-start | bytes 786440 | tf_op jit(solution)/shard_map/ppermute | solution.py:24
  54.8 1.3 %collective-permute-done.9.ct_far_ref = bf16[4,8,32,128]{3,2,1,0:T(8,128)(2,1)} collective-permute-done((bf16[4,8,32,128]{3,2,1,0:T(8,128)(2,1)}, bf16[4,8,32,128]{3,2,1,0:T(8,128)(2,1)}, u32[]{:S(2)}, u32[]{:S(2)}) %collective-permute-start.9) | collective-permute-done | bytes 262176 | tf_op jit(solution)/shard_map/ppermute | solution.py:24
  56.2 1.6 %copy-done = bf16[512,4,512]{2,1,0:T(4,128)(2,1)S(1)} copy-done((bf16[512,4,512]{2,1,0:T(4,128)(2,1)S(1)}, bf16[512,4,512]{2,1,0:T(4,128)(2,1)}, u32[]{:S(2)}) %copy-start) | copy-done | bytes 2097176
  57.8 15.6 %screen.1 = bf16[8,16,8,128]{3,2,1,0:T(8,128)(2,1)} custom-call(s32[3]{0:T(128)S(1)} %pad_add_fusion.me_ref, s32[16,64]{1,0:T(8,128)S(1)} %copy-done.1, bf16[512,4,512]{2,1,0:T(4,128)(2,1)S(1)} %copy-done, bf16[512,4,512]{2,1,0:T(4,128)(2,1)} %collective-permute-done.4.other_hbm, bf16[8,1040,128]{2,1,0:T(8,128)(2,1)S(1)} %all-to-all-done.1.every_ref, ...), custom_call_target="tpu_custom_call" | custom-call | flops 8000000000 | bytes 16000000 | tf_op jit(solution)/shard_map/screen/pallas_call | solution.py:246
  73.4 9.0 %all-to-all-start.2 = ((bf16[128,8,128]{2,1,0:T(8,128)(2,1)}), bf16[128,8,128]{2,1,0:T(8,128)(2,1)S(1)}, u32[]{:S(2)}, u32[]{:S(2)}) async-start(bf16[128,8,128]{2,1,0:T(8,128)(2,1)} %bitcast.17), calls=%async_computation.2 | async-start | bytes 524288 | tf_op jit(solution)/shard_map/all_to_all | solution.py:203
  83.0 0.4 pad_maximum_fusion
  83.4 0.2 copy.17
  83.6 9.8 %all-to-all-done.2 = bf16[128,8,128]{2,1,0:T(8,128)(2,1)S(1)} async-done(((bf16[128,8,128]{2,1,0:T(8,128)(2,1)}), bf16[128,8,128]{2,1,0:T(8,128)(2,1)S(1)}, u32[]{:S(2)}, u32[]{:S(2)}) %all-to-all-start.2) | async-done | bytes 262176 | tf_op jit(solution)/shard_map/all_to_all | solution.py:203
  93.4 0.1 copy.18
  93.5 0.3 fusion.1
  94.0 0.6 pad_maximum_fusion.4
  (30 shorter events, 1.3 us)
Async XLA Ops:
  1.7 10.5 %collective-permute-start = (bf16[1,64,128]{2,1,0:T(8,128)(2,1)}, bf16[1,64,128]{2,1,0:T(8,128)(2,1)S(1)}, u32[]{:S(2)}, u32[]{:S(2)}) collective-permute-start(bf16[1,64,128]{2,1,0:T(8,128)(2,1)} %bitcast.52), channel_id=1, source_target_pairs={{0,4},{4,0},{8,12},{12,8},{1,5},{5,1},{9,13},{13,9},{2,6},{6,2},{1... | collective-permute-start | bytes 49160 | tf_op jit(solution)/shard_map/ppermute | solution.py:24
  3.8 16.9 %all-to-all-start = ((bf16[8,224,128]{2,1,0:T(8,128)(2,1)}), bf16[8,224,128]{2,1,0:T(8,128)(2,1)S(1)}, u32[]{:S(2)}, u32[]{:S(2)}) async-start(bf16[8,224,128]{2,1,0:T(8,128)(2,1)} %get-tuple-element.13), calls=%async_computation | async-start | bytes 917504 | tf_op jit(solution)/shard_map/all_to_all | solution.py:203
  13.0 4.3 %collective-permute-start.1 = (bf16[2,64,128]{2,1,0:T(8,128)(2,1)S(1)}, bf16[2,64,128]{2,1,0:T(8,128)(2,1)S(1)}, u32[]{:S(2)}, u32[]{:S(2)}) collective-permute-start(bf16[2,64,128]{2,1,0:T(8,128)(2,1)S(1)} %pad_maximum_fusion.3), channel_id=1, source_target_pairs={{0,12},{4,8},{8,4},{12,0},{1,13},{5,9},{9,5},{13,1},{2,14},{6,10},... | collective-permute-start | bytes 98312 | tf_op jit(solution)/shard_map/ppermute | solution.py:24
  14.9 41.3 %collective-permute-start.4 = (bf16[512,4,512]{2,1,0:T(4,128)(2,1)}, bf16[512,4,512]{2,1,0:T(4,128)(2,1)}, u32[]{:S(2)}, u32[]{:S(2)}) collective-permute-start(bf16[512,4,512]{2,1,0:T(4,128)(2,1)} %own_ref.1), channel_id=1, source_target_pairs={{0,1},{1,0},{2,3},{3,2},{4,5},{5,4},{6,7},{7,6},{8,9},{9,8},{10,11... | collective-permute-start | bytes 6291464 | tf_op jit(solution)/shard_map/ppermute | solution.py:24
  17.2 3.5 %collective-permute-start.2 = (bf16[4,64,128]{2,1,0:T(8,128)(2,1)S(1)}, bf16[4,64,128]{2,1,0:T(8,128)(2,1)S(1)}, u32[]{:S(2)}, u32[]{:S(2)}) collective-permute-start(bf16[4,64,128]{2,1,0:T(8,128)(2,1)S(1)} %pad_maximum_fusion.2), channel_id=1, source_target_pairs={{0,2},{2,0},{64,66},{66,64},{1,3},{3,1},{65,67},{67,65},{4,6},{6,4... | collective-permute-start | bytes 196616 | tf_op jit(solution)/shard_map/ppermute | solution.py:24
  22.8 31.9 %all-to-all-start.1 = ((bf16[8,1040,128]{2,1,0:T(8,128)(2,1)}), bf16[8,1040,128]{2,1,0:T(8,128)(2,1)S(1)}, u32[]{:S(2)}, u32[]{:S(2)}) async-start(bf16[8,1040,128]{2,1,0:T(8,128)(2,1)} %pairs.1), calls=%async_computation.1 | async-start | bytes 4259840 | tf_op jit(solution)/shard_map/all_to_all | solution.py:203
  26.5 29.7 %copy-start.1 = (s32[16,64]{1,0:T(8,128)S(1)}, s32[16,64]{1,0:T(8,128)}, u32[]{:S(2)}) copy-start(s32[16,64]{1,0:T(8,128)} %pm_ref.1) | copy-start | bytes 12292
  26.5 3.9 %collective-permute-start.5 = (bf16[1,8,64,128]{3,2,1,0:T(8,128)(2,1)S(1)}, bf16[1,8,64,128]{3,2,1,0:T(8,128)(2,1)S(1)}, u32[]{:S(2)}, u32[]{:S(2)}) collective-permute-start(bf16[1,8,64,128]{3,2,1,0:T(8,128)(2,1)S(1)} %maximum_bitcast_fusion), channel_id=1, source_target_pairs={{0,16},{16,0},{32,48},{48,32},{1,17},{17,1},{33,49},{49,33},{2,18}... | collective-permute-start | bytes 393224 | tf_op jit(solution)/shard_map/ppermute | solution.py:24
  30.4 6.8 %collective-permute-start.6 = (bf16[2,8,64,128]{3,2,1,0:T(8,128)(2,1)S(1)}, bf16[2,8,64,128]{3,2,1,0:T(8,128)(2,1)S(1)}, u32[]{:S(2)}, u32[]{:S(2)}) collective-permute-start(bf16[2,8,64,128]{3,2,1,0:T(8,128)(2,1)S(1)} %pad_maximum_fusion.1), channel_id=1, source_target_pairs={{0,48},{16,32},{32,16},{48,0},{1,49},{17,33},{33,17},{49,1},{2,50}... | collective-permute-start | bytes 786440 | tf_op jit(solution)/shard_map/ppermute | solution.py:24
  37.3 10.2 %collective-permute-start.7 = (bf16[4,8,64,128]{3,2,1,0:T(8,128)(2,1)S(1)}, bf16[4,8,64,128]{3,2,1,0:T(8,128)(2,1)S(1)}, u32[]{:S(2)}, u32[]{:S(2)}) collective-permute-start(bf16[4,8,64,128]{3,2,1,0:T(8,128)(2,1)S(1)} %constant_dynamic-update-slice_fusion.near_ref), channel_id=1, source_target_pairs={{0,66},{2,64},{64,2},{66,0},{1,67},{3,65},{65,3},{67,1},{4,70},{6,... | collective-permute-start | bytes 1572872 | tf_op jit(solution)/shard_map/ppermute | solution.py:24
  41.1 13.7 %collective-permute-start.8 = (bf16[4,8,32,128]{3,2,1,0:T(8,128)(2,1)}, bf16[4,8,32,128]{3,2,1,0:T(8,128)(2,1)S(1)}, u32[]{:S(2)}, u32[]{:S(2)}) collective-permute-start(bf16[4,8,32,128]{3,2,1,0:T(8,128)(2,1)} %slice.21), channel_id=1, source_target_pairs={{0,1},{1,0},{2,3},{3,2},{4,5},{5,4},{6,7},{7,6},{8,9},{9,8},{10,11... | collective-permute-start | bytes 786440 | tf_op jit(solution)/shard_map/ppermute | solution.py:24
  48.2 7.9 %collective-permute-start.9 = (bf16[4,8,32,128]{3,2,1,0:T(8,128)(2,1)}, bf16[4,8,32,128]{3,2,1,0:T(8,128)(2,1)}, u32[]{:S(2)}, u32[]{:S(2)}) collective-permute-start(bf16[4,8,32,128]{3,2,1,0:T(8,128)(2,1)} %slice.22), channel_id=1, source_target_pairs={{0,1},{1,0},{2,3},{3,2},{4,5},{5,4},{6,7},{7,6},{8,9},{9,8},{10,11... | collective-permute-start | bytes 786440 | tf_op jit(solution)/shard_map/ppermute | solution.py:24
  54.7 27.8 %collective-permute-start.3 = (bf16[8,16,128]{2,1,0:T(8,128)(2,1)S(1)}, bf16[8,16,128]{2,1,0:T(8,128)(2,1)S(1)}, u32[]{:S(2)}, u32[]{:S(2)}) collective-permute-start(bf16[8,16,128]{2,1,0:T(8,128)(2,1)S(1)} %slice.20), channel_id=1, source_target_pairs={{0,1},{1,0},{2,3},{3,2},{4,5},{5,4},{6,7},{7,6},{8,9},{9,8},{10,11... | collective-permute-start | bytes 98312 | tf_op jit(solution)/shard_map/ppermute | solution.py:24
  56.2 1.6 %copy-start = (bf16[512,4,512]{2,1,0:T(4,128)(2,1)S(1)}, bf16[512,4,512]{2,1,0:T(4,128)(2,1)}, u32[]{:S(2)}) copy-start(bf16[512,4,512]{2,1,0:T(4,128)(2,1)} %own_ref.1) | copy-start | bytes 6291460
  73.4 20.0 %all-to-all-start.2 = ((bf16[128,8,128]{2,1,0:T(8,128)(2,1)}), bf16[128,8,128]{2,1,0:T(8,128)(2,1)S(1)}, u32[]{:S(2)}, u32[]{:S(2)}) async-start(bf16[128,8,128]{2,1,0:T(8,128)(2,1)} %bitcast.17), calls=%async_computation.2 | async-start | bytes 524288 | tf_op jit(solution)/shard_map/all_to_all | solution.py:203

commit v7 on v6

--- a/solution.py
+++ b/solution.py
@@ -144,7 +144,7 @@
     lax.fori_loop(0, 8, one_chip, 0, unroll=4)
     for fetch in fetches:
         fetch.wait()
-    lax.fori_loop(0, 64, eight_mats, 0)
+    lax.fori_loop(0, 64, eight_mats, 0, unroll=8)
     for chunk in range(4):
 
         def one_target(t, carry, chunk=chunk):

time: 95.3 us -> 95 us (level)
  transfers between devices with their start and end apart: 13 -> 13, of which waited for: 6 -> 6; matrix products, arithmetic and copies ran while one was open for 6% -> 6% of each run, Pallas kernels for 19% -> 18%
where the time goes in v7:
time: 95 us; the launch traced here: 94.4 us
  starting transfers between devices  45.9 us (48%)
  waiting for transfers between devices  21 us (22%)
  Pallas kernels  19 us (20%)
  local copies, waits for them, and re-layouts  5.94 us (6%)
  other arithmetic  2.04 us (2%)
    ppermute x10, starting transfers between devices, swap(): return lax.ppermute(x, axes, [(i, i ^ mask) for i in range(size)])  25.8 us
    all_to_all x3, starting transfers between devices, all_to_all(): return lax.all_to_all(x, axes, split_axis=0, concat_axis=0, tiled=True)  20.1 us
    pallas_call x1, Pallas kernels, local(): pl.pallas_call(screen_kernel, out_shape=jax.ShapeDtypeStruct((8, 16, 8, 1...  15.3 us
    ppermute x10, waiting for transfers between devices, swap(): return lax.ppermute(x, axes, [(i, i ^ mask) for i in range(size)])  11.2 us
    all_to_all x3, waiting for transfers between devices, all_to_all(): return lax.all_to_all(x, axes, split_axis=0, concat_axis=0, tiled=True)  9.76 us
    unnamed x7, local copies, waits for them, and re-layouts  2.48 us
    pallas_call x1, Pallas kernels, local(): pl.pallas_call(pair_kernel, out_shape=jax.ShapeDtypeStruct((8, TV + 16, 1...  2.07 us
  transfers between devices with their start and end apart: 13, of which 6 were waited for; matrix products, arithmetic and copies ran while one was open for 6% of the time, Pallas kernels for 18%

profile of v7, /device:TPU:1, one launch (start us, length us, event | category | flops | bytes accessed | tf_op | source)
XLA Modules:
  0.0 94.4 jit_solution(12020323779867725505)
XLA Ops:
  0.0 1.7 %prepare.1 = (bf16[8,224,128]{2,1,0:T(8,128)(2,1)}, bf16[64,128]{1,0:T(8,128)(2,1)}) custom-call(bf16[128,128]{1,0:T(8,128)(2,1)} %bitcast.50, bf16[4,64,64]{2,1,0:T(8,128)(2,1)} %cs_ref.1, bf16[2,32,64]{2,1,0:T(8,128)(2,1)} %bitcast.51), custom_call_target="tpu_custom_call" | custom-call | tf_op jit(solution)/shard_map/prepare/pallas_call | solution.py:208
  1.7 2.1 %collective-permute-start = (bf16[1,64,128]{2,1,0:T(8,128)(2,1)}, bf16[1,64,128]{2,1,0:T(8,128)(2,1)S(1)}, u32[]{:S(2)}, u32[]{:S(2)}) collective-permute-start(bf16[1,64,128]{2,1,0:T(8,128)(2,1)} %bitcast.52), channel_id=1, source_target_pairs={{0,4},{4,0},{8,12},{12,8},{1,5},{5,1},{9,13},{13,9},{2,6},{6,2},{1... | collective-permute-start | bytes 49160 | tf_op jit(solution)/shard_map/ppermute | solution.py:24
  3.8 7.5 %all-to-all-start = ((bf16[8,224,128]{2,1,0:T(8,128)(2,1)}), bf16[8,224,128]{2,1,0:T(8,128)(2,1)S(1)}, u32[]{:S(2)}, u32[]{:S(2)}) async-start(bf16[8,224,128]{2,1,0:T(8,128)(2,1)} %get-tuple-element.13), calls=%async_computation | async-start | bytes 917504 | tf_op jit(solution)/shard_map/all_to_all | solution.py:203
  11.3 0.9 copy.11
  12.2 0.7 pad_maximum_fusion.3
  13.0 1.9 %collective-permute-start.1 = (bf16[2,64,128]{2,1,0:T(8,128)(2,1)S(1)}, bf16[2,64,128]{2,1,0:T(8,128)(2,1)S(1)}, u32[]{:S(2)}, u32[]{:S(2)}) collective-permute-start(bf16[2,64,128]{2,1,0:T(8,128)(2,1)S(1)} %pad_maximum_fusion.3), channel_id=1, source_target_pairs={{0,12},{4,8},{8,4},{12,0},{1,13},{5,9},{9,5},{13,1},{2,14},{6,10},... | collective-permute-start | bytes 98312 | tf_op jit(solution)/shard_map/ppermute | solution.py:24
  14.9 1.5 %collective-permute-start.4 = (bf16[512,4,512]{2,1,0:T(4,128)(2,1)}, bf16[512,4,512]{2,1,0:T(4,128)(2,1)}, u32[]{:S(2)}, u32[]{:S(2)}) collective-permute-start(bf16[512,4,512]{2,1,0:T(4,128)(2,1)} %own_ref.1), channel_id=1, source_target_pairs={{0,1},{1,0},{2,3},{3,2},{4,5},{5,4},{6,7},{7,6},{8,9},{9,8},{10,11... | collective-permute-start | bytes 6291464 | tf_op jit(solution)/shard_map/ppermute | solution.py:24
  16.4 0.9 collective-permute-done.1
  17.2 0.4 collective-permute-start.2
  17.6 0.8 reshape.38.tv_ref
  18.5 2.2 %collective-permute-done.2 = bf16[4,64,128]{2,1,0:T(8,128)(2,1)S(1)} collective-permute-done((bf16[4,64,128]{2,1,0:T(8,128)(2,1)S(1)}, bf16[4,64,128]{2,1,0:T(8,128)(2,1)S(1)}, u32[]{:S(2)}, u32[]{:S(2)}) %collective-permute-start.2) | collective-permute-done | bytes 65568 | tf_op jit(solution)/shard_map/ppermute | solution.py:24
  20.8 2.1 %pairs.1 = bf16[8,1040,128]{2,1,0:T(8,128)(2,1)} custom-call(bf16[4,32,64]{2,1,0:T(8,128)(2,1)S(1)} %copy.12.sv_ref, bf16[8,224,128]{2,1,0:T(8,128)(2,1)S(1)} %all-to-all-done.near_ref, bf16[16,128]{1,0:T(8,128)(2,1)S(1)} %reshape.38.tv_ref), custom_call_target="tpu_custom_call" | custom-call | tf_op jit(solution)/shard_map/pairs/pallas_call | solution.py:230
  22.8 3.6 %all-to-all-start.1 = ((bf16[8,1040,128]{2,1,0:T(8,128)(2,1)}), bf16[8,1040,128]{2,1,0:T(8,128)(2,1)S(1)}, u32[]{:S(2)}, u32[]{:S(2)}) async-start(bf16[8,1040,128]{2,1,0:T(8,128)(2,1)} %pairs.1), calls=%async_computation.1 | async-start | bytes 4259840 | tf_op jit(solution)/shard_map/all_to_all | solution.py:203
  26.5 1.4 %collective-permute-start.5 = (bf16[1,8,64,128]{3,2,1,0:T(8,128)(2,1)S(1)}, bf16[1,8,64,128]{3,2,1,0:T(8,128)(2,1)S(1)}, u32[]{:S(2)}, u32[]{:S(2)}) collective-permute-start(bf16[1,8,64,128]{3,2,1,0:T(8,128)(2,1)S(1)} %maximum_bitcast_fusion), channel_id=1, source_target_pairs={{0,16},{16,0},{32,48},{48,32},{1,17},{17,1},{33,49},{49,33},{2,18}... | collective-permute-start | bytes 393224 | tf_op jit(solution)/shard_map/ppermute | solution.py:24
  27.9 2.5 %collective-permute-done.5 = bf16[1,8,64,128]{3,2,1,0:T(8,128)(2,1)S(1)} collective-permute-done((bf16[1,8,64,128]{3,2,1,0:T(8,128)(2,1)S(1)}, bf16[1,8,64,128]{3,2,1,0:T(8,128)(2,1)S(1)}, u32[]{:S(2)}, u32[]{:S(2)}) %collective-permute-start.5) | collective-permute-done | bytes 131104 | tf_op jit(solution)/shard_map/ppermute | solution.py:24
  30.4 2.5 %collective-permute-start.6 = (bf16[2,8,64,128]{3,2,1,0:T(8,128)(2,1)S(1)}, bf16[2,8,64,128]{3,2,1,0:T(8,128)(2,1)S(1)}, u32[]{:S(2)}, u32[]{:S(2)}) collective-permute-start(bf16[2,8,64,128]{3,2,1,0:T(8,128)(2,1)S(1)} %pad_maximum_fusion.1), channel_id=1, source_target_pairs={{0,48},{16,32},{32,16},{48,0},{1,49},{17,33},{33,17},{49,1},{2,50}... | collective-permute-start | bytes 786440 | tf_op jit(solution)/shard_map/ppermute | solution.py:24
  32.9 4.3 %collective-permute-done.6 = bf16[2,8,64,128]{3,2,1,0:T(8,128)(2,1)S(1)} collective-permute-done((bf16[2,8,64,128]{3,2,1,0:T(8,128)(2,1)S(1)}, bf16[2,8,64,128]{3,2,1,0:T(8,128)(2,1)S(1)}, u32[]{:S(2)}, u32[]{:S(2)}) %collective-permute-start.6) | collective-permute-done | bytes 262176 | tf_op jit(solution)/shard_map/ppermute | solution.py:24
  37.3 3.1 %collective-permute-start.7 = (bf16[4,8,64,128]{3,2,1,0:T(8,128)(2,1)S(1)}, bf16[4,8,64,128]{3,2,1,0:T(8,128)(2,1)S(1)}, u32[]{:S(2)}, u32[]{:S(2)}) collective-permute-start(bf16[4,8,64,128]{3,2,1,0:T(8,128)(2,1)S(1)} %constant_dynamic-update-slice_fusion.near_ref), channel_id=1, source_target_pairs={{0,66},{2,64},{64,2},{66,0},{1,67},{3,65},{65,3},{67,1},{4,70},{6,... | collective-permute-start | bytes 1572872 | tf_op jit(solution)/shard_map/ppermute | solution.py:24
  40.4 0.7 slice.21
  41.1 6.4 %collective-permute-start.8 = (bf16[4,8,32,128]{3,2,1,0:T(8,128)(2,1)}, bf16[4,8,32,128]{3,2,1,0:T(8,128)(2,1)S(1)}, u32[]{:S(2)}, u32[]{:S(2)}) collective-permute-start(bf16[4,8,32,128]{3,2,1,0:T(8,128)(2,1)} %slice.21), channel_id=1, source_target_pairs={{0,1},{1,0},{2,3},{3,2},{4,5},{5,4},{6,7},{7,6},{8,9},{9,8},{10,11... | collective-permute-start | bytes 786440 | tf_op jit(solution)/shard_map/ppermute | solution.py:24
  47.5 0.7 slice.22
  48.2 6.4 %collective-permute-start.9 = (bf16[4,8,32,128]{3,2,1,0:T(8,128)(2,1)}, bf16[4,8,32,128]{3,2,1,0:T(8,128)(2,1)}, u32[]{:S(2)}, u32[]{:S(2)}) collective-permute-start(bf16[4,8,32,128]{3,2,1,0:T(8,128)(2,1)} %slice.22), channel_id=1, source_target_pairs={{0,1},{1,0},{2,3},{3,2},{4,5},{5,4},{6,7},{7,6},{8,9},{9,8},{10,11... | collective-permute-start | bytes 786440 | tf_op jit(solution)/shard_map/ppermute | solution.py:24
  54.8 1.3 %collective-permute-done.9.ct_far_ref = bf16[4,8,32,128]{3,2,1,0:T(8,128)(2,1)} collective-permute-done((bf16[4,8,32,128]{3,2,1,0:T(8,128)(2,1)}, bf16[4,8,32,128]{3,2,1,0:T(8,128)(2,1)}, u32[]{:S(2)}, u32[]{:S(2)}) %collective-permute-start.9) | collective-permute-done | bytes 262176 | tf_op jit(solution)/shard_map/ppermute | solution.py:24
  56.2 1.6 %copy-done = bf16[512,4,512]{2,1,0:T(4,128)(2,1)S(1)} copy-done((bf16[512,4,512]{2,1,0:T(4,128)(2,1)S(1)}, bf16[512,4,512]{2,1,0:T(4,128)(2,1)}, u32[]{:S(2)}) %copy-start) | copy-done | bytes 2097176
  57.8 15.3 %screen.1 = bf16[8,16,8,128]{3,2,1,0:T(8,128)(2,1)} custom-call(s32[3]{0:T(128)S(1)} %pad_add_fusion.me_ref, s32[16,64]{1,0:T(8,128)S(1)} %copy-done.1, bf16[512,4,512]{2,1,0:T(4,128)(2,1)S(1)} %copy-done, bf16[512,4,512]{2,1,0:T(4,128)(2,1)} %collective-permute-done.4.other_hbm, bf16[8,1040,128]{2,1,0:T(8,128)(2,1)S(1)} %all-to-all-done.1.every_ref, ...), custom_call_target="tpu_custom_call" | custom-call | flops 8000000000 | bytes 16000000 | tf_op jit(solution)/shard_map/screen/pallas_call | solution.py:246
  73.2 9.0 %all-to-all-start.2 = ((bf16[128,8,128]{2,1,0:T(8,128)(2,1)}), bf16[128,8,128]{2,1,0:T(8,128)(2,1)S(1)}, u32[]{:S(2)}, u32[]{:S(2)}) async-start(bf16[128,8,128]{2,1,0:T(8,128)(2,1)} %bitcast.17), calls=%async_computation.2 | async-start | bytes 524288 | tf_op jit(solution)/shard_map/all_to_all | solution.py:203
  82.7 0.4 pad_maximum_fusion
  83.2 0.2 copy.17
  83.4 9.8 %all-to-all-done.2 = bf16[128,8,128]{2,1,0:T(8,128)(2,1)S(1)} async-done(((bf16[128,8,128]{2,1,0:T(8,128)(2,1)}), bf16[128,8,128]{2,1,0:T(8,128)(2,1)S(1)}, u32[]{:S(2)}, u32[]{:S(2)}) %all-to-all-start.2) | async-done | bytes 262176 | tf_op jit(solution)/shard_map/all_to_all | solution.py:203
  93.1 0.1 copy.18
  93.3 0.3 fusion.1
  93.7 0.6 pad_maximum_fusion.4
  (30 shorter events, 1.3 us)
Async XLA Ops:
  1.7 10.5 %collective-permute-start = (bf16[1,64,128]{2,1,0:T(8,128)(2,1)}, bf16[1,64,128]{2,1,0:T(8,128)(2,1)S(1)}, u32[]{:S(2)}, u32[]{:S(2)}) collective-permute-start(bf16[1,64,128]{2,1,0:T(8,128)(2,1)} %bitcast.52), channel_id=1, source_target_pairs={{0,4},{4,0},{8,12},{12,8},{1,5},{5,1},{9,13},{13,9},{2,6},{6,2},{1... | collective-permute-start | bytes 49160 | tf_op jit(solution)/shard_map/ppermute | solution.py:24
  3.8 16.9 %all-to-all-start = ((bf16[8,224,128]{2,1,0:T(8,128)(2,1)}), bf16[8,224,128]{2,1,0:T(8,128)(2,1)S(1)}, u32[]{:S(2)}, u32[]{:S(2)}) async-start(bf16[8,224,128]{2,1,0:T(8,128)(2,1)} %get-tuple-element.13), calls=%async_computation | async-start | bytes 917504 | tf_op jit(solution)/shard_map/all_to_all | solution.py:203
  13.0 4.3 %collective-permute-start.1 = (bf16[2,64,128]{2,1,0:T(8,128)(2,1)S(1)}, bf16[2,64,128]{2,1,0:T(8,128)(2,1)S(1)}, u32[]{:S(2)}, u32[]{:S(2)}) collective-permute-start(bf16[2,64,128]{2,1,0:T(8,128)(2,1)S(1)} %pad_maximum_fusion.3), channel_id=1, source_target_pairs={{0,12},{4,8},{8,4},{12,0},{1,13},{5,9},{9,5},{13,1},{2,14},{6,10},... | collective-permute-start | bytes 98312 | tf_op jit(solution)/shard_map/ppermute | solution.py:24
  14.9 41.3 %collective-permute-start.4 = (bf16[512,4,512]{2,1,0:T(4,128)(2,1)}, bf16[512,4,512]{2,1,0:T(4,128)(2,1)}, u32[]{:S(2)}, u32[]{:S(2)}) collective-permute-start(bf16[512,4,512]{2,1,0:T(4,128)(2,1)} %own_ref.1), channel_id=1, source_target_pairs={{0,1},{1,0},{2,3},{3,2},{4,5},{5,4},{6,7},{7,6},{8,9},{9,8},{10,11... | collective-permute-start | bytes 6291464 | tf_op jit(solution)/shard_map/ppermute | solution.py:24
  17.2 3.5 %collective-permute-start.2 = (bf16[4,64,128]{2,1,0:T(8,128)(2,1)S(1)}, bf16[4,64,128]{2,1,0:T(8,128)(2,1)S(1)}, u32[]{:S(2)}, u32[]{:S(2)}) collective-permute-start(bf16[4,64,128]{2,1,0:T(8,128)(2,1)S(1)} %pad_maximum_fusion.2), channel_id=1, source_target_pairs={{0,2},{2,0},{64,66},{66,64},{1,3},{3,1},{65,67},{67,65},{4,6},{6,4... | collective-permute-start | bytes 196616 | tf_op jit(solution)/shard_map/ppermute | solution.py:24
  22.8 31.9 %all-to-all-start.1 = ((bf16[8,1040,128]{2,1,0:T(8,128)(2,1)}), bf16[8,1040,128]{2,1,0:T(8,128)(2,1)S(1)}, u32[]{:S(2)}, u32[]{:S(2)}) async-start(bf16[8,1040,128]{2,1,0:T(8,128)(2,1)} %pairs.1), calls=%async_computation.1 | async-start | bytes 4259840 | tf_op jit(solution)/shard_map/all_to_all | solution.py:203
  26.5 29.7 %copy-start.1 = (s32[16,64]{1,0:T(8,128)S(1)}, s32[16,64]{1,0:T(8,128)}, u32[]{:S(2)}) copy-start(s32[16,64]{1,0:T(8,128)} %pm_ref.1) | copy-start | bytes 12292
  26.5 3.9 %collective-permute-start.5 = (bf16[1,8,64,128]{3,2,1,0:T(8,128)(2,1)S(1)}, bf16[1,8,64,128]{3,2,1,0:T(8,128)(2,1)S(1)}, u32[]{:S(2)}, u32[]{:S(2)}) collective-permute-start(bf16[1,8,64,128]{3,2,1,0:T(8,128)(2,1)S(1)} %maximum_bitcast_fusion), channel_id=1, source_target_pairs={{0,16},{16,0},{32,48},{48,32},{1,17},{17,1},{33,49},{49,33},{2,18}... | collective-permute-start | bytes 393224 | tf_op jit(solution)/shard_map/ppermute | solution.py:24
  30.4 6.8 %collective-permute-start.6 = (bf16[2,8,64,128]{3,2,1,0:T(8,128)(2,1)S(1)}, bf16[2,8,64,128]{3,2,1,0:T(8,128)(2,1)S(1)}, u32[]{:S(2)}, u32[]{:S(2)}) collective-permute-start(bf16[2,8,64,128]{3,2,1,0:T(8,128)(2,1)S(1)} %pad_maximum_fusion.1), channel_id=1, source_target_pairs={{0,48},{16,32},{32,16},{48,0},{1,49},{17,33},{33,17},{49,1},{2,50}... | collective-permute-start | bytes 786440 | tf_op jit(solution)/shard_map/ppermute | solution.py:24
  37.3 10.2 %collective-permute-start.7 = (bf16[4,8,64,128]{3,2,1,0:T(8,128)(2,1)S(1)}, bf16[4,8,64,128]{3,2,1,0:T(8,128)(2,1)S(1)}, u32[]{:S(2)}, u32[]{:S(2)}) collective-permute-start(bf16[4,8,64,128]{3,2,1,0:T(8,128)(2,1)S(1)} %constant_dynamic-update-slice_fusion.near_ref), channel_id=1, source_target_pairs={{0,66},{2,64},{64,2},{66,0},{1,67},{3,65},{65,3},{67,1},{4,70},{6,... | collective-permute-start | bytes 1572872 | tf_op jit(solution)/shard_map/ppermute | solution.py:24
  41.1 13.7 %collective-permute-start.8 = (bf16[4,8,32,128]{3,2,1,0:T(8,128)(2,1)}, bf16[4,8,32,128]{3,2,1,0:T(8,128)(2,1)S(1)}, u32[]{:S(2)}, u32[]{:S(2)}) collective-permute-start(bf16[4,8,32,128]{3,2,1,0:T(8,128)(2,1)} %slice.21), channel_id=1, source_target_pairs={{0,1},{1,0},{2,3},{3,2},{4,5},{5,4},{6,7},{7,6},{8,9},{9,8},{10,11... | collective-permute-start | bytes 786440 | tf_op jit(solution)/shard_map/ppermute | solution.py:24
  48.2 7.9 %collective-permute-start.9 = (bf16[4,8,32,128]{3,2,1,0:T(8,128)(2,1)}, bf16[4,8,32,128]{3,2,1,0:T(8,128)(2,1)}, u32[]{:S(2)}, u32[]{:S(2)}) collective-permute-start(bf16[4,8,32,128]{3,2,1,0:T(8,128)(2,1)} %slice.22), channel_id=1, source_target_pairs={{0,1},{1,0},{2,3},{3,2},{4,5},{5,4},{6,7},{7,6},{8,9},{9,8},{10,11... | collective-permute-start | bytes 786440 | tf_op jit(solution)/shard_map/ppermute | solution.py:24
  54.7 27.5 %collective-permute-start.3 = (bf16[8,16,128]{2,1,0:T(8,128)(2,1)S(1)}, bf16[8,16,128]{2,1,0:T(8,128)(2,1)S(1)}, u32[]{:S(2)}, u32[]{:S(2)}) collective-permute-start(bf16[8,16,128]{2,1,0:T(8,128)(2,1)S(1)} %slice.20), channel_id=1, source_target_pairs={{0,1},{1,0},{2,3},{3,2},{4,5},{5,4},{6,7},{7,6},{8,9},{9,8},{10,11... | collective-permute-start | bytes 98312 | tf_op jit(solution)/shard_map/ppermute | solution.py:24
  56.2 1.6 %copy-start = (bf16[512,4,512]{2,1,0:T(4,128)(2,1)S(1)}, bf16[512,4,512]{2,1,0:T(4,128)(2,1)}, u32[]{:S(2)}) copy-start(bf16[512,4,512]{2,1,0:T(4,128)(2,1)} %own_ref.1) | copy-start | bytes 6291460
  73.2 20.0 %all-to-all-start.2 = ((bf16[128,8,128]{2,1,0:T(8,128)(2,1)}), bf16[128,8,128]{2,1,0:T(8,128)(2,1)S(1)}, u32[]{:S(2)}, u32[]{:S(2)}) async-start(bf16[128,8,128]{2,1,0:T(8,128)(2,1)} %bitcast.17), calls=%async_computation.2 | async-start | bytes 524288 | tf_op jit(solution)/shard_map/all_to_all | solution.py:203
